TPU v7x, 512 devices: a whole 4x8x8 slice. The times are simulated.
512 devices in a mesh: section: 4 (over x), tile: 128 (over z, y, core).
Axes of the slice: x: 4, y: 8, z: 8, core: 2. Of those that a mesh axis runs over, the one named last changes fastest.
Arguments:
- features: bfloat16 [512, 16, 16, 256], P('tile'), may hold values from -6 to 6
- out_cotangent: bfloat16 [512, 16, 16, 256], P('tile'), may hold values from -24 to 24
- w_reduce: bfloat16 [4, 256, 64], P('section'), may hold values from -0.375 to 0.375
- w_taps: bfloat16 [4, 576, 64], P('section'), may hold values from -0.25 to 0.25
- w_expand: bfloat16 [4, 64, 256], P('section'), may hold values from -0.75 to 0.75
- norm_scale: float32 [4, 384], P('section'), may hold values from 0.25 to 1.75
- norm_shift: float32 [4, 384], P('section'), may hold values from -2 to 2
- owner: int32 [512], replicated, may hold values from 0 to 511, as said below
- neighbours: int32 [512, 4], replicated, may hold values from -1 to 511, as said below
Outputs:
- block_outputs: bfloat16 [4, 512, 16, 16, 256], P('section', 'tile')
- input_grads: bfloat16 [4, 512, 16, 16, 256], P('section', 'tile')
- grad_reduce: float32 [4, 256, 64], P('section')
- grad_taps: float32 [4, 576, 64], P('section')
- grad_expand: float32 [4, 64, 256], P('section')
Inputs may be any that keep to these rules, and one draw needn't show every extreme that they name: `owner`: A permutation of the rows; the rows 4 k to 4 k + 3 belong to index k of tile. The tiles form a band 8 tiles across; two neighbouring tiles are owned by indices of tile at most 3 apart, and west and east neighbours by indices at most 1 apart. Symmetric: if neighbours[t, 0] = u then neighbours[u, 1] = t, and likewise for west and east; -1 at the band's border.
All inputs are finite; a program needn't handle non-finite values.
Results may differ from a plain program's by a relative error of at most 0.039.
Values may be sent and summed in bfloat16 or wider, within the bound.
No kernel may reach another device: no remote copies, remote signals or barrier semaphores. Data moves between devices by JAX's collectives and lax.ppermute only.
A program may use at most 64 MiB of HBM per device.

v0:
```python
import jax
import jax.numpy as jnp
import numpy as np
from jax import lax
from jax.experimental import pallas as pl
from jax.experimental.pallas import tpu as pltpu
from jax.sharding import Mesh
from jax.sharding import PartitionSpec as P

TILE_AXES = ("z", "y", "core")
SIDE = 16
REGION = 32
HALO = 8
PIXELS = REGION * REGION
WIDTH = 64
CHANS = 256
TAPS = 9
BF = jnp.bfloat16
F32 = jnp.float32
VMEM_LIMIT = 56 * 1024 * 1024


def mm(left, right):
    return jnp.dot(left, right, preferred_element_type=F32)


def mm_first(left, right):
    return lax.dot_general(left, right, (((0,), (0,)), ((), ())), preferred_element_type=F32)


def silu_parts(value):
    sig = 0.5 + 0.5 * jnp.tanh(0.5 * value)
    out = value * sig
    return (out, sig + out * (1.0 - sig))


def around(tile, owner, near, here):
    north, south = (near[tile * 4], near[tile * 4 + 1])
    west, east = (near[tile * 4 + 2], near[tile * 4 + 3])

    def step(first, way, second, other):
        one = jnp.where(first >= 0, near[jnp.maximum(first, 0) * 4 + way], -1)
        two = jnp.where(second >= 0, near[jnp.maximum(second, 0) * 4 + other], -1)
        return jnp.where(one >= 0, one, two)

    ids = [
        step(north, 2, west, 0), north, step(north, 3, east, 0),
        west, tile, east,
        step(south, 2, west, 1), south, step(south, 3, east, 1),
    ]
    places, found = ([], [])
    for item in ids:
        row = owner[jnp.maximum(item, 0)]
        device = row >> 2
        gap = (device >> 1) - (here >> 1)
        order = 2 * jnp.abs(gap) - jnp.where(gap < 0, 1, 0)
        place = order * 4 + (row & 3) + jnp.where((device & 1) == (here & 1), 0, 20)
        places.append(jnp.clip(place, 0, 39))
        found.append(item >= 0)
    return (places, found)


BANDS = ((0, HALO, 0, HALO), (HALO, SIDE, 3, 0), (HALO + SIDE, HALO, 6, 0))


def build_region(pool, region, lane, places, found):
    for top, rows, first, start in BANDS:
        parts = []
        for k in range(3):
            part = pool[places[first + k], pl.ds(start, rows)].astype(F32)
            part = jnp.where(found[first + k], part, 0.0)
            cut = (slice(HALO, SIDE), slice(0, SIDE), slice(0, HALO))[k]
            parts.append(part[:, cut, :])
        band = jnp.concatenate(parts, axis=1).reshape(rows * REGION, CHANS).astype(BF)
        region[pl.ds(top * REGION, rows * REGION), pl.ds(lane * CHANS, CHANS)] = band


def build_present(present, found_pair):
    for top, rows, first, _ in BANDS:
        shape = (rows * REGION, 2 * WIDTH)
        col = lax.broadcasted_iota(jnp.int32, shape, 0) % REGION
        lane = lax.broadcasted_iota(jnp.int32, shape, 1)
        sides = []
        for found in found_pair:
            flags = [jnp.where(found[first + k], 1.0, 0.0) for k in range(3)]
            sides.append(
                jnp.where(col < HALO, flags[0], jnp.where(col < HALO + SIDE, flags[1], flags[2]))
            )
        present[pl.ds(top * REGION, rows * REGION), :] = jnp.where(lane < WIDTH, sides[0], sides[1])


def build_masks(masks):
    shape = (PIXELS, 2 * WIDTH)
    pixel = lax.broadcasted_iota(jnp.int32, shape, 0)
    row, col = (pixel // REGION, pixel % REGION)
    low, high = (HALO, HALO + SIDE)
    west = (col == low) | (col == high)
    east = (col == low - 1) | (col == high - 1)
    above = (row == low - 1) | (row == high - 1)
    below = (row == low) | (row == high)
    for k, (across, along) in enumerate(
        ((above, west), (above, east), (below, west), (below, east))
    ):
        masks[k] = jnp.where(across & along, 0.0, 1.0).astype(BF)


def store_shifted(shifted, masks, start, value):
    count = value.shape[0]
    rows = pl.ds(start, count)
    left = pltpu.roll(value, 1, 0).astype(BF)
    right = pltpu.roll(value, count - 1, 0).astype(BF)
    shifted[0, rows, :] = left
    shifted[1, rows, :] = value.astype(BF)
    shifted[2, rows, :] = right
    shifted[3, rows, :] = left * masks[0, rows, :]
    shifted[4, rows, :] = right * masks[1, rows, :]
    shifted[5, rows, :] = left * masks[2, rows, :]
    shifted[6, rows, :] = right * masks[3, rows, :]


TAP_SOURCES = ((3, -1), (1, -1), (4, -1), (0, 0), (1, 0), (2, 0), (5, 1), (1, 1), (6, 1))


def columns_at(shifted, start, count):
    return jnp.concatenate(
        [shifted[k, pl.ds(start + dy * REGION, count), :] for k, dy in TAP_SOURCES], axis=1
    )


def load_pool(sources, pool, sems):
    copies, at = ([], 0)
    for k, source in enumerate(sources):
        rows = source.shape[0]
        copies.append(pltpu.make_async_copy(source, pool.at[pl.ds(at, rows)], sems.at[k]))
        at += rows
    for copy in copies:
        copy.start()
    for copy in copies:
        copy.wait()


def inner_tile(region, lane):
    value = region[pl.ds(HALO * REGION, SIDE * REGION), pl.ds(lane * CHANS, CHANS)].astype(F32)
    value = value.reshape(SIDE, REGION, CHANS)[:, HALO : HALO + SIDE, :]
    return value.astype(BF)


INNER = (HALO * REGION, SIDE * REGION)


def forward_kernel(
    meta, owner, near, *refs
):
    sources, refs = (refs[:SOURCES], refs[SOURCES:])
    (w_red, w_tap, w_exp, norms, s_one, s_two, s_three, a_own, h_one, h_two, out,
     pool, sems, region, present, masks, shifted) = refs
    pair = pl.program_id(0)
    here, section = (meta[0], meta[1])

    @pl.when(pair == 0)
    def _():
        load_pool(sources, pool, sems)
        build_masks(masks)

    founds = []
    for lane in range(2):
        places, found = around(meta[2 + pair * 2 + lane], owner, near, here)
        build_region(pool, region, lane, places, found)
        founds.append(found)
    build_present(present, founds)

    def block(b, carry):
        mine = b == section

        @pl.when(mine)
        def _():
            a_own[0] = region[pl.ds(*INNER), :]

        def front(j, c):
            start = pl.multiple_of(j * 256, 256)
            rows = pl.ds(start, 256)
            pre = mm(region[rows, :], w_red[b]) * norms[b, 0:1, :128] + norms[b, 1:2, :128]
            hidden, slope = silu_parts(pre)
            there = present[rows, :]
            s_one[0, b, rows, :] = (slope * there * norms[b, 0:1, :128]).astype(BF)
            store_shifted(shifted, masks, start, hidden * there)
            return c

        lax.fori_loop(0, 4, front, 0)

        def tail(j, c):
            start = pl.multiple_of(REGION + j * 320, 32)
            rows = pl.ds(start, 320)
            pre = mm(columns_at(shifted, start, 320), w_tap[b])
            pre = pre * norms[b, 2:3, :128] + norms[b, 3:4, :128]
            hidden, slope = silu_parts(pre)
            s_two[0, b, rows, :] = (slope * norms[b, 2:3, :128]).astype(BF)
            hidden = hidden.astype(BF)

            @pl.when(mine)
            def _():
                h_two[0, rows, :] = hidden

            pre = (
                region[rows, :].astype(F32)
                + mm(hidden, w_exp[b]) * norms[b, 4:5, :]
                + norms[b, 5:6, :]
            )
            value, slope = silu_parts(pre)
            region[rows, :] = value.astype(BF)
            s_three[0, b, rows, :] = slope.astype(BF)
            return c

        lax.fori_loop(0, 3, tail, 0)

        @pl.when(mine)
        def _():
            h_one[0] = shifted[1]
            out[0] = inner_tile(region, 0)
            out[1] = inner_tile(region, 1)

        return carry

    lax.fori_loop(0, 4, block, 0)


def fold_pair(value, rows, cols):
    return value[:rows, :cols] + value[rows:, cols:]


def backward_kernel(meta, owner, near, *refs):
    sources, refs = (refs[:SOURCES], refs[SOURCES:])
    (w_red, w_tap, w_exp, norms, s_one, s_two, s_three, a_own, h_one, h_two, grad_in, grads,
     pool, sems, region, masks, shifted, d_one, total) = refs
    pair = pl.program_id(0)
    here, section = (meta[0], meta[1])

    @pl.when(pair == 0)
    def _():
        load_pool(sources, pool, sems)
        build_masks(masks)
        total[...] = jnp.zeros_like(total)

    for lane in range(2):
        places, found = around(meta[2 + pair * 2 + lane], owner, near, here)
        build_region(pool, region, lane, places, found)

    def keep_inner(value):
        col = lax.broadcasted_iota(jnp.int32, value.shape, 0) % REGION
        return jnp.where((col >= HALO) & (col < HALO + SIDE), value, 0.0).astype(BF)

    def block(step, carry):
        b = 3 - step
        mine = b == section

        def first(j, c):
            start = pl.multiple_of(4 * REGION + j * 256, 128)
            rows = pl.ds(start, 256)
            d_three = region[rows, :].astype(F32) * s_three[0, b, rows, :].astype(F32)
            e_three = (d_three * norms[b, 4:5, :]).astype(BF)
            d_two = mm(e_three, w_exp[b]) * s_two[0, b, rows, :].astype(F32)
            store_shifted(shifted, masks, start, d_two)
            return c

        lax.fori_loop(0, 3, first, 0)

        @pl.when(mine)
        def _():
            rows = pl.ds(*INNER)
            d_three = region[rows, :].astype(F32) * s_three[0, b, rows, :].astype(F32)
            e_three = keep_inner(d_three * norms[b, 4:5, :])
            total_e = fold_pair(mm_first(h_two[0, rows, :], e_three), WIDTH, CHANS)
            total[416:480, :] += total_e[:, :128]
            total[480:544, :] += total_e[:, 128:]
            d_two = keep_inner(shifted[1, rows, :].astype(F32))
            around_rows = pl.ds(INNER[0] - REGION, INNER[1] + 2 * REGION)
            hidden = h_one[0, around_rows, :].astype(F32)
            left = pltpu.roll(hidden, 1, 0).astype(BF)
            right = pltpu.roll(hidden, hidden.shape[0] - 1, 0).astype(BF)
            middle = hidden.astype(BF)
            gated = [
                (left * masks[0, around_rows, :], 0), (middle, 0), (right * masks[1, around_rows, :], 0),
                (left, 1), (middle, 1), (right, 1),
                (left * masks[2, around_rows, :], 2), (middle, 2), (right * masks[3, around_rows, :], 2),
            ]
            for tap, (value, dy) in enumerate(gated):
                column = value[dy * REGION : dy * REGION + INNER[1]]
                piece = fold_pair(mm_first(column, d_two), WIDTH, WIDTH)
                if tap < 4:
                    total[tap * 64 : tap * 64 + 64, :64] += piece
                elif tap > 4:
                    at = (tap - 5) * 64 + 32
                    total[at : at + 64, 64:] += piece
                else:
                    total[256:288, :64] += piece[:32]
                    total[0:32, 64:] += piece[32:]

        def second(j, c):
            start = pl.multiple_of(5 * REGION + j * 352, 32)
            rows = pl.ds(start, 352)
            d_hidden = mm(columns_at(shifted, start, 352), w_tap[b])
            d_first = (d_hidden * s_one[0, b, rows, :].astype(F32)).astype(BF)
            d_one[rows, :] = d_first
            d_three = region[rows, :].astype(F32) * s_three[0, b, rows, :].astype(F32)
            region[rows, :] = (d_three + mm(d_first, w_red[b])).astype(BF)
            return c

        lax.fori_loop(0, 2, second, 0)

        @pl.when(mine)
        def _():
            rows = pl.ds(*INNER)
            d_first = keep_inner(d_one[rows, :].astype(F32))
            piece = fold_pair(mm_first(a_own[0], d_first), CHANS, WIDTH)
            total[288:416, :64] += piece[:128]
            total[288:416, 64:] += piece[128:]
            grad_in[0] = inner_tile(region, 0)
            grad_in[1] = inner_tile(region, 1)

        return carry

    lax.fori_loop(0, 4, block, 0)

    @pl.when(pair == 1)
    def _():
        grads[...] = total[...].astype(BF)


SOURCES = 6


def run_kernel(body, scalars, sources, weights, blocked, outs, scratch):
    any_spec = pl.BlockSpec(memory_space=pl.ANY)

    def whole(item):
        return pl.BlockSpec(item.shape, lambda i, *_, n=len(item.shape): (0,) * n)

    def split(shape, count):
        return pl.BlockSpec(
            (count,) + tuple(shape[1:]), lambda i, *_, n=len(shape): (i,) + (0,) * (n - 1)
        )

    in_specs = (
        [any_spec] * len(sources)
        + [whole(item) for item in weights]
        + [split(item.shape, item.shape[0] // 2) for item in blocked]
    )
    out_specs = [whole(o) if fixed else split(o.shape, o.shape[0] // 2) for o, fixed in outs]
    return pl.pallas_call(
        body,
        grid_spec=pltpu.PrefetchScalarGridSpec(
            num_scalar_prefetch=len(scalars),
            grid=(2,),
            in_specs=in_specs,
            out_specs=out_specs,
            scratch_shapes=scratch,
        ),
        out_shape=[o for o, _ in outs],
        compiler_params=pltpu.CompilerParams(
            dimension_semantics=("arbitrary",), vmem_limit_bytes=VMEM_LIMIT
        ),
    )(*scalars, *sources, *weights, *blocked)


def shift(block, axes, distance):
    devices = range(lax.axis_size(axes))
    return lax.ppermute(block, axes, [(i, i + distance) for i in devices if i + distance in devices])


def other_core(block):
    return lax.ppermute(block, "core", [(0, 1), (1, 0)])


def gather_pool(own):
    close = jnp.concatenate([shift(own, TILE_AXES, 2), shift(own, TILE_AXES, -2)])
    far = jnp.concatenate([shift(own, TILE_AXES, 4), shift(own, TILE_AXES, -4)])
    return [own, close, far, other_core(own), other_core(close), other_core(far)]


def swap_chunks(parts, axes):
    return lax.all_to_all(parts, axes, 0, 0, tiled=True)


def sum_over_tiles(values):
    plane = ("y", "core")
    across = lax.axis_size(plane)
    deep = lax.axis_size("z")
    parts = values.reshape(across, -1)
    mine = jnp.sum(swap_chunks(parts, plane).astype(F32), axis=0)
    copies = jnp.broadcast_to(mine.astype(BF)[None], (deep,) + mine.shape)
    total = jnp.sum(swap_chunks(copies, "z").astype(F32), axis=0)
    copies = jnp.broadcast_to(total.astype(BF)[None], (across,) + total.shape)
    return swap_chunks(copies, plane).astype(F32).reshape(values.shape)


def split_float(value):
    high = value.astype(BF)
    low = (value - high.astype(F32)).astype(BF)
    return (high, low)


def gather_params(w_reduce, w_taps, w_expand, norm_scale, norm_shift):
    pieces = [w_reduce, w_taps, w_expand]
    for item in (norm_scale, norm_shift):
        pieces.extend(split_float(item))
    packed = jnp.concatenate([item.reshape(-1, 128) for item in pieces])
    every = lax.all_gather(packed, "section", axis=0, tiled=False)
    at = 0
    cut = []
    for item in pieces:
        rows = item.size // 128
        cut.append(every[:, at : at + rows].reshape((-1,) + item.shape[1:]))
        at += rows
    scale = cut[3].astype(F32) + cut[4].astype(F32)
    offset = cut[5].astype(F32) + cut[6].astype(F32)
    return (cut[0], cut[1], cut[2], scale, offset)


def twice(weights):
    zero = jnp.zeros_like(weights)
    return jnp.concatenate(
        [jnp.concatenate([weights, zero], axis=-1), jnp.concatenate([zero, weights], axis=-1)],
        axis=-2,
    )


def norm_rows(scale, offset):
    rows = []
    for low, high in ((0, 64), (64, 128), (128, 384)):
        for item in (scale, offset):
            part = jnp.concatenate([item[:, low:high]] * 2, axis=1)
            rows.append(jnp.pad(part, ((0, 0), (0, 512 - part.shape[1]))))
    rows.extend([jnp.zeros_like(rows[0])] * 2)
    return jnp.stack(rows, axis=1)


def on_device(
    features, out_cotangent, w_reduce, w_taps, w_expand, norm_scale, norm_shift, owner, neighbours
):
    here = lax.axis_index(TILE_AXES).astype(jnp.int32)
    section = lax.axis_index("section").astype(jnp.int32)
    slots = here * 4 + jnp.arange(4, dtype=jnp.int32)
    hit = owner[None, :] == slots[:, None]
    ids = jnp.sum(
        jnp.where(hit, jnp.arange(owner.shape[0], dtype=jnp.int32)[None, :], 0), axis=1
    )
    meta = jnp.concatenate([here[None], section[None], ids.astype(jnp.int32)])
    scalars = (meta, owner, neighbours.reshape(-1))

    sources = gather_pool(features)
    w_red, w_tap, w_exp, scale, offset = gather_params(
        w_reduce, w_taps, w_expand, norm_scale, norm_shift
    )
    taps = w_tap.reshape(4, TAPS, WIDTH, WIDTH)
    norms = norm_rows(scale, offset)
    ahead = (twice(w_red), twice(taps).reshape(4, TAPS * 128, 128), twice(w_exp), norms)
    back = (
        twice(w_red.swapaxes(1, 2)),
        twice(taps[:, ::-1].swapaxes(2, 3)).reshape(4, TAPS * 128, 128),
        twice(w_exp.swapaxes(1, 2)),
        norms,
    )
    waiting, *sources = lax.optimization_barrier((out_cotangent, *sources))
    later = gather_pool(waiting)

    def like(*shape):
        return jax.ShapeDtypeStruct(shape, BF)

    pool = [pltpu.VMEM((40, SIDE, SIDE, CHANS), BF), pltpu.SemaphoreType.DMA((SOURCES,))]
    region = pltpu.VMEM((PIXELS, 2 * CHANS), BF)
    narrow = (PIXELS, 2 * WIDTH)
    s_one, s_two, s_three, a_own, h_one, h_two, out = run_kernel(
        forward_kernel,
        scalars,
        sources,
        ahead,
        (),
        [
            (like(2, 4, *narrow), False),
            (like(2, 4, *narrow), False),
            (like(2, 4, PIXELS, 2 * CHANS), False),
            (like(2, INNER[1], 2 * CHANS), False),
            (like(2, *narrow), False),
            (like(2, *narrow), False),
            (like(4, SIDE, SIDE, CHANS), False),
        ],
        pool
        + [region, pltpu.VMEM(narrow, F32), pltpu.VMEM((4,) + narrow, BF), pltpu.VMEM((7,) + narrow, BF)],
    )
    grad_in, grads = run_kernel(
        backward_kernel,
        scalars,
        later,
        back,
        (s_one, s_two, s_three, a_own, h_one, h_two),
        [(like(4, SIDE, SIDE, CHANS), False), (like(544, 128), True)],
        pool
        + [
            region,
            pltpu.VMEM((4,) + narrow, BF),
            pltpu.VMEM((7,) + narrow, BF),
            pltpu.VMEM(narrow, BF),
            pltpu.VMEM((544, 128), F32),
        ],
    )
    total = sum_over_tiles(grads)
    g_taps = jnp.concatenate([total[:288, :64], total[:288, 64:]])
    g_reduce = jnp.concatenate([total[288:416, :64], total[288:416, 64:]])
    g_expand = jnp.concatenate([total[416:480], total[480:544]], axis=1)
    return (out[None], grad_in[None], g_reduce[None], g_taps[None], g_expand[None])


def fine_mesh(mesh):
    shape = (mesh.devices.shape[0], mesh.devices.shape[1] // 16, 8, 2)
    return Mesh(mesh.devices.reshape(shape), ("section",) + TILE_AXES)


def solution(mesh):
    tiles = P(TILE_AXES, None, None, None)
    owned = P("section", TILE_AXES, None, None, None)
    weights = P("section", None, None)
    return jax.shard_map(
        on_device,
        mesh=fine_mesh(mesh),
        in_specs=(
            tiles, tiles, weights, weights, weights, P("section", None), P("section", None), P(), P(),
        ),
        out_specs=(owned, owned, weights, weights, weights),
        check_vma=False,
    )
```

profile of v0, /device:TPU:1, one launch (start us, length us, event | category | flops | bytes accessed | tf_op | source)
XLA Modules:
  0.0 231.8 jit_solution(4176806496850262026)
XLA Ops:
  0.6 4.1 %collective-permute-start = (bf16[4,16,16,256]{3,2,1,0:T(8,128)(2,1)}, bf16[4,16,16,256]{3,2,1,0:T(8,128)(2,1)S(1)}, u32[]{:S(2)}, u32[]{:S(2)}) collective-permute-start(bf16[4,16,16,256]{3,2,1,0:T(8,128)(2,1)} %refs_0_), channel_id=1, source_target_pairs={{0,2},{1,3},{2,4},{3,5},{4,6},{5,7},{6,8},{7,9},{8,10},{9,11},{10,... | collective-permute-start | bytes 1572872 | tf_op jit(solution)/shard_map/ppermute | solution.py:367
  6.0 5.8 %collective-permute-start.2 = (bf16[4,16,16,256]{3,2,1,0:T(8,128)(2,1)}, bf16[4,16,16,256]{3,2,1,0:T(8,128)(2,1)}, u32[]{:S(2)}, u32[]{:S(2)}) collective-permute-start(bf16[4,16,16,256]{3,2,1,0:T(8,128)(2,1)} %refs_0_), channel_id=1, source_target_pairs={{0,4},{1,5},{2,6},{3,7},{4,8},{5,9},{6,10},{7,11},{8,12},{9,13},{1... | collective-permute-start | bytes 1572872 | tf_op jit(solution)/shard_map/ppermute | solution.py:367
  13.1 3.4 %collective-permute-start.4 = (bf16[4,16,16,256]{3,2,1,0:T(8,128)(2,1)}, bf16[4,16,16,256]{3,2,1,0:T(8,128)(2,1)}, u32[]{:S(2)}, u32[]{:S(2)}) collective-permute-start(bf16[4,16,16,256]{3,2,1,0:T(8,128)(2,1)} %refs_0_), channel_id=1, source_target_pairs={{0,1},{1,0},{2,3},{3,2},{4,5},{5,4},{6,7},{7,6},{8,9},{9,8},{10,11... | collective-permute-start | bytes 1572872 | tf_op jit(solution)/shard_map/ppermute | solution.py:371
  21.2 11.5 %all-gather.1 = bf16[4,556,128]{2,1,0:T(8,128)(2,1)S(1)} all-gather(bf16[1,556,128]{2,1,0:T(8,128)(2,1)S(1)} %bitcast.34), channel_id=2, replica_groups=mesh['section'=4,'z'=8,'y'=8,'core'=2] {'section'}, dimensions={0}, use_global_device_ids=true | all-gather | bytes 711680 | tf_op jit(solution)/shard_map/all_gather | solution.py:407
  32.8 4.0 %collective-permute-start.5 = (bf16[8,16,16,256]{3,2,1,0:T(8,128)(2,1)S(1)}, bf16[8,16,16,256]{3,2,1,0:T(8,128)(2,1)S(1)}, u32[]{:S(2)}, u32[]{:S(2)}) collective-permute-start(bf16[8,16,16,256]{3,2,1,0:T(8,128)(2,1)S(1)} %constant_dynamic-update-slice_fusion.refs_1_), channel_id=1, source_target_pairs={{0,1},{1,0},{2,3},{3,2},{4,5},{5,4},{6,7},{7,6},{8,9},{9,8},{10,11... | collective-permute-start | bytes 3145736 | tf_op jit(solution)/shard_map/ppermute | solution.py:371
  37.8 5.0 %collective-permute-done.3 = bf16[4,16,16,256]{3,2,1,0:T(8,128)(2,1)} collective-permute-done((bf16[4,16,16,256]{3,2,1,0:T(8,128)(2,1)}, bf16[4,16,16,256]{3,2,1,0:T(8,128)(2,1)}, u32[]{:S(2)}, u32[]{:S(2)}) %collective-permute-start.3) | collective-permute-done | bytes 524320 | tf_op jit(solution)/shard_map/ppermute | solution.py:367
  43.9 3.8 %collective-permute-start.6 = (bf16[8,16,16,256]{3,2,1,0:T(8,128)(2,1)S(1)}, bf16[8,16,16,256]{3,2,1,0:T(8,128)(2,1)S(1)}, u32[]{:S(2)}, u32[]{:S(2)}) collective-permute-start(bf16[8,16,16,256]{3,2,1,0:T(8,128)(2,1)S(1)} %constant_dynamic-update-slice_fusion.2.refs_2_), channel_id=1, source_target_pairs={{0,1},{1,0},{2,3},{3,2},{4,5},{5,4},{6,7},{7,6},{8,9},{9,8},{10,11... | collective-permute-start | bytes 3145736 | tf_op jit(solution)/shard_map/ppermute | solution.py:371
  48.1 1.8 collective-permute-done.6.refs_5_
  50.0 2.1 collective-permute-start.7
  53.5 9.3 %collective-permute-start.9 = (bf16[4,16,16,256]{3,2,1,0:T(8,128)(2,1)}, bf16[4,16,16,256]{3,2,1,0:T(8,128)(2,1)}, u32[]{:S(2)}, u32[]{:S(2)}) collective-permute-start(bf16[4,16,16,256]{3,2,1,0:T(8,128)(2,1)} %refs_0_.1), channel_id=1, source_target_pairs={{0,4},{1,5},{2,6},{3,7},{4,8},{5,9},{6,10},{7,11},{8,12},{9,13},{1... | collective-permute-start | bytes 1572872 | tf_op jit(solution)/shard_map/ppermute | solution.py:367
  65.4 1.9 constant_dynamic-update-slice_fusion.5
  67.3 3.6 %collective-permute-done.8 = bf16[4,16,16,256]{3,2,1,0:T(8,128)(2,1)} collective-permute-done((bf16[4,16,16,256]{3,2,1,0:T(8,128)(2,1)}, bf16[4,16,16,256]{3,2,1,0:T(8,128)(2,1)}, u32[]{:S(2)}, u32[]{:S(2)}) %collective-permute-start.8) | collective-permute-done | bytes 524320 | tf_op jit(solution)/shard_map/ppermute | solution.py:367
  70.9 1.9 constant_dynamic-update-slice_fusion.4.refs_1_
  72.7 3.1 %collective-permute-start.12 = (bf16[8,16,16,256]{3,2,1,0:T(8,128)(2,1)}, bf16[8,16,16,256]{3,2,1,0:T(8,128)(2,1)}, u32[]{:S(2)}, u32[]{:S(2)}) collective-permute-start(bf16[8,16,16,256]{3,2,1,0:T(8,128)(2,1)} %constant_dynamic-update-slice_fusion.4.refs_1_), channel_id=1, source_target_pairs={{0,1},{1,0},{2,3},{3,2},{4,5},{5,4},{6,7},{7,6},{8,9},{9,8},{10,11... | collective-permute-start | bytes 3145736 | tf_op jit(solution)/shard_map/ppermute | solution.py:371
  76.9 17.2 %collective-permute-done.10 = bf16[4,16,16,256]{3,2,1,0:T(8,128)(2,1)} collective-permute-done((bf16[4,16,16,256]{3,2,1,0:T(8,128)(2,1)}, bf16[4,16,16,256]{3,2,1,0:T(8,128)(2,1)}, u32[]{:S(2)}, u32[]{:S(2)}) %collective-permute-start.10) | collective-permute-done | bytes 524320 | tf_op jit(solution)/shard_map/ppermute | solution.py:367
  95.3 3.4 %collective-permute-start.13 = (bf16[8,16,16,256]{3,2,1,0:T(8,128)(2,1)S(1)}, bf16[8,16,16,256]{3,2,1,0:T(8,128)(2,1)}, u32[]{:S(2)}, u32[]{:S(2)}) collective-permute-start(bf16[8,16,16,256]{3,2,1,0:T(8,128)(2,1)S(1)} %constant_dynamic-update-slice_fusion.6.refs_2_), channel_id=1, source_target_pairs={{0,1},{1,0},{2,3},{3,2},{4,5},{5,4},{6,7},{7,6},{8,9},{9,8},{10,11... | collective-permute-start | bytes 3145736 | tf_op jit(solution)/shard_map/ppermute | solution.py:371
  101.8 1.9 collective-permute-start.11
  108.2 1.4 fusion.5
  109.6 38.9 %shard_map.128 = (bf16[2,4,1024,128]{3,2,1,0:T(8,128)(2,1)}, bf16[2,4,1024,128]{3,2,1,0:T(8,128)(2,1)}, bf16[2,4,1024,512]{3,2,1,0:T(8,128)(2,1)}, bf16[2,512,51...) custom-call(s32[6]{0:T(128)} %pad_add_fusion.meta, ...), custom_call_target="tpu_custom_call" | custom-call | tf_op jit(solution)/shard_map/pallas_call | solution.py:349
  148.5 30.1 %shard_map.129 = (bf16[4,16,16,256]{3,2,1,0:T(8,128)(2,1)}, bf16[544,128]{1,0:T(8,128)(2,1)}) custom-call(s32[6]{0:T(128)} %pad_add_fusion.meta, s32[512]{0:T(512)} %owner.3, s32[2048]{0:T(1024)} %reshape.81.near, bf16[4,16,16,256]{3,2,1,0:T(8,128)(2,1)} %refs_0_.1, bf16[8,16,16,256]{3,2,1,0:T(8,128)(2,1)} %constant_dynamic-update-slice_fusion.4.refs_1_, ...), custom_call_target="tpu_custom_call" | custom-call | tf_op jit(solution)/shard_map/pallas_call | solution.py:349
  181.6 14.0 %all_to_all.22 = bf16[16,2,2176]{2,1,0:T(2,128)(2,1)S(1)} all-to-all(bf16[16,2,2176]{2,1,0:T(2,128)(2,1)S(1)} %reshape.102), channel_id=1, replica_groups=mesh['section'=4,'z'=8,'y'=8,'core'=2] {'y','core'}, dimensions={0} | all-to-all | bytes 278528 | tf_op jit(solution)/shard_map/all_to_all | solution.py:381
  197.1 17.1 %all_to_all.23 = bf16[8,2,2176]{2,1,0:T(2,128)(2,1)S(1)} all-to-all(bf16[8,2,2176]{2,1,0:T(2,128)(2,1)S(1)} %reshape.104), channel_id=1, replica_groups=mesh['section'=4,'z'=8,'y'=8,'core'=2] {'z'}, dimensions={0} | all-to-all | bytes 139264 | tf_op jit(solution)/shard_map/all_to_all | solution.py:381
  214.6 1.4 reduce.14
  216.1 12.9 %all_to_all.24 = bf16[16,2,2176]{2,1,0:T(2,128)(2,1)S(1)} all-to-all(bf16[16,2,2176]{2,1,0:T(2,128)(2,1)S(1)} %reshape.106), channel_id=1, replica_groups=mesh['section'=4,'z'=8,'y'=8,'core'=2] {'y','core'}, dimensions={0} | all-to-all | bytes 278528 | tf_op jit(solution)/shard_map/all_to_all | solution.py:381
  (104 shorter events, 30.9 us)
Async XLA Ops:
  0.6 32.0 %collective-permute-start = (bf16[4,16,16,256]{3,2,1,0:T(8,128)(2,1)}, bf16[4,16,16,256]{3,2,1,0:T(8,128)(2,1)S(1)}, u32[]{:S(2)}, u32[]{:S(2)}) collective-permute-start(bf16[4,16,16,256]{3,2,1,0:T(8,128)(2,1)} %refs_0_), channel_id=1, source_target_pairs={{0,2},{1,3},{2,4},{3,5},{4,6},{5,7},{6,8},{7,9},{8,10},{9,11},{10,... | collective-permute-start | bytes 1572872 | tf_op jit(solution)/shard_map/ppermute | solution.py:367
  4.7 28.0 %collective-permute-start.1 = (bf16[4,16,16,256]{3,2,1,0:T(8,128)(2,1)}, bf16[4,16,16,256]{3,2,1,0:T(8,128)(2,1)S(1)}, u32[]{:S(2)}, u32[]{:S(2)}) collective-permute-start(bf16[4,16,16,256]{3,2,1,0:T(8,128)(2,1)} %refs_0_), channel_id=1, source_target_pairs={{2,0},{3,1},{4,2},{5,3},{6,4},{7,5},{8,6},{9,7},{10,8},{11,9},{12,... | collective-permute-start | bytes 1572872 | tf_op jit(solution)/shard_map/ppermute | solution.py:367
  6.0 30.8 %collective-permute-start.2 = (bf16[4,16,16,256]{3,2,1,0:T(8,128)(2,1)}, bf16[4,16,16,256]{3,2,1,0:T(8,128)(2,1)}, u32[]{:S(2)}, u32[]{:S(2)}) collective-permute-start(bf16[4,16,16,256]{3,2,1,0:T(8,128)(2,1)} %refs_0_), channel_id=1, source_target_pairs={{0,4},{1,5},{2,6},{3,7},{4,8},{5,9},{6,10},{7,11},{8,12},{9,13},{1... | collective-permute-start | bytes 1572872 | tf_op jit(solution)/shard_map/ppermute | solution.py:367
  11.8 31.0 %collective-permute-start.3 = (bf16[4,16,16,256]{3,2,1,0:T(8,128)(2,1)}, bf16[4,16,16,256]{3,2,1,0:T(8,128)(2,1)}, u32[]{:S(2)}, u32[]{:S(2)}) collective-permute-start(bf16[4,16,16,256]{3,2,1,0:T(8,128)(2,1)} %refs_0_), channel_id=1, source_target_pairs={{4,0},{5,1},{6,2},{7,3},{8,4},{9,5},{10,6},{11,7},{12,8},{13,9},{1... | collective-permute-start | bytes 1572872 | tf_op jit(solution)/shard_map/ppermute | solution.py:367
  13.1 35.0 %collective-permute-start.4 = (bf16[4,16,16,256]{3,2,1,0:T(8,128)(2,1)}, bf16[4,16,16,256]{3,2,1,0:T(8,128)(2,1)}, u32[]{:S(2)}, u32[]{:S(2)}) collective-permute-start(bf16[4,16,16,256]{3,2,1,0:T(8,128)(2,1)} %refs_0_), channel_id=1, source_target_pairs={{0,1},{1,0},{2,3},{3,2},{4,5},{5,4},{6,7},{7,6},{8,9},{9,8},{10,11... | collective-permute-start | bytes 1572872 | tf_op jit(solution)/shard_map/ppermute | solution.py:371
  32.7 15.2 %copy-start.5 = (s32[512]{0:T(512)S(1)}, s32[512]{0:T(512)}, u32[]{:S(2)}) copy-start(s32[512]{0:T(512)} %owner.3) | copy-start | bytes 6148
  32.8 34.5 %copy-start = (bf16[8,16,16,256]{3,2,1,0:T(8,128)(2,1)}, bf16[8,16,16,256]{3,2,1,0:T(8,128)(2,1)S(1)}, u32[]{:S(2)}) copy-start(bf16[8,16,16,256]{3,2,1,0:T(8,128)(2,1)S(1)} %constant_dynamic-update-slice_fusion.refs_1_) | copy-start | bytes 3145732
  32.8 15.3 %collective-permute-start.5 = (bf16[8,16,16,256]{3,2,1,0:T(8,128)(2,1)S(1)}, bf16[8,16,16,256]{3,2,1,0:T(8,128)(2,1)S(1)}, u32[]{:S(2)}, u32[]{:S(2)}) collective-permute-start(bf16[8,16,16,256]{3,2,1,0:T(8,128)(2,1)S(1)} %constant_dynamic-update-slice_fusion.refs_1_), channel_id=1, source_target_pairs={{0,1},{1,0},{2,3},{3,2},{4,5},{5,4},{6,7},{7,6},{8,9},{9,8},{10,11... | collective-permute-start | bytes 3145736 | tf_op jit(solution)/shard_map/ppermute | solution.py:371
  43.9 33.0 %copy-start.1 = (bf16[8,16,16,256]{3,2,1,0:T(8,128)(2,1)}, bf16[8,16,16,256]{3,2,1,0:T(8,128)(2,1)S(1)}, u32[]{:S(2)}) copy-start(bf16[8,16,16,256]{3,2,1,0:T(8,128)(2,1)S(1)} %constant_dynamic-update-slice_fusion.2.refs_2_) | copy-start | bytes 3145732
  43.9 6.0 %collective-permute-start.6 = (bf16[8,16,16,256]{3,2,1,0:T(8,128)(2,1)S(1)}, bf16[8,16,16,256]{3,2,1,0:T(8,128)(2,1)S(1)}, u32[]{:S(2)}, u32[]{:S(2)}) collective-permute-start(bf16[8,16,16,256]{3,2,1,0:T(8,128)(2,1)S(1)} %constant_dynamic-update-slice_fusion.2.refs_2_), channel_id=1, source_target_pairs={{0,1},{1,0},{2,3},{3,2},{4,5},{5,4},{6,7},{7,6},{8,9},{9,8},{10,11... | collective-permute-start | bytes 3145736 | tf_op jit(solution)/shard_map/ppermute | solution.py:371
  48.1 16.2 %copy-start.3 = (bf16[8,16,16,256]{3,2,1,0:T(8,128)(2,1)}, bf16[8,16,16,256]{3,2,1,0:T(8,128)(2,1)S(1)}, u32[]{:S(2)}) copy-start(bf16[8,16,16,256]{3,2,1,0:T(8,128)(2,1)S(1)} %collective-permute-done.5.refs_4_) | copy-start | bytes 3145732
  50.0 14.3 %copy-start.4 = (bf16[8,16,16,256]{3,2,1,0:T(8,128)(2,1)}, bf16[8,16,16,256]{3,2,1,0:T(8,128)(2,1)S(1)}, u32[]{:S(2)}) copy-start(bf16[8,16,16,256]{3,2,1,0:T(8,128)(2,1)S(1)} %collective-permute-done.6.refs_5_) | copy-start | bytes 3145732
  50.0 15.4 %collective-permute-start.7 = (bf16[4,16,16,256]{3,2,1,0:T(8,128)(2,1)}, bf16[4,16,16,256]{3,2,1,0:T(8,128)(2,1)}, u32[]{:S(2)}, u32[]{:S(2)}) collective-permute-start(bf16[4,16,16,256]{3,2,1,0:T(8,128)(2,1)} %refs_0_.1), channel_id=1, source_target_pairs={{0,2},{1,3},{2,4},{3,5},{4,6},{5,7},{6,8},{7,9},{8,10},{9,11},{10,... | collective-permute-start | bytes 1572872 | tf_op jit(solution)/shard_map/ppermute | solution.py:367
  52.1 18.7 %collective-permute-start.8 = (bf16[4,16,16,256]{3,2,1,0:T(8,128)(2,1)}, bf16[4,16,16,256]{3,2,1,0:T(8,128)(2,1)}, u32[]{:S(2)}, u32[]{:S(2)}) collective-permute-start(bf16[4,16,16,256]{3,2,1,0:T(8,128)(2,1)} %refs_0_.1), channel_id=1, source_target_pairs={{2,0},{3,1},{4,2},{5,3},{6,4},{7,5},{8,6},{9,7},{10,8},{11,9},{12,... | collective-permute-start | bytes 1572872 | tf_op jit(solution)/shard_map/ppermute | solution.py:367
  53.5 22.3 %collective-permute-start.9 = (bf16[4,16,16,256]{3,2,1,0:T(8,128)(2,1)}, bf16[4,16,16,256]{3,2,1,0:T(8,128)(2,1)}, u32[]{:S(2)}, u32[]{:S(2)}) collective-permute-start(bf16[4,16,16,256]{3,2,1,0:T(8,128)(2,1)} %refs_0_.1), channel_id=1, source_target_pairs={{0,4},{1,5},{2,6},{3,7},{4,8},{5,9},{6,10},{7,11},{8,12},{9,13},{1... | collective-permute-start | bytes 1572872 | tf_op jit(solution)/shard_map/ppermute | solution.py:367
  62.9 31.3 %collective-permute-start.10 = (bf16[4,16,16,256]{3,2,1,0:T(8,128)(2,1)}, bf16[4,16,16,256]{3,2,1,0:T(8,128)(2,1)}, u32[]{:S(2)}, u32[]{:S(2)}) collective-permute-start(bf16[4,16,16,256]{3,2,1,0:T(8,128)(2,1)} %refs_0_.1), channel_id=1, source_target_pairs={{4,0},{5,1},{6,2},{7,3},{8,4},{9,5},{10,6},{11,7},{12,8},{13,9},{1... | collective-permute-start | bytes 1572872 | tf_op jit(solution)/shard_map/ppermute | solution.py:367
  72.7 75.8 %collective-permute-start.12 = (bf16[8,16,16,256]{3,2,1,0:T(8,128)(2,1)}, bf16[8,16,16,256]{3,2,1,0:T(8,128)(2,1)}, u32[]{:S(2)}, u32[]{:S(2)}) collective-permute-start(bf16[8,16,16,256]{3,2,1,0:T(8,128)(2,1)} %constant_dynamic-update-slice_fusion.4.refs_1_), channel_id=1, source_target_pairs={{0,1},{1,0},{2,3},{3,2},{4,5},{5,4},{6,7},{7,6},{8,9},{9,8},{10,11... | collective-permute-start | bytes 3145736 | tf_op jit(solution)/shard_map/ppermute | solution.py:371
  95.3 8.9 %copy-start.2 = (bf16[8,16,16,256]{3,2,1,0:T(8,128)(2,1)}, bf16[8,16,16,256]{3,2,1,0:T(8,128)(2,1)S(1)}, u32[]{:S(2)}) copy-start(bf16[8,16,16,256]{3,2,1,0:T(8,128)(2,1)S(1)} %constant_dynamic-update-slice_fusion.6.refs_2_) | copy-start | bytes 3145732
  95.3 53.2 %collective-permute-start.13 = (bf16[8,16,16,256]{3,2,1,0:T(8,128)(2,1)S(1)}, bf16[8,16,16,256]{3,2,1,0:T(8,128)(2,1)}, u32[]{:S(2)}, u32[]{:S(2)}) collective-permute-start(bf16[8,16,16,256]{3,2,1,0:T(8,128)(2,1)S(1)} %constant_dynamic-update-slice_fusion.6.refs_2_), channel_id=1, source_target_pairs={{0,1},{1,0},{2,3},{3,2},{4,5},{5,4},{6,7},{7,6},{8,9},{9,8},{10,11... | collective-permute-start | bytes 3145736 | tf_op jit(solution)/shard_map/ppermute | solution.py:371
  98.9 5.2 %copy-start.6 = (s32[512,4]{0,1:T(4,128)S(1)}, s32[512,4]{0,1:T(4,128)}, u32[]{:S(2)}) copy-start(s32[512,4]{0,1:T(4,128)} %param.17) | copy-start | bytes 24580
  101.8 46.7 %collective-permute-start.11 = (bf16[4,16,16,256]{3,2,1,0:T(8,128)(2,1)}, bf16[4,16,16,256]{3,2,1,0:T(8,128)(2,1)}, u32[]{:S(2)}, u32[]{:S(2)}) collective-permute-start(bf16[4,16,16,256]{3,2,1,0:T(8,128)(2,1)} %refs_0_.1), channel_id=1, source_target_pairs={{0,1},{1,0},{2,3},{3,2},{4,5},{5,4},{6,7},{7,6},{8,9},{9,8},{10,11... | collective-permute-start | bytes 1572872 | tf_op jit(solution)/shard_map/ppermute | solution.py:371
where the time goes:
time: 233 us; the launch traced here: 232 us
  Pallas kernels  69 us (30%)
  blocking collectives  55.5 us (24%)
  starting transfers between devices  46 us (20%)
  waiting for transfers between devices  27.7 us (12%)
  local copies, waits for them, and re-layouts  17.9 us (8%)
  other arithmetic  14.5 us (6%)
    pallas_call x2, Pallas kernels, run_kernel(): pl.pallas_call(body, grid_spec=pltpu.PrefetchScalarGridSpec(num_scalar_pr...  69 us
    all_to_all x3, blocking collectives, swap_chunks(): return lax.all_to_all(parts, axes, 0, 0, tiled=True)  44 us
    ppermute x8, starting transfers between devices, shift(): lax.ppermute(block, axes, [(i, i + distance) for i in devices if i + dist...  26.4 us
    ppermute x8, waiting for transfers between devices, shift(): lax.ppermute(block, axes, [(i, i + distance) for i in devices if i + dist...  25.9 us
    ppermute x6, starting transfers between devices, other_core(): return lax.ppermute(block, 'core', [(0, 1), (1, 0)])  19.6 us
    all_gather x1, blocking collectives, gather_params(): every = lax.all_gather(packed, 'section', axis=0, tiled=False)  11.5 us
    unnamed x27, local copies, waits for them, and re-layouts  6.49 us
    concatenate x6, other arithmetic, twice(): jnp.concatenate([jnp.concatenate([weights, zero], axis=-1), jnp.concatena...  6.44 us
  transfers between devices with their start and end apart: 14, of which 4 were waited for; matrix products, arithmetic and copies ran while one was open for 10% of the time, Pallas kernels for 17%

commit v1 on v0

v1 whole, which is shorter than its diff:
```python
import jax
import jax.numpy as jnp
from jax import lax
from jax.experimental import pallas as pl
from jax.experimental.pallas import tpu as pltpu
from jax.sharding import Mesh
from jax.sharding import PartitionSpec as P

TILE_AXES = ("z", "y", "core")
SIDE = 16
REGION = 32
HALO = 8
RIM = 4
PIXELS = REGION * REGION
WIDTH = 64
CHANS = 256
TAPS = 9
BF = jnp.bfloat16
F32 = jnp.float32
VMEM_LIMIT = 56 * 1024 * 1024


def mm(left, right):
    return jnp.dot(left, right, preferred_element_type=F32)


def mm_first(left, right):
    return lax.dot_general(left, right, (((0,), (0,)), ((), ())), preferred_element_type=F32)


def silu_parts(value):
    sig = 0.5 + 0.5 * jnp.tanh(0.5 * value)
    out = value * sig
    return (out, sig + out * (1.0 - sig))


def around(tile, owner, near):
    north, south = (near[tile * 4], near[tile * 4 + 1])
    west, east = (near[tile * 4 + 2], near[tile * 4 + 3])

    def step(first, way, second, other):
        one = jnp.where(first >= 0, near[jnp.maximum(first, 0) * 4 + way], -1)
        two = jnp.where(second >= 0, near[jnp.maximum(second, 0) * 4 + other], -1)
        return jnp.where(one >= 0, one, two)

    ids = [
        step(north, 2, west, 0), north, step(north, 3, east, 0),
        west, tile, east,
        step(south, 2, west, 1), south, step(south, 3, east, 1),
    ]
    found = [item >= 0 for item in ids]
    rows = [owner[jnp.maximum(item, 0)] for item in ids]
    return (rows, found)


def pool_place(row, here):
    device, slot = (row >> 2, row & 3)
    gap = (device >> 1) - (here >> 1)
    side = jnp.where(gap < 0, 0, 1)
    near = jnp.where(gap == 0, 0, 4 + 4 * side) + slot
    place = jnp.where(jnp.abs(gap) <= 1, near, 12 + 4 * side + slot)
    place = place + jnp.where((device & 1) == (here & 1), 0, 20)
    return jnp.clip(place, 0, 39)


def bands_of(halo):
    return (
        (HALO - halo, halo, 0, SIDE - halo),
        (HALO, SIDE, 3, 0),
        (HALO + SIDE, halo, 6, 0),
    )


def build_region(pool, region, lane, places, found, halo):
    for top, rows, first, start in bands_of(halo):
        parts = []
        for k in range(3):
            part = pool[places[first + k], pl.ds(start, rows)].astype(F32)
            part = jnp.where(found[first + k], part, 0.0)
            cut = (slice(HALO, SIDE), slice(0, SIDE), slice(0, HALO))[k]
            parts.append(part[:, cut, :])
        band = jnp.concatenate(parts, axis=1).reshape(rows * REGION, CHANS).astype(BF)
        region[pl.ds(top * REGION, rows * REGION), pl.ds(lane * CHANS, CHANS)] = band


def build_present(present, found_pair):
    for top, rows, first, _ in bands_of(HALO):
        shape = (rows * REGION, 2 * WIDTH)
        col = lax.broadcasted_iota(jnp.int32, shape, 0) % REGION
        lane = lax.broadcasted_iota(jnp.int32, shape, 1)
        sides = []
        for found in found_pair:
            flags = [jnp.where(found[first + k], 1.0, 0.0) for k in range(3)]
            sides.append(
                jnp.where(col < HALO, flags[0], jnp.where(col < HALO + SIDE, flags[1], flags[2]))
            )
        present[pl.ds(top * REGION, rows * REGION), :] = jnp.where(lane < WIDTH, sides[0], sides[1])


def build_masks(masks):
    shape = (PIXELS, 2 * WIDTH)
    pixel = lax.broadcasted_iota(jnp.int32, shape, 0)
    row, col = (pixel // REGION, pixel % REGION)
    low, high = (HALO, HALO + SIDE)
    west = (col == low) | (col == high)
    east = (col == low - 1) | (col == high - 1)
    above = (row == low - 1) | (row == high - 1)
    below = (row == low) | (row == high)
    for k, (across, along) in enumerate(
        ((above, west), (above, east), (below, west), (below, east))
    ):
        masks[k] = jnp.where(across & along, 0.0, 1.0).astype(BF)


def store_shifted(shifted, masks, start, value):
    count = value.shape[0]
    rows = pl.ds(start, count)
    left = pltpu.roll(value, 1, 0).astype(BF)
    right = pltpu.roll(value, count - 1, 0).astype(BF)
    shifted[0, rows, :] = left
    shifted[1, rows, :] = value.astype(BF)
    shifted[2, rows, :] = right
    shifted[3, rows, :] = left * masks[0, rows, :]
    shifted[4, rows, :] = right * masks[1, rows, :]
    shifted[5, rows, :] = left * masks[2, rows, :]
    shifted[6, rows, :] = right * masks[3, rows, :]


TAP_SOURCES = ((3, -1), (1, -1), (4, -1), (0, 0), (1, 0), (2, 0), (5, 1), (1, 1), (6, 1))


def columns_at(shifted, start, count):
    return jnp.concatenate(
        [shifted[k, pl.ds(start + dy * REGION, count), :] for k, dy in TAP_SOURCES], axis=1
    )


def run_copies(copies):
    for copy in copies:
        copy.start()
    for copy in copies:
        copy.wait()


def pool_copies(sources, pools, sems):
    feats, cots = ([], [])

    def add(group, source, target):
        sem = sems.at[len(feats) + len(cots)]
        group.append(pltpu.make_async_copy(source, target, sem))

    for core in range(2):
        at = 20 * core
        for source in sources[core][:3]:
            add(feats, source.at[pl.ds(0, 4)], pools[0].at[pl.ds(at, 4)])
            add(cots, source.at[pl.ds(4, 4)], pools[1].at[pl.ds(at, 4)])
            at += 4
        for source in sources[core][3:]:
            for k in range(4):
                add(feats, source.at[pl.ds(k * SIDE, SIDE)], pools[0].at[at])
                for end in range(2):
                    add(
                        cots,
                        source.at[pl.ds(4 * (SIDE + end * RIM) + k * RIM, RIM)],
                        pools[1].at[at, pl.ds(end * (SIDE - RIM), RIM)],
                    )
                at += 1
    return (feats, cots)


COPIES = 2 * (3 * 2 + 8 * 3)


def inner_tile(region, lane):
    value = region[pl.ds(HALO * REGION, SIDE * REGION), pl.ds(lane * CHANS, CHANS)].astype(F32)
    value = value.reshape(SIDE, REGION, CHANS)[:, HALO : HALO + SIDE, :]
    return value.astype(BF)


INNER = (HALO * REGION, SIDE * REGION)


def fold_pair(value, rows, cols):
    return value[:rows, :cols] + value[rows:, cols:]


def whole_kernel(meta, owner, near, *refs):
    sources, refs = ((refs[:5], refs[5:10]), refs[10:])
    (w_red, w_tap, w_exp, v_red, v_tap, v_exp, norms, out, grad_in, grads,
     feats, cots, sems, region, present, masks, shifted, s_one, s_two, s_three,
     a_own, h_one, h_two, d_one, total) = refs
    pair = pl.program_id(0)
    here, section = (meta[0], meta[1])
    copies = pool_copies(sources, (feats, cots), sems)

    @pl.when(pair == 0)
    def _():
        for group in copies:
            for copy in group:
                copy.start()
        build_masks(masks)
        total[...] = jnp.zeros_like(total)
        for copy in copies[0]:
            copy.wait()

    founds, places = ([], [])
    for lane in range(2):
        rows, found = around(meta[2 + pair * 2 + lane], owner, near)
        place = [pool_place(row, here) for row in rows]
        build_region(feats, region, lane, place, found, HALO)
        founds.append(found)
        places.append(place)
    build_present(present, founds)

    def ahead(b, carry):
        mine = b == section

        @pl.when(mine)
        def _():
            a_own[...] = region[pl.ds(*INNER), :]

        def front(j, c):
            start = pl.multiple_of(j * 256, 256)
            rows = pl.ds(start, 256)
            pre = mm(region[rows, :], w_red[b]) * norms[b, 0:1, :128] + norms[b, 1:2, :128]
            hidden, slope = silu_parts(pre)
            there = present[rows, :]
            s_one[b, rows, :] = (slope * there * norms[b, 0:1, :128]).astype(BF)
            store_shifted(shifted, masks, start, hidden * there)
            return c

        lax.fori_loop(0, 4, front, 0)

        def tail(j, c):
            start = pl.multiple_of(REGION + j * 320, 32)
            rows = pl.ds(start, 320)
            pre = mm(columns_at(shifted, start, 320), w_tap[b])
            pre = pre * norms[b, 2:3, :128] + norms[b, 3:4, :128]
            hidden, slope = silu_parts(pre)
            s_two[b, rows, :] = (slope * norms[b, 2:3, :128]).astype(BF)
            hidden = hidden.astype(BF)

            @pl.when(mine)
            def _():
                h_two[rows, :] = hidden

            pre = (
                region[rows, :].astype(F32)
                + mm(hidden, w_exp[b]) * norms[b, 4:5, :]
                + norms[b, 5:6, :]
            )
            value, slope = silu_parts(pre)
            region[rows, :] = value.astype(BF)
            s_three[b, rows, :] = slope.astype(BF)
            return c

        lax.fori_loop(0, 3, tail, 0)

        @pl.when(mine)
        def _():
            h_one[...] = shifted[1]
            out[0] = inner_tile(region, 0)
            out[1] = inner_tile(region, 1)

        return carry

    lax.fori_loop(0, 4, ahead, 0)

    @pl.when(pair == 0)
    def _():
        for copy in copies[1]:
            copy.wait()

    for lane in range(2):
        build_region(cots, region, lane, places[lane], founds[lane], RIM)

    def keep_inner(value):
        col = lax.broadcasted_iota(jnp.int32, value.shape, 0) % REGION
        return jnp.where((col >= HALO) & (col < HALO + SIDE), value, 0.0).astype(BF)

    def back(step, carry):
        b = 3 - step
        mine = b == section

        def first(j, c):
            start = pl.multiple_of(4 * REGION + j * 256, 128)
            rows = pl.ds(start, 256)
            d_three = region[rows, :].astype(F32) * s_three[b, rows, :].astype(F32)
            e_three = (d_three * norms[b, 4:5, :]).astype(BF)
            d_two = mm(e_three, v_exp[b]) * s_two[b, rows, :].astype(F32)
            store_shifted(shifted, masks, start, d_two)
            return c

        lax.fori_loop(0, 3, first, 0)

        @pl.when(mine)
        def _():
            rows = pl.ds(*INNER)
            d_three = region[rows, :].astype(F32) * s_three[b, rows, :].astype(F32)
            e_three = keep_inner(d_three * norms[b, 4:5, :])
            total_e = fold_pair(mm_first(h_two[rows, :], e_three), WIDTH, CHANS)
            total[416:480, :] += total_e[:, :128]
            total[480:544, :] += total_e[:, 128:]
            d_two = keep_inner(shifted[1, rows, :].astype(F32))
            around_rows = pl.ds(INNER[0] - REGION, INNER[1] + 2 * REGION)
            hidden = h_one[around_rows, :].astype(F32)
            left = pltpu.roll(hidden, 1, 0).astype(BF)
            right = pltpu.roll(hidden, hidden.shape[0] - 1, 0).astype(BF)
            middle = hidden.astype(BF)
            gated = [
                (left * masks[0, around_rows, :], 0), (middle, 0), (right * masks[1, around_rows, :], 0),
                (left, 1), (middle, 1), (right, 1),
                (left * masks[2, around_rows, :], 2), (middle, 2), (right * masks[3, around_rows, :], 2),
            ]
            for tap, (value, dy) in enumerate(gated):
                column = value[dy * REGION : dy * REGION + INNER[1]]
                piece = fold_pair(mm_first(column, d_two), WIDTH, WIDTH)
                if tap < 4:
                    total[tap * 64 : tap * 64 + 64, :64] += piece
                elif tap > 4:
                    at = (tap - 5) * 64 + 32
                    total[at : at + 64, 64:] += piece
                else:
                    total[256:288, :64] += piece[:32]
                    total[0:32, 64:] += piece[32:]

        def second(j, c):
            start = pl.multiple_of(5 * REGION + j * 352, 32)
            rows = pl.ds(start, 352)
            d_hidden = mm(columns_at(shifted, start, 352), v_tap[b])
            d_first = (d_hidden * s_one[b, rows, :].astype(F32)).astype(BF)
            d_one[rows, :] = d_first
            d_three = region[rows, :].astype(F32) * s_three[b, rows, :].astype(F32)
            region[rows, :] = (d_three + mm(d_first, v_red[b])).astype(BF)
            return c

        lax.fori_loop(0, 2, second, 0)

        @pl.when(mine)
        def _():
            rows = pl.ds(*INNER)
            d_first = keep_inner(d_one[rows, :].astype(F32))
            piece = fold_pair(mm_first(a_own[...], d_first), CHANS, WIDTH)
            total[288:416, :64] += piece[:128]
            total[288:416, 64:] += piece[128:]
            grad_in[0] = inner_tile(region, 0)
            grad_in[1] = inner_tile(region, 1)

        return carry

    lax.fori_loop(0, 4, back, 0)

    @pl.when(pair == 1)
    def _():
        grads[...] = total[...].astype(BF)


def run_kernel(scalars, sources, weights):
    def whole(item):
        return pl.BlockSpec(item.shape, lambda i, *_, n=len(item.shape): (0,) * n)

    tiles = jax.ShapeDtypeStruct((4, SIDE, SIDE, CHANS), BF)
    grads = jax.ShapeDtypeStruct((640, 128), BF)
    pair = pl.BlockSpec((2, SIDE, SIDE, CHANS), lambda i, *_: (i, 0, 0, 0))
    narrow = (PIXELS, 2 * WIDTH)
    pool = pltpu.VMEM((40, SIDE, SIDE, CHANS), BF)
    wide = (PIXELS, 2 * CHANS)
    return pl.pallas_call(
        whole_kernel,
        grid_spec=pltpu.PrefetchScalarGridSpec(
            num_scalar_prefetch=len(scalars),
            grid=(2,),
            in_specs=[pl.BlockSpec(memory_space=pl.ANY)] * len(sources)
            + [whole(item) for item in weights],
            out_specs=[pair, pair, whole(grads)],
            scratch_shapes=[
                pool,
                pool,
                pltpu.SemaphoreType.DMA((COPIES,)),
                pltpu.VMEM(wide, BF),
                pltpu.VMEM(narrow, F32),
                pltpu.VMEM((4,) + narrow, BF),
                pltpu.VMEM((7,) + narrow, BF),
                pltpu.VMEM((4,) + narrow, BF),
                pltpu.VMEM((4,) + narrow, BF),
                pltpu.VMEM((4,) + wide, BF),
                pltpu.VMEM((INNER[1], 2 * CHANS), BF),
                pltpu.VMEM(narrow, BF),
                pltpu.VMEM(narrow, BF),
                pltpu.VMEM(narrow, BF),
                pltpu.VMEM((640, 128), F32),
            ],
        ),
        out_shape=[tiles, tiles, grads],
        compiler_params=pltpu.CompilerParams(
            dimension_semantics=("arbitrary",), vmem_limit_bytes=VMEM_LIMIT
        ),
    )(*scalars, *sources, *weights)


def shift(block, axes, distance):
    devices = range(lax.axis_size(axes))
    return lax.ppermute(block, axes, [(i, i + distance) for i in devices if i + distance in devices])


def other_core(block):
    return lax.ppermute(block, "core", [(0, 1), (1, 0)])


def trimmed(both):
    ends = (both[4:, :RIM], both[4:, SIDE - RIM :])
    return jnp.concatenate([item.reshape(-1, SIDE, CHANS) for item in (both[:4], *ends)])


def exchange(features, cotangent):
    both = jnp.concatenate([features, cotangent])
    column = [both]
    for distance in (2, -2):
        column.append(shift(both, TILE_AXES, distance))
    for k, distance in ((1, 2), (2, -2)):
        column.append(shift(trimmed(column[k]), TILE_AXES, distance))
    return column + [other_core(item) for item in column]


def swap_chunks(parts, axes):
    return lax.all_to_all(parts, axes, 0, 0, tiled=True)


def sum_over_tiles(values):
    plane = ("y", "core")
    across = lax.axis_size(plane)
    rows = values.shape[0] // across
    got = swap_chunks(values, plane).reshape(across, rows, 128)
    mine = jnp.sum(got.astype(F32), axis=0).astype(BF)
    got = swap_chunks(jnp.tile(mine, (lax.axis_size("z"), 1)), "z").reshape(-1, rows, 128)
    total = jnp.sum(got.astype(F32), axis=0).astype(BF)
    return swap_chunks(jnp.tile(total, (across, 1)), plane).astype(F32)


def split_float(value):
    high = value.astype(BF)
    low = (value - high.astype(F32)).astype(BF)
    return (high, low)


def gather_params(w_reduce, w_taps, w_expand, norm_scale, norm_shift):
    pieces = [w_reduce, w_taps, w_expand]
    for item in (norm_scale, norm_shift):
        pieces.extend(split_float(item))
    packed = jnp.concatenate([item.reshape(-1, 128) for item in pieces])
    every = lax.all_gather(packed, "section", axis=0, tiled=False)
    at = 0
    cut = []
    for item in pieces:
        rows = item.size // 128
        cut.append(every[:, at : at + rows].reshape((-1,) + item.shape[1:]))
        at += rows
    scale = cut[3].astype(F32) + cut[4].astype(F32)
    offset = cut[5].astype(F32) + cut[6].astype(F32)
    return (cut[0], cut[1], cut[2], scale, offset)


def twice(weights):
    zero = jnp.zeros_like(weights)
    return jnp.concatenate(
        [jnp.concatenate([weights, zero], axis=-1), jnp.concatenate([zero, weights], axis=-1)],
        axis=-2,
    )


def norm_rows(scale, offset):
    rows = []
    for low, high in ((0, 64), (64, 128), (128, 384)):
        for item in (scale, offset):
            part = jnp.concatenate([item[:, low:high]] * 2, axis=1)
            rows.append(jnp.pad(part, ((0, 0), (0, 512 - part.shape[1]))))
    rows.extend([jnp.zeros_like(rows[0])] * 2)
    return jnp.stack(rows, axis=1)


def on_device(
    features, out_cotangent, w_reduce, w_taps, w_expand, norm_scale, norm_shift, owner, neighbours
):
    here = lax.axis_index(TILE_AXES).astype(jnp.int32)
    section = lax.axis_index("section").astype(jnp.int32)
    slots = here * 4 + jnp.arange(4, dtype=jnp.int32)
    hit = owner[None, :] == slots[:, None]
    ids = jnp.sum(
        jnp.where(hit, jnp.arange(owner.shape[0], dtype=jnp.int32)[None, :], 0), axis=1
    )
    meta = jnp.concatenate([here[None], section[None], ids.astype(jnp.int32)])
    scalars = (meta, owner, neighbours.reshape(-1))

    sources = exchange(features, out_cotangent)
    w_red, w_tap, w_exp, scale, offset = gather_params(
        w_reduce, w_taps, w_expand, norm_scale, norm_shift
    )
    taps = w_tap.reshape(4, TAPS, WIDTH, WIDTH)
    weights = (
        twice(w_red),
        twice(taps).reshape(4, TAPS * 128, 128),
        twice(w_exp),
        twice(w_red.swapaxes(1, 2)),
        twice(taps[:, ::-1].swapaxes(2, 3)).reshape(4, TAPS * 128, 128),
        twice(w_exp.swapaxes(1, 2)),
        norm_rows(scale, offset),
    )
    out, grad_in, grads = run_kernel(scalars, sources, weights)
    total = sum_over_tiles(grads)
    g_taps = jnp.concatenate([total[:288, :64], total[:288, 64:]])
    g_reduce = jnp.concatenate([total[288:416, :64], total[288:416, 64:]])
    g_expand = jnp.concatenate([total[416:480], total[480:544]], axis=1)
    return (out[None], grad_in[None], g_reduce[None], g_taps[None], g_expand[None])


def fine_mesh(mesh):
    shape = (mesh.devices.shape[0], mesh.devices.shape[1] // 16, 8, 2)
    return Mesh(mesh.devices.reshape(shape), ("section",) + TILE_AXES)


def solution(mesh):
    tiles = P(TILE_AXES, None, None, None)
    owned = P("section", TILE_AXES, None, None, None)
    weights = P("section", None, None)
    return jax.shard_map(
        on_device,
        mesh=fine_mesh(mesh),
        in_specs=(
            tiles, tiles, weights, weights, weights, P("section", None), P("section", None), P(), P(),
        ),
        out_specs=(owned, owned, weights, weights, weights),
        check_vma=False,
    )
```

time: 233 us -> 184 us (0.79)
  waiting for transfers between devices: 27.7 us -> 10.5 us
  starting transfers between devices: 46 us -> 29.8 us
  Pallas kernels: 69 us -> 58.2 us
  other arithmetic: 14.5 us -> 10 us
  blocking collectives: 55.5 us -> 58.4 us
  local copies, waits for them, and re-layouts: 17.9 us -> 15.1 us
    ppermute x8 -> x4, waiting for transfers between devices: 25.9 us -> 10.4 us  [shift(): lax.ppermute(block, axes, [(i, i + distance) for i in devices if i + dist...]
    ppermute x8 -> x4, starting transfers between devices: 26.4 us -> 11.5 us  [shift(): lax.ppermute(block, axes, [(i, i + distance) for i in devices if i + dist...]
    pallas_call x2 -> x1, Pallas kernels: 69 us -> 58.2 us  [run_kernel(): pl.pallas_call(whole_kernel, grid_spec=pltpu.PrefetchScalarGridSpec(num_s...]
    all_to_all x3, blocking collectives: 44 us -> 48.4 us  [swap_chunks(): return lax.all_to_all(parts, axes, 0, 0, tiled=True)]
    another operation x8, local copies, waits for them, and re-layouts: 0.77 us -> 5.08 us  [norm_rows(): return jnp.stack(rows, axis=1)]
    concatenate x4 -> x1, local copies, waits for them, and re-layouts: 4.06 us -> 0.87 us  [exchange(): both = jnp.concatenate([features, cotangent])]
    unnamed x27 -> x36, local copies, waits for them, and re-layouts: 6.49 us -> 3.53 us
    broadcast_in_dim x2 -> x0, other arithmetic: 2.48 us -> none  [the longest x1 1.44 us: sum_over_tiles(): copies = jnp.broadcast_to(total.astype(BF)[None], (across,) + total.shape)]
  transfers between devices with their start and end apart: 14 -> 9, of which waited for: 4 -> 1; matrix products, arithmetic and copies ran while one was open for 10% -> 10% of each run, Pallas kernels for 17% -> 0%
where the time goes in v1:
time: 184 us; the launch traced here: 183 us
  blocking collectives  58.4 us (32%)
  Pallas kernels  58.2 us (32%)
  starting transfers between devices  29.8 us (16%)
  local copies, waits for them, and re-layouts  15.1 us (8%)
  waiting for transfers between devices  10.5 us (6%)
  other arithmetic  10 us (5%)
    pallas_call x1, Pallas kernels, run_kernel(): pl.pallas_call(whole_kernel, grid_spec=pltpu.PrefetchScalarGridSpec(num_s...  58.2 us
    all_to_all x3, blocking collectives, swap_chunks(): return lax.all_to_all(parts, axes, 0, 0, tiled=True)  48.4 us
    ppermute x5, starting transfers between devices, other_core(): return lax.ppermute(block, 'core', [(0, 1), (1, 0)])  18.3 us
    ppermute x4, starting transfers between devices, shift(): lax.ppermute(block, axes, [(i, i + distance) for i in devices if i + dist...  11.5 us
    ppermute x4, waiting for transfers between devices, shift(): lax.ppermute(block, axes, [(i, i + distance) for i in devices if i + dist...  10.4 us
    all_gather x1, blocking collectives, gather_params(): every = lax.all_gather(packed, 'section', axis=0, tiled=False)  9.98 us
    concatenate x4, other arithmetic, twice(): jnp.concatenate([jnp.concatenate([weights, zero], axis=-1), jnp.concatena...  5.12 us
    another operation x8, local copies, waits for them, and re-layouts, norm_rows(): return jnp.stack(rows, axis=1)  5.08 us
  transfers between devices with their start and end apart: 9, of which 1 were waited for; matrix products, arithmetic and copies ran while one was open for 10% of the time, Pallas kernels for 0%

profile of v1, /device:TPU:1, one launch (start us, length us, event | category | flops | bytes accessed | tf_op | source)
XLA Modules:
  0.0 183.2 jit_solution(16787626831485274727)
XLA Ops:
  0.7 2.0 %constant_dynamic-update-slice_fusion.1 = bf16[8,16,16,256]{3,2,1,0:T(8,128)(2,1)} fusion(bf16[4,16,16,256]{3,2,1,0:T(8,128)(2,1)} %param.9), kind=kLoop, calls=%fused_computation.44 | loop fusion | bytes 1048576
  3.5 8.8 %collective-permute-start.4 = (bf16[8,16,16,256]{3,2,1,0:T(8,128)(2,1)}, bf16[8,16,16,256]{3,2,1,0:T(8,128)(2,1)}, u32[]{:S(2)}, u32[]{:S(2)}) collective-permute-start(bf16[8,16,16,256]{3,2,1,0:T(8,128)(2,1)} %constant_dynamic-update-slice_fusion.refs_0_), channel_id=1, source_target_pairs={{0,1},{1,0},{2,3},{3,2},{4,5},{5,4},{6,7},{7,6},{8,9},{9,8},{10,11... | collective-permute-start | bytes 3145736 | tf_op jit(solution)/shard_map/ppermute | solution.py:407
  12.3 1.3 collective-permute-start.1
  13.6 4.1 %collective-permute-start = (bf16[8,16,16,256]{3,2,1,0:T(8,128)(2,1)}, bf16[8,16,16,256]{3,2,1,0:T(8,128)(2,1)S(1)}, u32[]{:S(2)}, u32[]{:S(2)}) collective-permute-start(bf16[8,16,16,256]{3,2,1,0:T(8,128)(2,1)} %constant_dynamic-update-slice_fusion.refs_0_), channel_id=1, source_target_pairs={{0,2},{1,3},{2,4},{3,5},{4,6},{5,7},{6,8},{7,9},{8,10},{9,11},{10,... | collective-permute-start | bytes 3145736 | tf_op jit(solution)/shard_map/ppermute | solution.py:403
  18.5 10.0 %all-gather.1 = bf16[4,556,128]{2,1,0:T(8,128)(2,1)S(1)} all-gather(bf16[1,556,128]{2,1,0:T(8,128)(2,1)S(1)} %bitcast.42), channel_id=2, replica_groups=mesh['section'=4,'z'=8,'y'=8,'core'=2] {'section'}, dimensions={0}, use_global_device_ids=true | all-gather | bytes 711680 | tf_op jit(solution)/shard_map/all_gather | solution.py:451
  28.8 10.4 %collective-permute-done.1.refs_2_ = bf16[8,16,16,256]{3,2,1,0:T(8,128)(2,1)S(1)} collective-permute-done((bf16[8,16,16,256]{3,2,1,0:T(8,128)(2,1)}, bf16[8,16,16,256]{3,2,1,0:T(8,128)(2,1)S(1)}, u32[]{:S(2)}, u32[]{:S(2)}) %collective-permute-start.1) | collective-permute-done | bytes 1048608 | tf_op jit(solution)/shard_map/ppermute | solution.py:403
  39.3 1.1 pad_maximum_fusion.1
  40.4 1.3 collective-permute-start.3
  41.8 1.1 pad_maximum_fusion
  42.9 4.9 %collective-permute-start.2 = (bf16[96,16,256]{2,1,0:T(8,128)(2,1)}, bf16[96,16,256]{2,1,0:T(8,128)(2,1)}, u32[]{:S(2)}, u32[]{:S(2)}) collective-permute-start(bf16[96,16,256]{2,1,0:T(8,128)(2,1)} %pad_maximum_fusion), channel_id=1, source_target_pairs={{0,2},{1,3},{2,4},{3,5},{4,6},{5,7},{6,8},{7,9},{8,10},{9,11},{10,... | collective-permute-start | bytes 2359304 | tf_op jit(solution)/shard_map/ppermute | solution.py:403
  47.9 3.3 %collective-permute-start.6 = (bf16[8,16,16,256]{3,2,1,0:T(8,128)(2,1)S(1)}, bf16[8,16,16,256]{3,2,1,0:T(8,128)(2,1)}, u32[]{:S(2)}, u32[]{:S(2)}) collective-permute-start(bf16[8,16,16,256]{3,2,1,0:T(8,128)(2,1)S(1)} %collective-permute-done.1.refs_2_), channel_id=1, source_target_pairs={{0,1},{1,0},{2,3},{3,2},{4,5},{5,4},{6,7},{7,6},{8,9},{9,8},{10,11... | collective-permute-start | bytes 3145736 | tf_op jit(solution)/shard_map/ppermute | solution.py:407
  51.2 1.9 %collective-permute-start.5 = (bf16[8,16,16,256]{3,2,1,0:T(8,128)(2,1)S(1)}, bf16[8,16,16,256]{3,2,1,0:T(8,128)(2,1)}, u32[]{:S(2)}, u32[]{:S(2)}) collective-permute-start(bf16[8,16,16,256]{3,2,1,0:T(8,128)(2,1)S(1)} %collective-permute-done.refs_1_), channel_id=1, source_target_pairs={{0,1},{1,0},{2,3},{3,2},{4,5},{5,4},{6,7},{7,6},{8,9},{9,8},{10,11... | collective-permute-start | bytes 3145736 | tf_op jit(solution)/shard_map/ppermute | solution.py:407
  60.2 1.5 stack.31.refs_16_
  61.7 0.9 select_reduce_fusion
  62.6 2.4 %collective-permute-start.8 = (bf16[96,16,256]{2,1,0:T(8,128)(2,1)}, bf16[96,16,256]{2,1,0:T(8,128)(2,1)S(1)}, u32[]{:S(2)}, u32[]{:S(2)}) collective-permute-start(bf16[96,16,256]{2,1,0:T(8,128)(2,1)} %collective-permute-done.3.refs_4_), channel_id=1, source_target_pairs={{0,1},{1,0},{2,3},{3,2},{4,5},{5,4},{6,7},{7,6},{8,9},{9,8},{10,11... | collective-permute-start | bytes 2359304 | tf_op jit(solution)/shard_map/ppermute | solution.py:407
  65.0 1.9 %collective-permute-start.7 = (bf16[96,16,256]{2,1,0:T(8,128)(2,1)}, bf16[96,16,256]{2,1,0:T(8,128)(2,1)S(1)}, u32[]{:S(2)}, u32[]{:S(2)}) collective-permute-start(bf16[96,16,256]{2,1,0:T(8,128)(2,1)} %collective-permute-done.2.refs_3_), channel_id=1, source_target_pairs={{0,1},{1,0},{2,3},{3,2},{4,5},{5,4},{6,7},{7,6},{8,9},{9,8},{10,11... | collective-permute-start | bytes 2359304 | tf_op jit(solution)/shard_map/ppermute | solution.py:407
  67.7 1.3 fusion.14
  69.0 1.1 fusion.16
  70.0 1.4 fusion.4
  71.4 1.4 fusion.5
  73.9 58.2 %shard_map.128 = (bf16[4,16,16,256]{3,2,1,0:T(8,128)(2,1)}, bf16[4,16,16,256]{3,2,1,0:T(8,128)(2,1)}, bf16[640,128]{1,0:T(8,128)(2,1)}) custom-call(s32[6]{0:T(128)} %pad_add_fusion.meta, s32[512]{0:T(512)} %owner.1, s32[2048]{0:T(1024)} %reshape.101.near, bf16[8,16,16,256]{3,2,1,0:T(8,128)(2,1)} %constant_dynamic-update-slice_fusion.refs_0_, ...), custom_call_target="tpu_custom_call" | custom-call | tf_op jit(solution)/shard_map/pallas_call | solution.py:368
  132.2 14.7 %all_to_all.21 = bf16[16,40,128]{2,1,0:T(8,128)(2,1)S(1)} all-to-all(bf16[16,40,128]{2,1,0:T(8,128)(2,1)} %bitcast.49), channel_id=1, replica_groups=mesh['section'=4,'z'=8,'y'=8,'core'=2] {'y','core'}, dimensions={0} | all-to-all | bytes 327680 | tf_op jit(solution)/shard_map/all_to_all | solution.py:426
  147.0 20.9 %all_to_all.22 = bf16[8,40,128]{2,1,0:T(8,128)(2,1)S(1)} all-to-all(bf16[8,40,128]{2,1,0:T(8,128)(2,1)S(1)} %tile.4), channel_id=1, replica_groups=mesh['section'=4,'z'=8,'y'=8,'core'=2] {'z'}, dimensions={0} | all-to-all | bytes 163840 | tf_op jit(solution)/shard_map/all_to_all | solution.py:426
  167.9 12.8 %all_to_all.23 = bf16[16,40,128]{2,1,0:T(8,128)(2,1)S(1)} all-to-all(bf16[16,40,128]{2,1,0:T(8,128)(2,1)S(1)} %tile.5), channel_id=1, replica_groups=mesh['section'=4,'z'=8,'y'=8,'core'=2] {'y','core'}, dimensions={0} | all-to-all | bytes 327680 | tf_op jit(solution)/shard_map/all_to_all | solution.py:426
  (99 shorter events, 13.5 us)
Async XLA Ops:
  0.6 2.0 %copy-start.9 = (bf16[4,16,16,256]{3,2,1,0:T(8,128)(2,1)S(1)}, bf16[4,16,16,256]{3,2,1,0:T(8,128)(2,1)}, u32[]{:S(2)}) copy-start(bf16[4,16,16,256]{3,2,1,0:T(8,128)(2,1)} %param.10) | copy-start | bytes 1572868
  0.6 17.0 %copy-start.14 = (f32[1,384]{1,0:T(1,128)S(1)}, f32[1,384]{1,0:T(1,128)}, u32[]{:S(2)}) copy-start(f32[1,384]{1,0:T(1,128)} %param.14) | copy-start | bytes 4612
  0.7 17.1 %copy-start.15 = (f32[1,384]{1,0:T(1,128)S(1)}, f32[1,384]{1,0:T(1,128)}, u32[]{:S(2)}) copy-start(f32[1,384]{1,0:T(1,128)} %param.15) | copy-start | bytes 4612
  0.7 17.1 %copy-start.12 = (bf16[1,64,256]{2,1,0:T(8,128)(2,1)S(1)}, bf16[1,64,256]{2,1,0:T(8,128)(2,1)}, u32[]{:S(2)}) copy-start(bf16[1,64,256]{2,1,0:T(8,128)(2,1)} %param.13) | copy-start | bytes 98308
  0.7 17.1 %copy-start.11 = (bf16[1,256,64]{1,2,0:T(8,128)(2,1)S(1)}, bf16[1,256,64]{1,2,0:T(8,128)(2,1)}, u32[]{:S(2)}) copy-start(bf16[1,256,64]{1,2,0:T(8,128)(2,1)} %param.11) | copy-start | bytes 98308
  0.7 17.3 %copy-start.10 = (bf16[1,576,64]{1,2,0:T(8,128)(2,1)S(1)}, bf16[1,576,64]{1,2,0:T(8,128)(2,1)}, u32[]{:S(2)}) copy-start(bf16[1,576,64]{1,2,0:T(8,128)(2,1)} %param.12) | copy-start | bytes 221188
  3.5 69.3 %collective-permute-start.4 = (bf16[8,16,16,256]{3,2,1,0:T(8,128)(2,1)}, bf16[8,16,16,256]{3,2,1,0:T(8,128)(2,1)}, u32[]{:S(2)}, u32[]{:S(2)}) collective-permute-start(bf16[8,16,16,256]{3,2,1,0:T(8,128)(2,1)} %constant_dynamic-update-slice_fusion.refs_0_), channel_id=1, source_target_pairs={{0,1},{1,0},{2,3},{3,2},{4,5},{5,4},{6,7},{7,6},{8,9},{9,8},{10,11... | collective-permute-start | bytes 3145736 | tf_op jit(solution)/shard_map/ppermute | solution.py:407
  12.3 26.9 %collective-permute-start.1 = (bf16[8,16,16,256]{3,2,1,0:T(8,128)(2,1)}, bf16[8,16,16,256]{3,2,1,0:T(8,128)(2,1)S(1)}, u32[]{:S(2)}, u32[]{:S(2)}) collective-permute-start(bf16[8,16,16,256]{3,2,1,0:T(8,128)(2,1)} %constant_dynamic-update-slice_fusion.refs_0_), channel_id=1, source_target_pairs={{2,0},{3,1},{4,2},{5,3},{6,4},{7,5},{8,6},{9,7},{10,8},{11,9},{12,... | collective-permute-start | bytes 3145736 | tf_op jit(solution)/shard_map/ppermute | solution.py:403
  13.6 28.1 %collective-permute-start = (bf16[8,16,16,256]{3,2,1,0:T(8,128)(2,1)}, bf16[8,16,16,256]{3,2,1,0:T(8,128)(2,1)S(1)}, u32[]{:S(2)}, u32[]{:S(2)}) collective-permute-start(bf16[8,16,16,256]{3,2,1,0:T(8,128)(2,1)} %constant_dynamic-update-slice_fusion.refs_0_), channel_id=1, source_target_pairs={{0,2},{1,3},{2,4},{3,5},{4,6},{5,7},{6,8},{7,9},{8,10},{9,11},{10,... | collective-permute-start | bytes 3145736 | tf_op jit(solution)/shard_map/ppermute | solution.py:403
  28.5 24.8 %copy-start.2 = (bf16[4,556,128]{2,1,0:T(8,128)(2,1)}, bf16[4,556,128]{2,1,0:T(8,128)(2,1)S(1)}, u32[]{:S(2)}) copy-start(bf16[4,556,128]{2,1,0:T(8,128)(2,1)S(1)} %all-gather.1) | copy-start | bytes 1708036
  39.2 8.7 %copy-start = (bf16[8,16,16,256]{3,2,1,0:T(8,128)(2,1)}, bf16[8,16,16,256]{3,2,1,0:T(8,128)(2,1)S(1)}, u32[]{:S(2)}) copy-start(bf16[8,16,16,256]{3,2,1,0:T(8,128)(2,1)S(1)} %collective-permute-done.1.refs_2_) | copy-start | bytes 3145732
  40.4 22.2 %collective-permute-start.3 = (bf16[96,16,256]{2,1,0:T(8,128)(2,1)}, bf16[96,16,256]{2,1,0:T(8,128)(2,1)}, u32[]{:S(2)}, u32[]{:S(2)}) collective-permute-start(bf16[96,16,256]{2,1,0:T(8,128)(2,1)} %pad_maximum_fusion.1), channel_id=1, source_target_pairs={{2,0},{3,1},{4,2},{5,3},{6,4},{7,5},{8,6},{9,7},{10,8},{11,9},{12,... | collective-permute-start | bytes 2359304 | tf_op jit(solution)/shard_map/ppermute | solution.py:403
  41.7 9.5 %copy-start.1 = (bf16[8,16,16,256]{3,2,1,0:T(8,128)(2,1)}, bf16[8,16,16,256]{3,2,1,0:T(8,128)(2,1)S(1)}, u32[]{:S(2)}) copy-start(bf16[8,16,16,256]{3,2,1,0:T(8,128)(2,1)S(1)} %collective-permute-done.refs_1_) | copy-start | bytes 3145732
  41.8 11.5 %copy-start.13 = (s32[512,4]{0,1:T(4,128)S(1)}, s32[512,4]{0,1:T(4,128)}, u32[]{:S(2)}) copy-start(s32[512,4]{0,1:T(4,128)} %param.17) | copy-start | bytes 24580
  42.9 22.1 %collective-permute-start.2 = (bf16[96,16,256]{2,1,0:T(8,128)(2,1)}, bf16[96,16,256]{2,1,0:T(8,128)(2,1)}, u32[]{:S(2)}, u32[]{:S(2)}) collective-permute-start(bf16[96,16,256]{2,1,0:T(8,128)(2,1)} %pad_maximum_fusion), channel_id=1, source_target_pairs={{0,2},{1,3},{2,4},{3,5},{4,6},{5,7},{6,8},{7,9},{8,10},{9,11},{10,... | collective-permute-start | bytes 2359304 | tf_op jit(solution)/shard_map/ppermute | solution.py:403
  47.9 24.9 %collective-permute-start.6 = (bf16[8,16,16,256]{3,2,1,0:T(8,128)(2,1)S(1)}, bf16[8,16,16,256]{3,2,1,0:T(8,128)(2,1)}, u32[]{:S(2)}, u32[]{:S(2)}) collective-permute-start(bf16[8,16,16,256]{3,2,1,0:T(8,128)(2,1)S(1)} %collective-permute-done.1.refs_2_), channel_id=1, source_target_pairs={{0,1},{1,0},{2,3},{3,2},{4,5},{5,4},{6,7},{7,6},{8,9},{9,8},{10,11... | collective-permute-start | bytes 3145736 | tf_op jit(solution)/shard_map/ppermute | solution.py:407
  51.2 21.6 %collective-permute-start.5 = (bf16[8,16,16,256]{3,2,1,0:T(8,128)(2,1)S(1)}, bf16[8,16,16,256]{3,2,1,0:T(8,128)(2,1)}, u32[]{:S(2)}, u32[]{:S(2)}) collective-permute-start(bf16[8,16,16,256]{3,2,1,0:T(8,128)(2,1)S(1)} %collective-permute-done.refs_1_), channel_id=1, source_target_pairs={{0,1},{1,0},{2,3},{3,2},{4,5},{5,4},{6,7},{7,6},{8,9},{9,8},{10,11... | collective-permute-start | bytes 3145736 | tf_op jit(solution)/shard_map/ppermute | solution.py:407
  53.2 6.4 %slice-start = ((bf16[4,556,128]{2,1,0:T(8,128)(2,1)}), bf16[4,288,128]{2,1,0:T(8,128)(2,1)S(1)}, s32[]{:S(2)}) async-start(bf16[4,556,128]{2,1,0:T(8,128)(2,1)} %copy-done.2), calls=%async_computation.3 | async-start | bytes 589824 | tf_op jit(solution)/shard_map/slice | solution.py:456
  57.8 1.8 copy-start.3
  61.7 6.0 %copy-start.5 = (bf16[4,64,256]{1,2,0:T(8,128)(2,1)S(1)}, bf16[4,64,256]{1,2,0:T(8,128)(2,1)}, u32[]{:S(2)}) copy-start(bf16[4,64,256]{1,2,0:T(8,128)(2,1)} %copy.49) | copy-start | bytes 393220
  62.6 10.2 %collective-permute-start.8 = (bf16[96,16,256]{2,1,0:T(8,128)(2,1)}, bf16[96,16,256]{2,1,0:T(8,128)(2,1)S(1)}, u32[]{:S(2)}, u32[]{:S(2)}) collective-permute-start(bf16[96,16,256]{2,1,0:T(8,128)(2,1)} %collective-permute-done.3.refs_4_), channel_id=1, source_target_pairs={{0,1},{1,0},{2,3},{3,2},{4,5},{5,4},{6,7},{7,6},{8,9},{9,8},{10,11... | collective-permute-start | bytes 2359304 | tf_op jit(solution)/shard_map/ppermute | solution.py:407
  65.0 7.8 %collective-permute-start.7 = (bf16[96,16,256]{2,1,0:T(8,128)(2,1)}, bf16[96,16,256]{2,1,0:T(8,128)(2,1)S(1)}, u32[]{:S(2)}, u32[]{:S(2)}) collective-permute-start(bf16[96,16,256]{2,1,0:T(8,128)(2,1)} %collective-permute-done.2.refs_3_), channel_id=1, source_target_pairs={{0,1},{1,0},{2,3},{3,2},{4,5},{5,4},{6,7},{7,6},{8,9},{9,8},{10,11... | collective-permute-start | bytes 2359304 | tf_op jit(solution)/shard_map/ppermute | solution.py:407
  67.6 1.4 copy-start.4
  67.6 1.4 copy-start.8
  (2 other events, 2.0 us)

commit v2 on v1

--- a/solution.py
+++ b/solution.py
@@ -14,7 +14,6 @@
 PIXELS = REGION * REGION
 WIDTH = 64
 CHANS = 256
-TAPS = 9
 BF = jnp.bfloat16
 F32 = jnp.float32
 VMEM_LIMIT = 56 * 1024 * 1024
@@ -112,34 +111,62 @@
         masks[k] = jnp.where(across & along, 0.0, 1.0).astype(BF)
 
 
-def store_shifted(shifted, masks, start, value):
+def low_lanes(rows):
+    return lax.broadcasted_iota(jnp.int32, (rows, 2 * WIDTH), 1) < WIDTH
+
+
+def build_gates(gates):
+    col = lax.broadcasted_iota(jnp.int32, (4 * REGION, 2 * WIDTH), 0) % REGION
+    west = (col == HALO) | (col == HALO + SIDE)
+    east = (col == HALO - 1) | (col == HALO + SIDE - 1)
+    left = jnp.where(west & low_lanes(4 * REGION), 0.0, 1.0).astype(BF)
+    gates[:, 0:128] = left
+    gates[:, 128:256] = left
+    gates[:, 256:384] = jnp.where(east, 0.0, 1.0).astype(BF)
+
+
+def store_shifted(stack, center, start, value):
     count = value.shape[0]
     rows = pl.ds(start, count)
-    left = pltpu.roll(value, 1, 0).astype(BF)
-    right = pltpu.roll(value, count - 1, 0).astype(BF)
-    shifted[0, rows, :] = left
-    shifted[1, rows, :] = value.astype(BF)
-    shifted[2, rows, :] = right
-    shifted[3, rows, :] = left * masks[0, rows, :]
-    shifted[4, rows, :] = right * masks[1, rows, :]
-    shifted[5, rows, :] = left * masks[2, rows, :]
-    shifted[6, rows, :] = right * masks[3, rows, :]
-
-
-TAP_SOURCES = ((3, -1), (1, -1), (4, -1), (0, 0), (1, 0), (2, 0), (5, 1), (1, 1), (6, 1))
-
-
-def columns_at(shifted, start, count):
-    return jnp.concatenate(
-        [shifted[k, pl.ds(start + dy * REGION, count), :] for k, dy in TAP_SOURCES], axis=1
-    )
-
-
-def run_copies(copies):
-    for copy in copies:
-        copy.start()
-    for copy in copies:
-        copy.wait()
+    low = low_lanes(count)
+    other = pltpu.roll(value, WIDTH, 1)
+    left = pltpu.roll(value, 1, 0)
+    other_left = pltpu.roll(other, 1, 0)
+    right = pltpu.roll(value, count - 1, 0)
+    stack[rows, 0:128] = jnp.where(low, left, other).astype(BF)
+    stack[rows, 128:256] = jnp.where(low, other_left, value).astype(BF)
+    stack[rows, 256:384] = right.astype(BF)
+    center[rows, :] = value.astype(BF)
+
+
+def row_products(first, second, third, weights):
+    one = mm(jnp.concatenate([first, third], axis=1), weights[0])
+    two = mm(jnp.concatenate([second, third], axis=1), weights[1])
+    low = low_lanes(first.shape[0])
+    above = jnp.where(low, one[:, :128], two[:, :128])
+    level = pltpu.roll(jnp.where(low, two[:, :128], one[:, :128]), WIDTH, 1)
+    return (above, level, one[:, 128:] + two[:, 128:])
+
+
+def convolve(stack, gates, products, start, count, weights):
+    rows = pl.ds(start, count)
+    parts = row_products(stack[rows, 0:128], stack[rows, 128:256], stack[rows, 256:384], weights)
+    for k in range(3):
+        products[k, rows, :] = parts[k]
+    upper, lower = ((HALO - 1) * REGION, (HALO + SIDE - 1) * REGION)
+    pair = 2 * REGION
+    edge = jnp.concatenate([stack[pl.ds(upper, pair), :], stack[pl.ds(lower, pair), :]])
+    edge = edge * gates[...]
+    above, _, below = row_products(edge[:, 0:128], edge[:, 128:256], edge[:, 256:384], weights)
+    for k, at in enumerate((upper, lower)):
+        products[0, pl.ds(at, REGION), :] = above[k * pair : k * pair + REGION]
+        products[2, pl.ds(at + REGION, REGION), :] = below[k * pair + REGION : (k + 1) * pair]
+    inner = pl.ds(start + REGION, count - pair)
+    return (
+        products[0, pl.ds(start, count - pair), :]
+        + products[1, inner, :]
+        + products[2, pl.ds(start + pair, count - pair), :]
+    )
 
 
 def pool_copies(sources, pools, sems):
@@ -187,7 +214,7 @@
 def whole_kernel(meta, owner, near, *refs):
     sources, refs = ((refs[:5], refs[5:10]), refs[10:])
     (w_red, w_tap, w_exp, v_red, v_tap, v_exp, norms, out, grad_in, grads,
-     feats, cots, sems, region, present, masks, shifted, s_one, s_two, s_three,
+     feats, cots, sems, region, present, masks, gates, stack, center, products, s_one, s_two, s_three,
      a_own, h_one, h_two, d_one, total) = refs
     pair = pl.program_id(0)
     here, section = (meta[0], meta[1])
@@ -199,6 +226,7 @@
             for copy in group:
                 copy.start()
         build_masks(masks)
+        build_gates(gates)
         total[...] = jnp.zeros_like(total)
         for copy in copies[0]:
             copy.wait()
@@ -219,22 +247,21 @@
         def _():
             a_own[...] = region[pl.ds(*INNER), :]
 
-        def front(j, c):
-            start = pl.multiple_of(j * 256, 256)
-            rows = pl.ds(start, 256)
+        def front():
+            start, count = (0, PIXELS)
+            rows = pl.ds(start, count)
             pre = mm(region[rows, :], w_red[b]) * norms[b, 0:1, :128] + norms[b, 1:2, :128]
             hidden, slope = silu_parts(pre)
             there = present[rows, :]
             s_one[b, rows, :] = (slope * there * norms[b, 0:1, :128]).astype(BF)
-            store_shifted(shifted, masks, start, hidden * there)
-            return c
-
-        lax.fori_loop(0, 4, front, 0)
-
-        def tail(j, c):
-            start = pl.multiple_of(REGION + j * 320, 32)
-            rows = pl.ds(start, 320)
-            pre = mm(columns_at(shifted, start, 320), w_tap[b])
+            store_shifted(stack, center, start, hidden * there)
+
+        front()
+
+        def tail():
+            start, count = (REGION, PIXELS - 2 * REGION)
+            rows = pl.ds(start, count)
+            pre = convolve(stack, gates, products, 0, PIXELS, w_tap[b])
             pre = pre * norms[b, 2:3, :128] + norms[b, 3:4, :128]
             hidden, slope = silu_parts(pre)
             s_two[b, rows, :] = (slope * norms[b, 2:3, :128]).astype(BF)
@@ -252,13 +279,12 @@
             value, slope = silu_parts(pre)
             region[rows, :] = value.astype(BF)
             s_three[b, rows, :] = slope.astype(BF)
-            return c
-
-        lax.fori_loop(0, 3, tail, 0)
+
+        tail()
 
         @pl.when(mine)
         def _():
-            h_one[...] = shifted[1]
+            h_one[...] = center[...]
             out[0] = inner_tile(region, 0)
             out[1] = inner_tile(region, 1)
 
@@ -282,16 +308,15 @@
         b = 3 - step
         mine = b == section
 
-        def first(j, c):
-            start = pl.multiple_of(4 * REGION + j * 256, 128)
-            rows = pl.ds(start, 256)
+        def first():
+            start, count = (4 * REGION, PIXELS - 8 * REGION)
+            rows = pl.ds(start, count)
             d_three = region[rows, :].astype(F32) * s_three[b, rows, :].astype(F32)
             e_three = (d_three * norms[b, 4:5, :]).astype(BF)
             d_two = mm(e_three, v_exp[b]) * s_two[b, rows, :].astype(F32)
-            store_shifted(shifted, masks, start, d_two)
-            return c
-
-        lax.fori_loop(0, 3, first, 0)
+            store_shifted(stack, center, start, d_two)
+
+        first()
 
         @pl.when(mine)
         def _():
@@ -301,7 +326,7 @@
             total_e = fold_pair(mm_first(h_two[rows, :], e_three), WIDTH, CHANS)
             total[416:480, :] += total_e[:, :128]
             total[480:544, :] += total_e[:, 128:]
-            d_two = keep_inner(shifted[1, rows, :].astype(F32))
+            d_two = keep_inner(center[rows, :].astype(F32))
             around_rows = pl.ds(INNER[0] - REGION, INNER[1] + 2 * REGION)
             hidden = h_one[around_rows, :].astype(F32)
             left = pltpu.roll(hidden, 1, 0).astype(BF)
@@ -324,17 +349,18 @@
                     total[256:288, :64] += piece[:32]
                     total[0:32, 64:] += piece[32:]
 
-        def second(j, c):
-            start = pl.multiple_of(5 * REGION + j * 352, 32)
-            rows = pl.ds(start, 352)
-            d_hidden = mm(columns_at(shifted, start, 352), v_tap[b])
+        def second():
+            start, count = (5 * REGION, PIXELS - 10 * REGION)
+            rows = pl.ds(start, count)
+            d_hidden = convolve(
+                stack, gates, products, 4 * REGION, PIXELS - 8 * REGION, v_tap[b]
+            )
             d_first = (d_hidden * s_one[b, rows, :].astype(F32)).astype(BF)
             d_one[rows, :] = d_first
             d_three = region[rows, :].astype(F32) * s_three[b, rows, :].astype(F32)
             region[rows, :] = (d_three + mm(d_first, v_red[b])).astype(BF)
-            return c
-
-        lax.fori_loop(0, 2, second, 0)
+
+        second()
 
         @pl.when(mine)
         def _():
@@ -380,7 +406,10 @@
                 pltpu.VMEM(wide, BF),
                 pltpu.VMEM(narrow, F32),
                 pltpu.VMEM((4,) + narrow, BF),
-                pltpu.VMEM((7,) + narrow, BF),
+                pltpu.VMEM((4 * REGION, 6 * WIDTH), BF),
+                pltpu.VMEM((PIXELS, 6 * WIDTH), BF),
+                pltpu.VMEM(narrow, BF),
+                pltpu.VMEM((3,) + narrow, F32),
                 pltpu.VMEM((4,) + narrow, BF),
                 pltpu.VMEM((4,) + narrow, BF),
                 pltpu.VMEM((4,) + wide, BF),
@@ -468,6 +497,19 @@
     )
 
 
+def tap_pair(taps):
+    blank = jnp.zeros_like(taps[:, 0, 0])
+
+    def grid(rows, cols):
+        lines = []
+        for dx in rows:
+            line = [blank if None in (dx, dy) else taps[:, dy, dx] for dy in cols]
+            lines.append(jnp.concatenate(line, axis=2))
+        return jnp.concatenate(lines, axis=1)
+
+    return jnp.stack([grid((0, 1, 2, None), (0, 1, 2, None)), grid((0, 1, None, 2), (1, 0, None, 2))], axis=1)
+
+
 def norm_rows(scale, offset):
     rows = []
     for low, high in ((0, 64), (64, 128), (128, 384)):
@@ -495,13 +537,14 @@
     w_red, w_tap, w_exp, scale, offset = gather_params(
         w_reduce, w_taps, w_expand, norm_scale, norm_shift
     )
-    taps = w_tap.reshape(4, TAPS, WIDTH, WIDTH)
+    taps = w_tap.reshape(4, 3, 3, WIDTH, WIDTH)
+    turned = taps[:, ::-1, ::-1].swapaxes(3, 4)
     weights = (
         twice(w_red),
-        twice(taps).reshape(4, TAPS * 128, 128),
+        tap_pair(taps),
         twice(w_exp),
         twice(w_red.swapaxes(1, 2)),
-        twice(taps[:, ::-1].swapaxes(2, 3)).reshape(4, TAPS * 128, 128),
+        tap_pair(turned),
         twice(w_exp.swapaxes(1, 2)),
         norm_rows(scale, offset),
     )

time: 184 us -> 164 us (0.89)
  Pallas kernels: 58.2 us -> 41.2 us
  waiting for transfers between devices: 10.5 us -> 4.14 us
  local copies, waits for them, and re-layouts: 15.1 us -> 18.1 us
    pallas_call x1, Pallas kernels: 58.2 us -> 41.2 us  [run_kernel(): pl.pallas_call(whole_kernel, grid_spec=pltpu.PrefetchScalarGridSpec(num_s...]
    ppermute x4, waiting for transfers between devices: 10.4 us -> 4.05 us  [shift(): lax.ppermute(block, axes, [(i, i + distance) for i in devices if i + dist...]
    another operation x0 -> x6, other arithmetic: none -> 5.01 us  [tap_pair(): jnp.stack([grid((0, 1, 2, None), (0, 1, 2, None)), grid((0, 1, None, 2),...]
    unnamed x36 -> x38, local copies, waits for them, and re-layouts: 3.53 us -> 7.95 us
    another operation x8, local copies, waits for them, and re-layouts: 5.08 us -> 0.76 us  [norm_rows(): return jnp.stack(rows, axis=1)]
    concatenate x4 -> x2, other arithmetic: 5.12 us -> 2.39 us  [twice(): jnp.concatenate([jnp.concatenate([weights, zero], axis=-1), jnp.concatena...]
    another operation x2 -> x5, local copies, waits for them, and re-layouts: 0.57 us -> 2.6 us  [the longest x2 1.53 us: on_device(): taps = w_tap.reshape(4, 3, 3, WIDTH, WIDTH)]
  transfers between devices with their start and end apart: 9 -> 9, of which waited for: 1 -> 2; matrix products, arithmetic and copies ran while one was open for 10% -> 12% of each run, Pallas kernels for 0% -> 0%
where the time goes in v2:
time: 164 us; the launch traced here: 163 us
  blocking collectives  57.3 us (35%)
  Pallas kernels  41.2 us (25%)
  starting transfers between devices  29.9 us (18%)
  local copies, waits for them, and re-layouts  18.1 us (11%)
  other arithmetic  11.7 us (7%)
  waiting for transfers between devices  4.14 us (3%)
    all_to_all x3, blocking collectives, swap_chunks(): return lax.all_to_all(parts, axes, 0, 0, tiled=True)  47.3 us
    pallas_call x1, Pallas kernels, run_kernel(): pl.pallas_call(whole_kernel, grid_spec=pltpu.PrefetchScalarGridSpec(num_s...  41.2 us
    ppermute x5, starting transfers between devices, other_core(): return lax.ppermute(block, 'core', [(0, 1), (1, 0)])  18.4 us
    ppermute x4, starting transfers between devices, shift(): lax.ppermute(block, axes, [(i, i + distance) for i in devices if i + dist...  11.5 us
    all_gather x1, blocking collectives, gather_params(): every = lax.all_gather(packed, 'section', axis=0, tiled=False)  9.98 us
    unnamed x38, local copies, waits for them, and re-layouts  7.95 us
    another operation x6, other arithmetic, tap_pair(): jnp.stack([grid((0, 1, 2, None), (0, 1, 2, None)), grid((0, 1, None, 2),...  5.01 us
    ppermute x4, waiting for transfers between devices, shift(): lax.ppermute(block, axes, [(i, i + distance) for i in devices if i + dist...  4.05 us
  transfers between devices with their start and end apart: 9, of which 2 were waited for; matrix products, arithmetic and copies ran while one was open for 12% of the time, Pallas kernels for 0%

profile of v2, /device:TPU:1, one launch (start us, length us, event | category | flops | bytes accessed | tf_op | source)
XLA Modules:
  0.0 163.4 jit_solution(16531277686224683597)
XLA Ops:
  0.6 1.9 %constant_dynamic-update-slice_fusion.1 = bf16[8,16,16,256]{3,2,1,0:T(8,128)(2,1)} fusion(bf16[4,16,16,256]{3,2,1,0:T(8,128)(2,1)} %param.9), kind=kLoop, calls=%fused_computation.90 | loop fusion | bytes 1048576
  3.4 8.9 %collective-permute-start.4 = (bf16[8,16,16,256]{3,2,1,0:T(8,128)(2,1)}, bf16[8,16,16,256]{3,2,1,0:T(8,128)(2,1)}, u32[]{:S(2)}, u32[]{:S(2)}) collective-permute-start(bf16[8,16,16,256]{3,2,1,0:T(8,128)(2,1)} %constant_dynamic-update-slice_fusion.refs_0_), channel_id=1, source_target_pairs={{0,1},{1,0},{2,3},{3,2},{4,5},{5,4},{6,7},{7,6},{8,9},{9,8},{10,11... | collective-permute-start | bytes 3145736 | tf_op jit(solution)/shard_map/ppermute | solution.py:436
  12.4 1.3 collective-permute-start.1
  13.7 4.1 %collective-permute-start = (bf16[8,16,16,256]{3,2,1,0:T(8,128)(2,1)}, bf16[8,16,16,256]{3,2,1,0:T(8,128)(2,1)S(1)}, u32[]{:S(2)}, u32[]{:S(2)}) collective-permute-start(bf16[8,16,16,256]{3,2,1,0:T(8,128)(2,1)} %constant_dynamic-update-slice_fusion.refs_0_), channel_id=1, source_target_pairs={{0,2},{1,3},{2,4},{3,5},{4,6},{5,7},{6,8},{7,9},{8,10},{9,11},{10,... | collective-permute-start | bytes 3145736 | tf_op jit(solution)/shard_map/ppermute | solution.py:432
  19.9 10.0 %all-gather.1 = bf16[4,556,128]{2,1,0:T(8,128)(2,1)S(1)} all-gather(bf16[1,556,128]{2,1,0:T(8,128)(2,1)S(1)} %bitcast.102), channel_id=2, replica_groups=mesh['section'=4,'z'=8,'y'=8,'core'=2] {'section'}, dimensions={0}, use_global_device_ids=true | all-gather | bytes 711680 | tf_op jit(solution)/shard_map/all_gather | solution.py:480
  30.9 1.2 reshape_reshape.3
  32.4 1.1 fusion.27
  35.2 4.0 %collective-permute-done.1.refs_2_ = bf16[8,16,16,256]{3,2,1,0:T(8,128)(2,1)S(1)} collective-permute-done((bf16[8,16,16,256]{3,2,1,0:T(8,128)(2,1)}, bf16[8,16,16,256]{3,2,1,0:T(8,128)(2,1)S(1)}, u32[]{:S(2)}, u32[]{:S(2)}) %collective-permute-start.1) | collective-permute-done | bytes 1048608 | tf_op jit(solution)/shard_map/ppermute | solution.py:432
  39.3 1.2 pad_maximum_fusion.3
  40.5 1.3 collective-permute-start.3
  41.8 1.2 pad_maximum_fusion.2
  43.0 4.9 %collective-permute-start.2 = (bf16[96,16,256]{2,1,0:T(8,128)(2,1)}, bf16[96,16,256]{2,1,0:T(8,128)(2,1)}, u32[]{:S(2)}, u32[]{:S(2)}) collective-permute-start(bf16[96,16,256]{2,1,0:T(8,128)(2,1)} %pad_maximum_fusion.2), channel_id=1, source_target_pairs={{0,2},{1,3},{2,4},{3,5},{4,6},{5,7},{6,8},{7,9},{8,10},{9,11},{10,... | collective-permute-start | bytes 2359304 | tf_op jit(solution)/shard_map/ppermute | solution.py:432
  52.0 1.3 pad_maximum_fusion
  56.1 1.3 fusion.22
  57.3 3.3 %collective-permute-start.6 = (bf16[8,16,16,256]{3,2,1,0:T(8,128)(2,1)S(1)}, bf16[8,16,16,256]{3,2,1,0:T(8,128)(2,1)S(1)}, u32[]{:S(2)}, u32[]{:S(2)}) collective-permute-start(bf16[8,16,16,256]{3,2,1,0:T(8,128)(2,1)S(1)} %collective-permute-done.1.refs_2_), channel_id=1, source_target_pairs={{0,1},{1,0},{2,3},{3,2},{4,5},{5,4},{6,7},{7,6},{8,9},{9,8},{10,11... | collective-permute-start | bytes 3145736 | tf_op jit(solution)/shard_map/ppermute | solution.py:436
  60.6 1.9 %collective-permute-start.5 = (bf16[8,16,16,256]{3,2,1,0:T(8,128)(2,1)S(1)}, bf16[8,16,16,256]{3,2,1,0:T(8,128)(2,1)S(1)}, u32[]{:S(2)}, u32[]{:S(2)}) collective-permute-start(bf16[8,16,16,256]{3,2,1,0:T(8,128)(2,1)S(1)} %collective-permute-done.refs_1_), channel_id=1, source_target_pairs={{0,1},{1,0},{2,3},{3,2},{4,5},{5,4},{6,7},{7,6},{8,9},{9,8},{10,11... | collective-permute-start | bytes 3145736 | tf_op jit(solution)/shard_map/ppermute | solution.py:436
  62.7 1.1 fusion.24
  63.8 2.4 %collective-permute-start.8 = (bf16[96,16,256]{2,1,0:T(8,128)(2,1)}, bf16[96,16,256]{2,1,0:T(8,128)(2,1)S(1)}, u32[]{:S(2)}, u32[]{:S(2)}) collective-permute-start(bf16[96,16,256]{2,1,0:T(8,128)(2,1)} %collective-permute-done.3.refs_4_), channel_id=1, source_target_pairs={{0,1},{1,0},{2,3},{3,2},{4,5},{5,4},{6,7},{7,6},{8,9},{9,8},{10,11... | collective-permute-start | bytes 2359304 | tf_op jit(solution)/shard_map/ppermute | solution.py:436
  66.3 1.9 %collective-permute-start.7 = (bf16[96,16,256]{2,1,0:T(8,128)(2,1)}, bf16[96,16,256]{2,1,0:T(8,128)(2,1)S(1)}, u32[]{:S(2)}, u32[]{:S(2)}) collective-permute-start(bf16[96,16,256]{2,1,0:T(8,128)(2,1)} %collective-permute-done.2.refs_3_), channel_id=1, source_target_pairs={{0,1},{1,0},{2,3},{3,2},{4,5},{5,4},{6,7},{7,6},{8,9},{9,8},{10,11... | collective-permute-start | bytes 2359304 | tf_op jit(solution)/shard_map/ppermute | solution.py:436
  69.5 1.1 pad_maximum_fusion.1.refs_14_
  72.4 41.2 %shard_map.128 = (bf16[4,16,16,256]{3,2,1,0:T(8,128)(2,1)}, bf16[4,16,16,256]{3,2,1,0:T(8,128)(2,1)}, bf16[640,128]{1,0:T(8,128)(2,1)}) custom-call(s32[6]{0:T(128)} %pad_add_fusion.meta, s32[512]{0:T(512)} %owner.1, s32[2048]{0:T(1024)} %reshape.95.near, bf16[8,16,16,256]{3,2,1,0:T(8,128)(2,1)} %constant_dynamic-update-slice_fusion.refs_0_, ...), custom_call_target="tpu_custom_call" | custom-call | tf_op jit(solution)/shard_map/pallas_call | solution.py:394
  113.5 13.6 %all_to_all.21 = bf16[16,40,128]{2,1,0:T(8,128)(2,1)S(1)} all-to-all(bf16[16,40,128]{2,1,0:T(8,128)(2,1)} %bitcast.109), channel_id=1, replica_groups=mesh['section'=4,'z'=8,'y'=8,'core'=2] {'y','core'}, dimensions={0} | all-to-all | bytes 327680 | tf_op jit(solution)/shard_map/all_to_all | solution.py:455
  127.2 20.6 %all_to_all.22 = bf16[8,40,128]{2,1,0:T(8,128)(2,1)S(1)} all-to-all(bf16[8,40,128]{2,1,0:T(8,128)(2,1)S(1)} %tile.4), channel_id=1, replica_groups=mesh['section'=4,'z'=8,'y'=8,'core'=2] {'z'}, dimensions={0} | all-to-all | bytes 163840 | tf_op jit(solution)/shard_map/all_to_all | solution.py:455
  147.8 13.1 %all_to_all.23 = bf16[16,40,128]{2,1,0:T(8,128)(2,1)S(1)} all-to-all(bf16[16,40,128]{2,1,0:T(8,128)(2,1)S(1)} %tile.5), channel_id=1, replica_groups=mesh['section'=4,'z'=8,'y'=8,'core'=2] {'y','core'}, dimensions={0} | all-to-all | bytes 327680 | tf_op jit(solution)/shard_map/all_to_all | solution.py:455
  (109 shorter events, 18.6 us)
Async XLA Ops:
  0.6 1.9 %copy-start.7 = (bf16[4,16,16,256]{3,2,1,0:T(8,128)(2,1)S(1)}, bf16[4,16,16,256]{3,2,1,0:T(8,128)(2,1)}, u32[]{:S(2)}) copy-start(bf16[4,16,16,256]{3,2,1,0:T(8,128)(2,1)} %param.10) | copy-start | bytes 1572868
  2.6 15.2 %copy-start.15 = (f32[1,384]{1,0:T(1,128)S(1)}, f32[1,384]{1,0:T(1,128)}, u32[]{:S(2)}) copy-start(f32[1,384]{1,0:T(1,128)} %param.14) | copy-start | bytes 4612
  2.6 15.2 %copy-start.12 = (bf16[1,64,256]{2,1,0:T(8,128)(2,1)S(1)}, bf16[1,64,256]{2,1,0:T(8,128)(2,1)}, u32[]{:S(2)}) copy-start(bf16[1,64,256]{2,1,0:T(8,128)(2,1)} %param.13) | copy-start | bytes 98308
  3.4 14.3 %copy-start.16 = (f32[1,384]{1,0:T(1,128)S(1)}, f32[1,384]{1,0:T(1,128)}, u32[]{:S(2)}) copy-start(f32[1,384]{1,0:T(1,128)} %param.15) | copy-start | bytes 4612
  3.4 67.1 %collective-permute-start.4 = (bf16[8,16,16,256]{3,2,1,0:T(8,128)(2,1)}, bf16[8,16,16,256]{3,2,1,0:T(8,128)(2,1)}, u32[]{:S(2)}, u32[]{:S(2)}) collective-permute-start(bf16[8,16,16,256]{3,2,1,0:T(8,128)(2,1)} %constant_dynamic-update-slice_fusion.refs_0_), channel_id=1, source_target_pairs={{0,1},{1,0},{2,3},{3,2},{4,5},{5,4},{6,7},{7,6},{8,9},{9,8},{10,11... | collective-permute-start | bytes 3145736 | tf_op jit(solution)/shard_map/ppermute | solution.py:436
  12.4 26.9 %collective-permute-start.1 = (bf16[8,16,16,256]{3,2,1,0:T(8,128)(2,1)}, bf16[8,16,16,256]{3,2,1,0:T(8,128)(2,1)S(1)}, u32[]{:S(2)}, u32[]{:S(2)}) collective-permute-start(bf16[8,16,16,256]{3,2,1,0:T(8,128)(2,1)} %constant_dynamic-update-slice_fusion.refs_0_), channel_id=1, source_target_pairs={{2,0},{3,1},{4,2},{5,3},{6,4},{7,5},{8,6},{9,7},{10,8},{11,9},{12,... | collective-permute-start | bytes 3145736 | tf_op jit(solution)/shard_map/ppermute | solution.py:432
  13.7 28.1 %collective-permute-start = (bf16[8,16,16,256]{3,2,1,0:T(8,128)(2,1)}, bf16[8,16,16,256]{3,2,1,0:T(8,128)(2,1)S(1)}, u32[]{:S(2)}, u32[]{:S(2)}) collective-permute-start(bf16[8,16,16,256]{3,2,1,0:T(8,128)(2,1)} %constant_dynamic-update-slice_fusion.refs_0_), channel_id=1, source_target_pairs={{0,2},{1,3},{2,4},{3,5},{4,6},{5,7},{6,8},{7,9},{8,10},{9,11},{10,... | collective-permute-start | bytes 3145736 | tf_op jit(solution)/shard_map/ppermute | solution.py:432
  18.6 0.9 copy-start.10
  39.2 18.1 %copy-start = (bf16[8,16,16,256]{3,2,1,0:T(8,128)(2,1)}, bf16[8,16,16,256]{3,2,1,0:T(8,128)(2,1)S(1)}, u32[]{:S(2)}) copy-start(bf16[8,16,16,256]{3,2,1,0:T(8,128)(2,1)S(1)} %collective-permute-done.1.refs_2_) | copy-start | bytes 3145732
  40.5 23.4 %collective-permute-start.3 = (bf16[96,16,256]{2,1,0:T(8,128)(2,1)}, bf16[96,16,256]{2,1,0:T(8,128)(2,1)}, u32[]{:S(2)}, u32[]{:S(2)}) collective-permute-start(bf16[96,16,256]{2,1,0:T(8,128)(2,1)} %pad_maximum_fusion.3), channel_id=1, source_target_pairs={{2,0},{3,1},{4,2},{5,3},{6,4},{7,5},{8,6},{9,7},{10,8},{11,9},{12,... | collective-permute-start | bytes 2359304 | tf_op jit(solution)/shard_map/ppermute | solution.py:432
  41.8 18.8 %copy-start.1 = (bf16[8,16,16,256]{3,2,1,0:T(8,128)(2,1)}, bf16[8,16,16,256]{3,2,1,0:T(8,128)(2,1)S(1)}, u32[]{:S(2)}) copy-start(bf16[8,16,16,256]{3,2,1,0:T(8,128)(2,1)S(1)} %collective-permute-done.refs_1_) | copy-start | bytes 3145732
  43.0 23.2 %collective-permute-start.2 = (bf16[96,16,256]{2,1,0:T(8,128)(2,1)}, bf16[96,16,256]{2,1,0:T(8,128)(2,1)}, u32[]{:S(2)}, u32[]{:S(2)}) collective-permute-start(bf16[96,16,256]{2,1,0:T(8,128)(2,1)} %pad_maximum_fusion.2), channel_id=1, source_target_pairs={{0,2},{1,3},{2,4},{3,5},{4,6},{5,7},{6,8},{7,9},{8,10},{9,11},{10,... | collective-permute-start | bytes 2359304 | tf_op jit(solution)/shard_map/ppermute | solution.py:432
  49.1 0.9 copy-start.9
  50.0 0.9 copy-start.8
  55.1 0.9 copy-start.4
  56.1 6.5 %copy-start.13 = (s32[512]{0:T(512)S(1)}, s32[512]{0:T(512)}, u32[]{:S(2)}) copy-start(s32[512]{0:T(512)} %owner.1) | copy-start | bytes 6148
  57.3 13.2 %collective-permute-start.6 = (bf16[8,16,16,256]{3,2,1,0:T(8,128)(2,1)S(1)}, bf16[8,16,16,256]{3,2,1,0:T(8,128)(2,1)S(1)}, u32[]{:S(2)}, u32[]{:S(2)}) collective-permute-start(bf16[8,16,16,256]{3,2,1,0:T(8,128)(2,1)S(1)} %collective-permute-done.1.refs_2_), channel_id=1, source_target_pairs={{0,1},{1,0},{2,3},{3,2},{4,5},{5,4},{6,7},{7,6},{8,9},{9,8},{10,11... | collective-permute-start | bytes 3145736 | tf_op jit(solution)/shard_map/ppermute | solution.py:436
  60.6 9.9 %collective-permute-start.5 = (bf16[8,16,16,256]{3,2,1,0:T(8,128)(2,1)S(1)}, bf16[8,16,16,256]{3,2,1,0:T(8,128)(2,1)S(1)}, u32[]{:S(2)}, u32[]{:S(2)}) collective-permute-start(bf16[8,16,16,256]{3,2,1,0:T(8,128)(2,1)S(1)} %collective-permute-done.refs_1_), channel_id=1, source_target_pairs={{0,1},{1,0},{2,3},{3,2},{4,5},{5,4},{6,7},{7,6},{8,9},{9,8},{10,11... | collective-permute-start | bytes 3145736 | tf_op jit(solution)/shard_map/ppermute | solution.py:436
  63.8 6.7 %collective-permute-start.8 = (bf16[96,16,256]{2,1,0:T(8,128)(2,1)}, bf16[96,16,256]{2,1,0:T(8,128)(2,1)S(1)}, u32[]{:S(2)}, u32[]{:S(2)}) collective-permute-start(bf16[96,16,256]{2,1,0:T(8,128)(2,1)} %collective-permute-done.3.refs_4_), channel_id=1, source_target_pairs={{0,1},{1,0},{2,3},{3,2},{4,5},{5,4},{6,7},{7,6},{8,9},{9,8},{10,11... | collective-permute-start | bytes 2359304 | tf_op jit(solution)/shard_map/ppermute | solution.py:436
  66.3 4.4 %collective-permute-start.7 = (bf16[96,16,256]{2,1,0:T(8,128)(2,1)}, bf16[96,16,256]{2,1,0:T(8,128)(2,1)S(1)}, u32[]{:S(2)}, u32[]{:S(2)}) collective-permute-start(bf16[96,16,256]{2,1,0:T(8,128)(2,1)} %collective-permute-done.2.refs_3_), channel_id=1, source_target_pairs={{0,1},{1,0},{2,3},{3,2},{4,5},{5,4},{6,7},{7,6},{8,9},{9,8},{10,11... | collective-permute-start | bytes 2359304 | tf_op jit(solution)/shard_map/ppermute | solution.py:436
  70.5 1.0 copy-start.2
  70.5 1.3 copy-start.3
  70.6 1.5 copy-start.5
  70.6 1.7 %copy-start.6 = (bf16[96,16,256]{2,1,0:T(8,128)(2,1)}, bf16[96,16,256]{2,1,0:T(8,128)(2,1)S(1)}, u32[]{:S(2)}) copy-start(bf16[96,16,256]{2,1,0:T(8,128)(2,1)S(1)} %collective-permute-done.7.refs_8_) | copy-start | bytes 2359300
  (2 other events, 1.5 us)

commit v3 on v2

--- a/solution.py
+++ b/solution.py
@@ -57,8 +57,9 @@
     gap = (device >> 1) - (here >> 1)
     side = jnp.where(gap < 0, 0, 1)
     near = jnp.where(gap == 0, 0, 4 + 4 * side) + slot
-    place = jnp.where(jnp.abs(gap) <= 1, near, 12 + 4 * side + slot)
-    place = place + jnp.where((device & 1) == (here & 1), 0, 20)
+    same = (device & 1) == (here & 1)
+    far = 12 + jnp.where(same, 4 * side, 0) + slot
+    place = jnp.where(jnp.abs(gap) <= 1, near, far) + jnp.where(same, 0, 20)
     return jnp.clip(place, 0, 39)
 
 
@@ -169,7 +170,7 @@
     )
 
 
-def pool_copies(sources, pools, sems):
+def pool_copies(sources, pools, stored, weights, sems):
     feats, cots = ([], [])
 
     def add(group, source, target):
@@ -192,10 +193,12 @@
                         pools[1].at[at, pl.ds(end * (SIDE - RIM), RIM)],
                     )
                 at += 1
+    for k, (source, target) in enumerate(zip(stored, weights)):
+        add(feats if k < 3 else cots, source, target)
     return (feats, cots)
 
 
-COPIES = 2 * (3 * 2 + 8 * 3)
+COPIES = 2 * 3 * 2 + 12 * 3 + 6
 
 
 def inner_tile(region, lane):
@@ -212,13 +215,15 @@
 
 
 def whole_kernel(meta, owner, near, *refs):
-    sources, refs = ((refs[:5], refs[5:10]), refs[10:])
-    (w_red, w_tap, w_exp, v_red, v_tap, v_exp, norms, out, grad_in, grads,
+    sources, stored, refs = ((refs[:5], refs[5:9]), refs[9:15], refs[15:])
+    weights, refs = (refs[-6:], refs[:-6])
+    w_red, w_tap, w_exp, v_red, v_tap, v_exp = weights
+    (norms, out, grad_in, grads,
      feats, cots, sems, region, present, masks, gates, stack, center, products, s_one, s_two, s_three,
      a_own, h_one, h_two, d_one, total) = refs
     pair = pl.program_id(0)
     here, section = (meta[0], meta[1])
-    copies = pool_copies(sources, (feats, cots), sems)
+    copies = pool_copies(sources, (feats, cots), stored, weights, sems)
 
     @pl.when(pair == 0)
     def _():
@@ -396,8 +401,8 @@
         grid_spec=pltpu.PrefetchScalarGridSpec(
             num_scalar_prefetch=len(scalars),
             grid=(2,),
-            in_specs=[pl.BlockSpec(memory_space=pl.ANY)] * len(sources)
-            + [whole(item) for item in weights],
+            in_specs=[pl.BlockSpec(memory_space=pl.ANY)] * (len(sources) + 6)
+            + [whole(weights[6])],
             out_specs=[pair, pair, whole(grads)],
             scratch_shapes=[
                 pool,
@@ -418,6 +423,7 @@
                 pltpu.VMEM(narrow, BF),
                 pltpu.VMEM(narrow, BF),
                 pltpu.VMEM((640, 128), F32),
+                *[pltpu.VMEM(item.shape, BF) for item in weights[:6]],
             ],
         ),
         out_shape=[tiles, tiles, grads],
@@ -441,14 +447,22 @@
     return jnp.concatenate([item.reshape(-1, SIDE, CHANS) for item in (both[:4], *ends)])
 
 
-def exchange(features, cotangent):
+def reach_close(features, cotangent):
     both = jnp.concatenate([features, cotangent])
-    column = [both]
-    for distance in (2, -2):
-        column.append(shift(both, TILE_AXES, distance))
-    for k, distance in ((1, 2), (2, -2)):
-        column.append(shift(trimmed(column[k]), TILE_AXES, distance))
-    return column + [other_core(item) for item in column]
+    return [both, shift(both, TILE_AXES, 2), shift(both, TILE_AXES, -2)]
+
+
+def reach_far(column):
+    return [
+        shift(trimmed(column[1]), TILE_AXES, 2),
+        shift(trimmed(column[2]), TILE_AXES, -2),
+    ]
+
+
+def swap_cores(column, far, early):
+    needed = jnp.where(lax.axis_index("core") == 0, far[1], far[0])
+    swapped = [other_core(column[0]), early, other_core(column[2]), other_core(needed)]
+    return [*column, *far, *swapped]
 
 
 def swap_chunks(parts, axes):
@@ -472,12 +486,12 @@
     return (high, low)
 
 
-def gather_params(w_reduce, w_taps, w_expand, norm_scale, norm_shift):
-    pieces = [w_reduce, w_taps, w_expand]
-    for item in (norm_scale, norm_shift):
-        pieces.extend(split_float(item))
+def gather_params(pieces):
     packed = jnp.concatenate([item.reshape(-1, 128) for item in pieces])
-    every = lax.all_gather(packed, "section", axis=0, tiled=False)
+    return lax.all_gather(packed, "section", axis=0, tiled=False)
+
+
+def cut_params(every, pieces):
     at = 0
     cut = []
     for item in pieces:
@@ -533,10 +547,13 @@
     meta = jnp.concatenate([here[None], section[None], ids.astype(jnp.int32)])
     scalars = (meta, owner, neighbours.reshape(-1))
 
-    sources = exchange(features, out_cotangent)
-    w_red, w_tap, w_exp, scale, offset = gather_params(
-        w_reduce, w_taps, w_expand, norm_scale, norm_shift
-    )
+    pieces = [w_reduce, w_taps, w_expand, *split_float(norm_scale), *split_float(norm_shift)]
+    column = reach_close(features, out_cotangent)
+    column, every = lax.optimization_barrier((column, gather_params(pieces)))
+    far = reach_far(column)
+    early = other_core(column[1])
+    every, early = lax.optimization_barrier((every, early))
+    w_red, w_tap, w_exp, scale, offset = cut_params(every, pieces)
     taps = w_tap.reshape(4, 3, 3, WIDTH, WIDTH)
     turned = taps[:, ::-1, ::-1].swapaxes(3, 4)
     weights = (
@@ -548,6 +565,8 @@
         twice(w_exp.swapaxes(1, 2)),
         norm_rows(scale, offset),
     )
+    far, weights = lax.optimization_barrier((far, weights))
+    sources = swap_cores(column, far, early)
     out, grad_in, grads = run_kernel(scalars, sources, weights)
     total = sum_over_tiles(grads)
     g_taps = jnp.concatenate([total[:288, :64], total[:288, 64:]])

time: 164 us -> 171 us (1.043)
  blocking collectives: 57.3 us -> 62.1 us
  waiting for transfers between devices: 4.14 us -> 6.46 us
    all_to_all x3, blocking collectives: 47.3 us -> 51.6 us  [swap_chunks(): return lax.all_to_all(parts, axes, 0, 0, tiled=True)]
    ppermute x4, waiting for transfers between devices: 4.05 us -> 6.45 us  [shift(): lax.ppermute(block, axes, [(i, i + distance) for i in devices if i + dist...]
    another operation x8, local copies, waits for them, and re-layouts: 0.76 us -> 3.16 us  [norm_rows(): return jnp.stack(rows, axis=1)]
    select_n x0 -> x1, other arithmetic: none -> 2.13 us  [swap_cores(): needed = jnp.where(lax.axis_index('core') == 0, far[1], far[0])]
    another operation x6, other arithmetic: 5.01 us -> 3.03 us  [tap_pair(): jnp.stack([grid((0, 1, 2, None), (0, 1, 2, None)), grid((0, 1, None, 2),...]
    ppermute x5 -> x4, starting transfers between devices: 18.4 us -> 17.5 us  [other_core(): return lax.ppermute(block, 'core', [(0, 1), (1, 0)])]
    unnamed x38 -> x46, local copies, waits for them, and re-layouts: 7.95 us -> 7.29 us
  transfers between devices with their start and end apart: 9 -> 8, of which waited for: 2 -> 3; matrix products, arithmetic and copies ran while one was open for 12% -> 12% of each run, Pallas kernels for 0% -> 0%
where the time goes in v3:
time: 171 us; the launch traced here: 170 us
  blocking collectives  62.1 us (36%)
  Pallas kernels  40.2 us (24%)
  starting transfers between devices  29.9 us (17%)
  local copies, waits for them, and re-layouts  18.6 us (11%)
  other arithmetic  11.4 us (7%)
  waiting for transfers between devices  6.46 us (4%)
    all_to_all x3, blocking collectives, swap_chunks(): return lax.all_to_all(parts, axes, 0, 0, tiled=True)  51.6 us
    pallas_call x1, Pallas kernels, run_kernel(): pl.pallas_call(whole_kernel, grid_spec=pltpu.PrefetchScalarGridSpec(num_s...  40.2 us
    ppermute x4, starting transfers between devices, other_core(): return lax.ppermute(block, 'core', [(0, 1), (1, 0)])  17.5 us
    ppermute x4, starting transfers between devices, shift(): lax.ppermute(block, axes, [(i, i + distance) for i in devices if i + dist...  12.4 us
    all_gather x1, blocking collectives, gather_params(): return lax.all_gather(packed, 'section', axis=0, tiled=False)  10.5 us
    unnamed x46, local copies, waits for them, and re-layouts  7.29 us
    ppermute x4, waiting for transfers between devices, shift(): lax.ppermute(block, axes, [(i, i + distance) for i in devices if i + dist...  6.45 us
  transfers between devices with their start and end apart: 8, of which 3 were waited for; matrix products, arithmetic and copies ran while one was open for 12% of the time, Pallas kernels for 0%

profile of v3, /device:TPU:1, one launch (start us, length us, event | category | flops | bytes accessed | tf_op | source)
XLA Modules:
  0.0 169.8 jit_solution(10124557309129025896)
XLA Ops:
  0.6 1.9 %constant_dynamic-update-slice_fusion.1 = bf16[8,16,16,256]{3,2,1,0:T(8,128)(2,1)} fusion(bf16[4,16,16,256]{3,2,1,0:T(8,128)(2,1)} %param.9), kind=kLoop, calls=%fused_computation.91 | loop fusion | bytes 1048576
  3.4 1.4 collective-permute-start.1
  4.9 4.7 %collective-permute-start = (bf16[8,16,16,256]{3,2,1,0:T(8,128)(2,1)}, bf16[8,16,16,256]{3,2,1,0:T(8,128)(2,1)S(1)}, u32[]{:S(2)}, u32[]{:S(2)}) collective-permute-start(bf16[8,16,16,256]{3,2,1,0:T(8,128)(2,1)} %constant_dynamic-update-slice_fusion.refs_0_), channel_id=1, source_target_pairs={{0,2},{1,3},{2,4},{3,5},{4,6},{5,7},{6,8},{7,9},{8,10},{9,11},{10,... | collective-permute-start | bytes 3145736 | tf_op jit(solution)/shard_map/ppermute | solution.py:438
  12.2 10.5 %all-gather.1 = bf16[4,556,128]{2,1,0:T(8,128)(2,1)S(1)} all-gather(bf16[1,556,128]{2,1,0:T(8,128)(2,1)S(1)} %bitcast.102), channel_id=2, replica_groups=mesh['section'=4,'z'=8,'y'=8,'core'=2] {'section'}, dimensions={0}, use_global_device_ids=true | all-gather | bytes 711680 | tf_op jit(solution)/shard_map/all_gather | solution.py:491
  22.7 2.0 %collective-permute-done.1.refs_2_ = bf16[8,16,16,256]{3,2,1,0:T(8,128)(2,1)S(1)} collective-permute-done((bf16[8,16,16,256]{3,2,1,0:T(8,128)(2,1)}, bf16[8,16,16,256]{3,2,1,0:T(8,128)(2,1)S(1)}, u32[]{:S(2)}, u32[]{:S(2)}) %collective-permute-start.1) | collective-permute-done | bytes 1048608 | tf_op jit(solution)/shard_map/ppermute | solution.py:438
  24.8 1.0 collective-permute-done.refs_1_
  25.8 9.3 %collective-permute-start.4 = (bf16[8,16,16,256]{3,2,1,0:T(8,128)(2,1)S(1)}, bf16[8,16,16,256]{3,2,1,0:T(8,128)(2,1)}, u32[]{:S(2)}, u32[]{:S(2)}) collective-permute-start(bf16[8,16,16,256]{3,2,1,0:T(8,128)(2,1)S(1)} %collective-permute-done.refs_1_), channel_id=1, source_target_pairs={{0,1},{1,0},{2,3},{3,2},{4,5},{5,4},{6,7},{7,6},{8,9},{9,8},{10,11... | collective-permute-start | bytes 3145736 | tf_op jit(solution)/shard_map/ppermute | solution.py:442
  35.2 1.9 %collective-permute-start.6 = (bf16[8,16,16,256]{3,2,1,0:T(8,128)(2,1)S(1)}, bf16[8,16,16,256]{3,2,1,0:T(8,128)(2,1)}, u32[]{:S(2)}, u32[]{:S(2)}) collective-permute-start(bf16[8,16,16,256]{3,2,1,0:T(8,128)(2,1)S(1)} %collective-permute-done.1.refs_2_), channel_id=1, source_target_pairs={{0,1},{1,0},{2,3},{3,2},{4,5},{5,4},{6,7},{7,6},{8,9},{9,8},{10,11... | collective-permute-start | bytes 3145736 | tf_op jit(solution)/shard_map/ppermute | solution.py:442
  38.2 5.0 %collective-permute-start.2 = (bf16[96,16,256]{2,1,0:T(8,128)(2,1)}, bf16[96,16,256]{2,1,0:T(8,128)(2,1)}, u32[]{:S(2)}, u32[]{:S(2)}) collective-permute-start(bf16[96,16,256]{2,1,0:T(8,128)(2,1)} %pad_maximum_fusion.2), channel_id=1, source_target_pairs={{0,2},{1,3},{2,4},{3,5},{4,6},{5,7},{6,8},{7,9},{8,10},{9,11},{10,... | collective-permute-start | bytes 2359304 | tf_op jit(solution)/shard_map/ppermute | solution.py:438
  43.2 1.0 pad_maximum_fusion.3
  44.2 1.3 collective-permute-start.3
  45.5 2.7 %collective-permute-start.5 = (bf16[8,16,16,256]{3,2,1,0:T(8,128)(2,1)}, bf16[8,16,16,256]{3,2,1,0:T(8,128)(2,1)}, u32[]{:S(2)}, u32[]{:S(2)}) collective-permute-start(bf16[8,16,16,256]{3,2,1,0:T(8,128)(2,1)} %constant_dynamic-update-slice_fusion.refs_0_), channel_id=1, source_target_pairs={{0,1},{1,0},{2,3},{3,2},{4,5},{5,4},{6,7},{7,6},{8,9},{9,8},{10,11... | collective-permute-start | bytes 3145736 | tf_op jit(solution)/shard_map/ppermute | solution.py:442
  51.2 1.1 fusion.28
  55.5 1.3 fusion.22
  56.8 1.1 fusion.24
  60.2 1.1 pad_maximum_fusion.1.refs_13_
  61.3 3.4 %collective-permute-done.3.refs_4_ = bf16[96,16,256]{2,1,0:T(8,128)(2,1)} collective-permute-done((bf16[96,16,256]{2,1,0:T(8,128)(2,1)}, bf16[96,16,256]{2,1,0:T(8,128)(2,1)}, u32[]{:S(2)}, u32[]{:S(2)}) %collective-permute-start.3) | collective-permute-done | bytes 786464 | tf_op jit(solution)/shard_map/ppermute | solution.py:438
  64.7 2.1 %broadcast_select_fusion = bf16[96,16,256]{2,1,0:T(8,128)(2,1)} fusion(bf16[96,16,256]{2,1,0:T(8,128)(2,1)} %collective-permute-done.3.refs_4_, bf16[96,16,256]{2,1,0:T(8,128)(2,1)} %collective-permute-done.2.refs_3_, pred[]{:T(512)S(6)} %eq.19), kind=kLoop, calls=%fused_computation.16 | loop fusion | flops 393216 | bytes 2359297 | tf_op jit(solution)/shard_map/jit(_where)/select_n | solution.py:463
  66.8 3.6 %collective-permute-start.7 = (bf16[96,16,256]{2,1,0:T(8,128)(2,1)}, bf16[96,16,256]{2,1,0:T(8,128)(2,1)S(1)}, u32[]{:S(2)}, u32[]{:S(2)}) collective-permute-start(bf16[96,16,256]{2,1,0:T(8,128)(2,1)} %broadcast_select_fusion), channel_id=1, source_target_pairs={{0,1},{1,0},{2,3},{3,2},{4,5},{5,4},{6,7},{7,6},{8,9},{9,8},{10,11... | collective-permute-start | bytes 2359304 | tf_op jit(solution)/shard_map/ppermute | solution.py:442
  73.5 1.0 copy.107.refs_10_
  75.4 40.2 %shard_map.128 = (bf16[4,16,16,256]{3,2,1,0:T(8,128)(2,1)}, bf16[4,16,16,256]{3,2,1,0:T(8,128)(2,1)}, bf16[640,128]{1,0:T(8,128)(2,1)}) custom-call(s32[6]{0:T(128)} %pad_add_fusion.meta, s32[512]{0:T(512)} %owner.1, s32[2048]{0:T(1024)} %reshape.95.near, bf16[8,16,16,256]{3,2,1,0:T(8,128)(2,1)} %constant_dynamic-update-slice_fusion.refs_0_, ...), custom_call_target="tpu_custom_call" | custom-call | tf_op jit(solution)/shard_map/pallas_call | solution.py:399
  115.6 20.0 %all_to_all.21 = bf16[16,40,128]{2,1,0:T(8,128)(2,1)S(1)} all-to-all(bf16[16,40,128]{2,1,0:T(8,128)(2,1)} %bitcast.109), channel_id=1, replica_groups=mesh['section'=4,'z'=8,'y'=8,'core'=2] {'y','core'}, dimensions={0} | all-to-all | bytes 327680 | tf_op jit(solution)/shard_map/all_to_all | solution.py:469
  135.7 18.2 %all_to_all.22 = bf16[8,40,128]{2,1,0:T(8,128)(2,1)S(1)} all-to-all(bf16[8,40,128]{2,1,0:T(8,128)(2,1)S(1)} %tile.4), channel_id=1, replica_groups=mesh['section'=4,'z'=8,'y'=8,'core'=2] {'z'}, dimensions={0} | all-to-all | bytes 163840 | tf_op jit(solution)/shard_map/all_to_all | solution.py:469
  154.0 13.4 %all_to_all.23 = bf16[16,40,128]{2,1,0:T(8,128)(2,1)S(1)} all-to-all(bf16[16,40,128]{2,1,0:T(8,128)(2,1)S(1)} %tile.5), channel_id=1, replica_groups=mesh['section'=4,'z'=8,'y'=8,'core'=2] {'y','core'}, dimensions={0} | all-to-all | bytes 327680 | tf_op jit(solution)/shard_map/all_to_all | solution.py:469
  (115 shorter events, 19.5 us)
Async XLA Ops:
  0.6 1.9 %copy-start.4 = (bf16[4,16,16,256]{3,2,1,0:T(8,128)(2,1)S(1)}, bf16[4,16,16,256]{3,2,1,0:T(8,128)(2,1)}, u32[]{:S(2)}) copy-start(bf16[4,16,16,256]{3,2,1,0:T(8,128)(2,1)} %param.10) | copy-start | bytes 1572868
  2.6 7.0 %copy-start.12 = (bf16[1,64,256]{2,1,0:T(8,128)(2,1)S(1)}, bf16[1,64,256]{2,1,0:T(8,128)(2,1)}, u32[]{:S(2)}) copy-start(bf16[1,64,256]{2,1,0:T(8,128)(2,1)} %param.13) | copy-start | bytes 98308
  3.4 6.2 %copy-start.7 = (bf16[1,256,64]{1,2,0:T(8,128)(2,1)S(1)}, bf16[1,256,64]{1,2,0:T(8,128)(2,1)}, u32[]{:S(2)}) copy-start(bf16[1,256,64]{1,2,0:T(8,128)(2,1)} %param.11) | copy-start | bytes 98308
  3.4 21.3 %collective-permute-start.1 = (bf16[8,16,16,256]{3,2,1,0:T(8,128)(2,1)}, bf16[8,16,16,256]{3,2,1,0:T(8,128)(2,1)S(1)}, u32[]{:S(2)}, u32[]{:S(2)}) collective-permute-start(bf16[8,16,16,256]{3,2,1,0:T(8,128)(2,1)} %constant_dynamic-update-slice_fusion.refs_0_), channel_id=1, source_target_pairs={{2,0},{3,1},{4,2},{5,3},{6,4},{7,5},{8,6},{9,7},{10,8},{11,9},{12,... | collective-permute-start | bytes 3145736 | tf_op jit(solution)/shard_map/ppermute | solution.py:438
  4.9 20.9 %collective-permute-start = (bf16[8,16,16,256]{3,2,1,0:T(8,128)(2,1)}, bf16[8,16,16,256]{3,2,1,0:T(8,128)(2,1)S(1)}, u32[]{:S(2)}, u32[]{:S(2)}) collective-permute-start(bf16[8,16,16,256]{3,2,1,0:T(8,128)(2,1)} %constant_dynamic-update-slice_fusion.refs_0_), channel_id=1, source_target_pairs={{0,2},{1,3},{2,4},{3,5},{4,6},{5,7},{6,8},{7,9},{8,10},{9,11},{10,... | collective-permute-start | bytes 3145736 | tf_op jit(solution)/shard_map/ppermute | solution.py:438
  9.6 0.9 copy-start.6
  24.8 12.4 %copy-start = (bf16[8,16,16,256]{3,2,1,0:T(8,128)(2,1)}, bf16[8,16,16,256]{3,2,1,0:T(8,128)(2,1)S(1)}, u32[]{:S(2)}) copy-start(bf16[8,16,16,256]{3,2,1,0:T(8,128)(2,1)S(1)} %collective-permute-done.1.refs_2_) | copy-start | bytes 3145732
  25.8 11.4 %copy-start.1 = (bf16[8,16,16,256]{3,2,1,0:T(8,128)(2,1)}, bf16[8,16,16,256]{3,2,1,0:T(8,128)(2,1)S(1)}, u32[]{:S(2)}) copy-start(bf16[8,16,16,256]{3,2,1,0:T(8,128)(2,1)S(1)} %collective-permute-done.refs_1_) | copy-start | bytes 3145732
  25.8 22.4 %collective-permute-start.4 = (bf16[8,16,16,256]{3,2,1,0:T(8,128)(2,1)S(1)}, bf16[8,16,16,256]{3,2,1,0:T(8,128)(2,1)}, u32[]{:S(2)}, u32[]{:S(2)}) collective-permute-start(bf16[8,16,16,256]{3,2,1,0:T(8,128)(2,1)S(1)} %collective-permute-done.refs_1_), channel_id=1, source_target_pairs={{0,1},{1,0},{2,3},{3,2},{4,5},{5,4},{6,7},{7,6},{8,9},{9,8},{10,11... | collective-permute-start | bytes 3145736 | tf_op jit(solution)/shard_map/ppermute | solution.py:442
  35.2 39.3 %collective-permute-start.6 = (bf16[8,16,16,256]{3,2,1,0:T(8,128)(2,1)S(1)}, bf16[8,16,16,256]{3,2,1,0:T(8,128)(2,1)}, u32[]{:S(2)}, u32[]{:S(2)}) collective-permute-start(bf16[8,16,16,256]{3,2,1,0:T(8,128)(2,1)S(1)} %collective-permute-done.1.refs_2_), channel_id=1, source_target_pairs={{0,1},{1,0},{2,3},{3,2},{4,5},{5,4},{6,7},{7,6},{8,9},{9,8},{10,11... | collective-permute-start | bytes 3145736 | tf_op jit(solution)/shard_map/ppermute | solution.py:442
  38.2 23.1 %collective-permute-start.2 = (bf16[96,16,256]{2,1,0:T(8,128)(2,1)}, bf16[96,16,256]{2,1,0:T(8,128)(2,1)}, u32[]{:S(2)}, u32[]{:S(2)}) collective-permute-start(bf16[96,16,256]{2,1,0:T(8,128)(2,1)} %pad_maximum_fusion.2), channel_id=1, source_target_pairs={{0,2},{1,3},{2,4},{3,5},{4,6},{5,7},{6,8},{7,9},{8,10},{9,11},{10,... | collective-permute-start | bytes 2359304 | tf_op jit(solution)/shard_map/ppermute | solution.py:438
  44.2 20.5 %collective-permute-start.3 = (bf16[96,16,256]{2,1,0:T(8,128)(2,1)}, bf16[96,16,256]{2,1,0:T(8,128)(2,1)}, u32[]{:S(2)}, u32[]{:S(2)}) collective-permute-start(bf16[96,16,256]{2,1,0:T(8,128)(2,1)} %pad_maximum_fusion.3), channel_id=1, source_target_pairs={{2,0},{3,1},{4,2},{5,3},{6,4},{7,5},{8,6},{9,7},{10,8},{11,9},{12,... | collective-permute-start | bytes 2359304 | tf_op jit(solution)/shard_map/ppermute | solution.py:438
  45.5 29.1 %collective-permute-start.5 = (bf16[8,16,16,256]{3,2,1,0:T(8,128)(2,1)}, bf16[8,16,16,256]{3,2,1,0:T(8,128)(2,1)}, u32[]{:S(2)}, u32[]{:S(2)}) collective-permute-start(bf16[8,16,16,256]{3,2,1,0:T(8,128)(2,1)} %constant_dynamic-update-slice_fusion.refs_0_), channel_id=1, source_target_pairs={{0,1},{1,0},{2,3},{3,2},{4,5},{5,4},{6,7},{7,6},{8,9},{9,8},{10,11... | collective-permute-start | bytes 3145736 | tf_op jit(solution)/shard_map/ppermute | solution.py:442
  51.2 1.1 copy-start.18
  51.2 1.8 %copy-start.16 = (f32[4,64]{1,0:T(4,128)S(1)}, f32[4,64]{1,0:T(4,128)}, u32[]{:S(2)}) copy-start(f32[4,64]{1,0:T(4,128)} %get-tuple-element.82) | copy-start | bytes 3076
  51.2 2.5 %copy-start.17 = (f32[4,64]{1,0:T(4,128)S(1)}, f32[4,64]{1,0:T(4,128)}, u32[]{:S(2)}) copy-start(f32[4,64]{1,0:T(4,128)} %get-tuple-element.85) | copy-start | bytes 3076
  52.2 2.8 %copy-start.5 = (bf16[4,128,128]{2,1,0:T(8,128)(2,1)S(1)}, bf16[4,128,128]{2,1,0:T(8,128)(2,1)}, u32[]{:S(2)}) copy-start(bf16[4,128,128]{2,1,0:T(8,128)(2,1)} %get-tuple-element.74) | copy-start | bytes 393220
  52.3 2.1 %copy-start.15 = (f32[4,64]{1,0:T(4,128)S(1)}, f32[4,64]{1,0:T(4,128)}, u32[]{:S(2)}) copy-start(f32[4,64]{1,0:T(4,128)} %get-tuple-element.83) | copy-start | bytes 3076
  56.8 1.2 copy-start.2
  58.0 0.7 copy-start.11
  58.1 0.7 copy-start.8
  58.1 0.7 copy-start.9
  66.8 7.7 %collective-permute-start.7 = (bf16[96,16,256]{2,1,0:T(8,128)(2,1)}, bf16[96,16,256]{2,1,0:T(8,128)(2,1)S(1)}, u32[]{:S(2)}, u32[]{:S(2)}) collective-permute-start(bf16[96,16,256]{2,1,0:T(8,128)(2,1)} %broadcast_select_fusion), channel_id=1, source_target_pairs={{0,1},{1,0},{2,3},{3,2},{4,5},{5,4},{6,7},{7,6},{8,9},{9,8},{10,11... | collective-permute-start | bytes 2359304 | tf_op jit(solution)/shard_map/ppermute | solution.py:442
  74.5 0.9 copy-start.3
  (5 other events, 3.4 us)

commit v4 on v3

--- a/solution.py
+++ b/solution.py
@@ -452,11 +452,8 @@
     return [both, shift(both, TILE_AXES, 2), shift(both, TILE_AXES, -2)]
 
 
-def reach_far(column):
-    return [
-        shift(trimmed(column[1]), TILE_AXES, 2),
-        shift(trimmed(column[2]), TILE_AXES, -2),
-    ]
+def reach_far(sent):
+    return [shift(sent[0], TILE_AXES, 2), shift(sent[1], TILE_AXES, -2)]
 
 
 def swap_cores(column, far, early):
@@ -550,7 +547,9 @@
     pieces = [w_reduce, w_taps, w_expand, *split_float(norm_scale), *split_float(norm_shift)]
     column = reach_close(features, out_cotangent)
     column, every = lax.optimization_barrier((column, gather_params(pieces)))
-    far = reach_far(column)
+    sent = [trimmed(column[1]), trimmed(column[2])]
+    column, sent = lax.optimization_barrier((column, sent))
+    far = reach_far(sent)
     early = other_core(column[1])
     every, early = lax.optimization_barrier((every, early))
     w_red, w_tap, w_exp, scale, offset = cut_params(every, pieces)

time: 171 us -> 168 us (0.982)
  local copies, waits for them, and re-layouts: 18.6 us -> 15.8 us
    another operation x8, local copies, waits for them, and re-layouts: 3.16 us -> 0.78 us  [norm_rows(): return jnp.stack(rows, axis=1)]
    concatenate x2 -> x4, other arithmetic: 2.36 us -> 3.63 us  [twice(): jnp.concatenate([jnp.concatenate([weights, zero], axis=-1), jnp.concatena...]
    unnamed x46 -> x36, local copies, waits for them, and re-layouts: 7.29 us -> 6.62 us
  transfers between devices with their start and end apart: 8 -> 8, of which waited for: 3 -> 3; matrix products, arithmetic and copies ran while one was open for 12% -> 10% of each run, Pallas kernels for 0% -> 0%
where the time goes in v4:
time: 168 us; the launch traced here: 167 us
  blocking collectives  63.7 us (38%)
  Pallas kernels  40.2 us (24%)
  starting transfers between devices  29.4 us (18%)
  local copies, waits for them, and re-layouts  15.8 us (9%)
  other arithmetic  11.6 us (7%)
  waiting for transfers between devices  4.89 us (3%)
    all_to_all x3, blocking collectives, swap_chunks(): return lax.all_to_all(parts, axes, 0, 0, tiled=True)  52.5 us
    pallas_call x1, Pallas kernels, run_kernel(): pl.pallas_call(whole_kernel, grid_spec=pltpu.PrefetchScalarGridSpec(num_s...  40.2 us
    ppermute x4, starting transfers between devices, other_core(): return lax.ppermute(block, 'core', [(0, 1), (1, 0)])  17.9 us
    ppermute x4, starting transfers between devices, shift(): lax.ppermute(block, axes, [(i, i + distance) for i in devices if i + dist...  11.5 us
    all_gather x1, blocking collectives, gather_params(): return lax.all_gather(packed, 'section', axis=0, tiled=False)  11.2 us
    unnamed x36, local copies, waits for them, and re-layouts  6.62 us
    ppermute x4, waiting for transfers between devices, shift(): lax.ppermute(block, axes, [(i, i + distance) for i in devices if i + dist...  4.88 us
    concatenate x4, other arithmetic, twice(): jnp.concatenate([jnp.concatenate([weights, zero], axis=-1), jnp.concatena...  3.63 us
  transfers between devices with their start and end apart: 8, of which 3 were waited for; matrix products, arithmetic and copies ran while one was open for 10% of the time, Pallas kernels for 0%

profile of v4, /device:TPU:1, one launch (start us, length us, event | category | flops | bytes accessed | tf_op | source)
XLA Modules:
  0.0 166.6 jit_solution(18156876959249018962)
XLA Ops:
  0.6 1.1 constant_dynamic-update-slice_fusion.1
  1.9 1.4 collective-permute-start.1
  3.3 4.7 %collective-permute-start = (bf16[8,16,16,256]{3,2,1,0:T(8,128)(2,1)S(1)}, bf16[8,16,16,256]{3,2,1,0:T(8,128)(2,1)S(1)}, u32[]{:S(2)}, u32[]{:S(2)}) collective-permute-start(bf16[8,16,16,256]{3,2,1,0:T(8,128)(2,1)S(1)} %constant_dynamic-update-slice_fusion.refs_0_), channel_id=1, source_target_pairs={{0,2},{1,3},{2,4},{3,5},{4,6},{5,7},{6,8},{7,9},{8,10},{9,11},{10,... | collective-permute-start | bytes 3145736 | tf_op jit(solution)/shard_map/ppermute | solution.py:438
  10.7 11.2 %all-gather.1 = bf16[4,556,128]{2,1,0:T(8,128)(2,1)} all-gather(bf16[1,556,128]{2,1,0:T(8,128)(2,1)S(1)} %bitcast.104), channel_id=2, replica_groups=mesh['section'=4,'z'=8,'y'=8,'core'=2] {'section'}, dimensions={0}, use_global_device_ids=true | all-gather | bytes 711680 | tf_op jit(solution)/shard_map/all_gather | solution.py:488
  21.9 1.2 collective-permute-done.1.refs_2_
  25.0 1.0 pad_maximum_fusion.3
  26.1 1.0 pad_maximum_fusion.2
  27.5 9.4 %collective-permute-start.4 = (bf16[8,16,16,256]{3,2,1,0:T(8,128)(2,1)S(1)}, bf16[8,16,16,256]{3,2,1,0:T(8,128)(2,1)}, u32[]{:S(2)}, u32[]{:S(2)}) collective-permute-start(bf16[8,16,16,256]{3,2,1,0:T(8,128)(2,1)S(1)} %copy-done.2), channel_id=1, source_target_pairs={{0,1},{1,0},{2,3},{3,2},{4,5},{5,4},{6,7},{7,6},{8,9},{9,8},{10,11... | collective-permute-start | bytes 3145736 | tf_op jit(solution)/shard_map/ppermute | solution.py:442
  36.9 4.0 %collective-permute-start.2 = (bf16[96,16,256]{2,1,0:T(8,128)(2,1)}, bf16[96,16,256]{2,1,0:T(8,128)(2,1)S(1)}, u32[]{:S(2)}, u32[]{:S(2)}) collective-permute-start(bf16[96,16,256]{2,1,0:T(8,128)(2,1)} %pad_maximum_fusion.2), channel_id=1, source_target_pairs={{0,2},{1,3},{2,4},{3,5},{4,6},{5,7},{6,8},{7,9},{8,10},{9,11},{10,... | collective-permute-start | bytes 2359304 | tf_op jit(solution)/shard_map/ppermute | solution.py:438
  41.0 1.3 collective-permute-start.3
  42.3 2.2 %collective-permute-start.5 = (bf16[8,16,16,256]{3,2,1,0:T(8,128)(2,1)}, bf16[8,16,16,256]{3,2,1,0:T(8,128)(2,1)}, u32[]{:S(2)}, u32[]{:S(2)}) collective-permute-start(bf16[8,16,16,256]{3,2,1,0:T(8,128)(2,1)} %copy-done.4), channel_id=1, source_target_pairs={{0,1},{1,0},{2,3},{3,2},{4,5},{5,4},{6,7},{7,6},{8,9},{9,8},{10,11... | collective-permute-start | bytes 3145736 | tf_op jit(solution)/shard_map/ppermute | solution.py:442
  44.5 2.1 %collective-permute-start.6 = (bf16[8,16,16,256]{3,2,1,0:T(8,128)(2,1)S(1)}, bf16[8,16,16,256]{3,2,1,0:T(8,128)(2,1)}, u32[]{:S(2)}, u32[]{:S(2)}) collective-permute-start(bf16[8,16,16,256]{3,2,1,0:T(8,128)(2,1)S(1)} %collective-permute-done.1.refs_2_), channel_id=1, source_target_pairs={{0,1},{1,0},{2,3},{3,2},{4,5},{5,4},{6,7},{7,6},{8,9},{9,8},{10,11... | collective-permute-start | bytes 3145736 | tf_op jit(solution)/shard_map/ppermute | solution.py:442
  47.7 1.0 fusion.32
  51.4 1.1 copy.104
  53.5 1.0 fusion.23.refs_14_
  58.1 1.1 pad_maximum_fusion.1.refs_13_
  59.1 2.9 %collective-permute-done.3.refs_4_ = bf16[96,16,256]{2,1,0:T(8,128)(2,1)} collective-permute-done((bf16[96,16,256]{2,1,0:T(8,128)(2,1)}, bf16[96,16,256]{2,1,0:T(8,128)(2,1)}, u32[]{:S(2)}, u32[]{:S(2)}) %collective-permute-start.3) | collective-permute-done | bytes 786464 | tf_op jit(solution)/shard_map/ppermute | solution.py:438
  62.0 1.0 broadcast_select_fusion
  63.0 4.1 %collective-permute-start.7 = (bf16[96,16,256]{2,1,0:T(8,128)(2,1)}, bf16[96,16,256]{2,1,0:T(8,128)(2,1)}, u32[]{:S(2)}, u32[]{:S(2)}) collective-permute-start(bf16[96,16,256]{2,1,0:T(8,128)(2,1)} %broadcast_select_fusion), channel_id=1, source_target_pairs={{0,1},{1,0},{2,3},{3,2},{4,5},{5,4},{6,7},{7,6},{8,9},{9,8},{10,11... | collective-permute-start | bytes 2359304 | tf_op jit(solution)/shard_map/ppermute | solution.py:442
  70.2 1.1 copy.107.refs_10_
  71.4 40.2 %shard_map.128 = (bf16[4,16,16,256]{3,2,1,0:T(8,128)(2,1)}, bf16[4,16,16,256]{3,2,1,0:T(8,128)(2,1)}, bf16[640,128]{1,0:T(8,128)(2,1)}) custom-call(s32[6]{0:T(128)} %pad_add_fusion.meta, s32[512]{0:T(512)} %owner.1, s32[2048]{0:T(1024)} %reshape.95.near, bf16[8,16,16,256]{3,2,1,0:T(8,128)(2,1)} %copy-done.4, bf16[8,16,16,256]{3,2,1,0:T(8,128)(2,1)} %copy-done.1, ...), custom_call_target="tpu_custom_call" | custom-call | tf_op jit(solution)/shard_map/pallas_call | solution.py:399
  111.6 21.0 %all_to_all.21 = bf16[16,40,128]{2,1,0:T(8,128)(2,1)S(1)} all-to-all(bf16[16,40,128]{2,1,0:T(8,128)(2,1)} %bitcast.111), channel_id=1, replica_groups=mesh['section'=4,'z'=8,'y'=8,'core'=2] {'y','core'}, dimensions={0} | all-to-all | bytes 327680 | tf_op jit(solution)/shard_map/all_to_all | solution.py:466
  132.6 18.2 %all_to_all.22 = bf16[8,40,128]{2,1,0:T(8,128)(2,1)S(1)} all-to-all(bf16[8,40,128]{2,1,0:T(8,128)(2,1)S(1)} %tile.4), channel_id=1, replica_groups=mesh['section'=4,'z'=8,'y'=8,'core'=2] {'z'}, dimensions={0} | all-to-all | bytes 163840 | tf_op jit(solution)/shard_map/all_to_all | solution.py:466
  150.8 13.4 %all_to_all.23 = bf16[16,40,128]{2,1,0:T(8,128)(2,1)S(1)} all-to-all(bf16[16,40,128]{2,1,0:T(8,128)(2,1)S(1)} %tile.5), channel_id=1, replica_groups=mesh['section'=4,'z'=8,'y'=8,'core'=2] {'y','core'}, dimensions={0} | all-to-all | bytes 327680 | tf_op jit(solution)/shard_map/all_to_all | solution.py:466
  (108 shorter events, 18.8 us)
Async XLA Ops:
  0.6 1.2 copy-start.7
  1.8 6.2 %copy-start.10 = (bf16[1,64,256]{2,1,0:T(8,128)(2,1)S(1)}, bf16[1,64,256]{2,1,0:T(8,128)(2,1)}, u32[]{:S(2)}) copy-start(bf16[1,64,256]{2,1,0:T(8,128)(2,1)} %param.13) | copy-start | bytes 98308
  1.9 22.1 %copy-start.4 = (bf16[8,16,16,256]{3,2,1,0:T(8,128)(2,1)}, bf16[8,16,16,256]{3,2,1,0:T(8,128)(2,1)S(1)}, u32[]{:S(2)}) copy-start(bf16[8,16,16,256]{3,2,1,0:T(8,128)(2,1)S(1)} %constant_dynamic-update-slice_fusion.refs_0_) | copy-start | bytes 3145732
  1.9 6.2 %copy-start.9 = (bf16[1,256,64]{1,2,0:T(8,128)(2,1)S(1)}, bf16[1,256,64]{1,2,0:T(8,128)(2,1)}, u32[]{:S(2)}) copy-start(bf16[1,256,64]{1,2,0:T(8,128)(2,1)} %param.11) | copy-start | bytes 98308
  1.9 21.2 %collective-permute-start.1 = (bf16[8,16,16,256]{3,2,1,0:T(8,128)(2,1)S(1)}, bf16[8,16,16,256]{3,2,1,0:T(8,128)(2,1)S(1)}, u32[]{:S(2)}, u32[]{:S(2)}) collective-permute-start(bf16[8,16,16,256]{3,2,1,0:T(8,128)(2,1)S(1)} %constant_dynamic-update-slice_fusion.refs_0_), channel_id=1, source_target_pairs={{2,0},{3,1},{4,2},{5,3},{6,4},{7,5},{8,6},{9,7},{10,8},{11,9},{12,... | collective-permute-start | bytes 3145736 | tf_op jit(solution)/shard_map/ppermute | solution.py:438
  3.3 20.6 %collective-permute-start = (bf16[8,16,16,256]{3,2,1,0:T(8,128)(2,1)S(1)}, bf16[8,16,16,256]{3,2,1,0:T(8,128)(2,1)S(1)}, u32[]{:S(2)}, u32[]{:S(2)}) collective-permute-start(bf16[8,16,16,256]{3,2,1,0:T(8,128)(2,1)S(1)} %constant_dynamic-update-slice_fusion.refs_0_), channel_id=1, source_target_pairs={{0,2},{1,3},{2,4},{3,5},{4,6},{5,7},{6,8},{7,9},{8,10},{9,11},{10,... | collective-permute-start | bytes 3145736 | tf_op jit(solution)/shard_map/ppermute | solution.py:438
  8.1 0.9 copy-start.8
  9.1 0.7 copy-start.13
  23.1 21.3 %copy-start = (bf16[8,16,16,256]{3,2,1,0:T(8,128)(2,1)}, bf16[8,16,16,256]{3,2,1,0:T(8,128)(2,1)S(1)}, u32[]{:S(2)}) copy-start(bf16[8,16,16,256]{3,2,1,0:T(8,128)(2,1)S(1)} %collective-permute-done.1.refs_2_) | copy-start | bytes 3145732
  23.9 1.0 copy-start.1
  25.0 1.1 slice-start
  26.0 1.5 copy-start.2
  27.5 19.1 %collective-permute-start.4 = (bf16[8,16,16,256]{3,2,1,0:T(8,128)(2,1)S(1)}, bf16[8,16,16,256]{3,2,1,0:T(8,128)(2,1)}, u32[]{:S(2)}, u32[]{:S(2)}) collective-permute-start(bf16[8,16,16,256]{3,2,1,0:T(8,128)(2,1)S(1)} %copy-done.2), channel_id=1, source_target_pairs={{0,1},{1,0},{2,3},{3,2},{4,5},{5,4},{6,7},{7,6},{8,9},{9,8},{10,11... | collective-permute-start | bytes 3145736 | tf_op jit(solution)/shard_map/ppermute | solution.py:442
  36.9 22.2 %collective-permute-start.2 = (bf16[96,16,256]{2,1,0:T(8,128)(2,1)}, bf16[96,16,256]{2,1,0:T(8,128)(2,1)S(1)}, u32[]{:S(2)}, u32[]{:S(2)}) collective-permute-start(bf16[96,16,256]{2,1,0:T(8,128)(2,1)} %pad_maximum_fusion.2), channel_id=1, source_target_pairs={{0,2},{1,3},{2,4},{3,5},{4,6},{5,7},{6,8},{7,9},{8,10},{9,11},{10,... | collective-permute-start | bytes 2359304 | tf_op jit(solution)/shard_map/ppermute | solution.py:438
  41.0 21.1 %collective-permute-start.3 = (bf16[96,16,256]{2,1,0:T(8,128)(2,1)}, bf16[96,16,256]{2,1,0:T(8,128)(2,1)}, u32[]{:S(2)}, u32[]{:S(2)}) collective-permute-start(bf16[96,16,256]{2,1,0:T(8,128)(2,1)} %pad_maximum_fusion.3), channel_id=1, source_target_pairs={{2,0},{3,1},{4,2},{5,3},{6,4},{7,5},{8,6},{9,7},{10,8},{11,9},{12,... | collective-permute-start | bytes 2359304 | tf_op jit(solution)/shard_map/ppermute | solution.py:438
  42.3 29.1 %collective-permute-start.5 = (bf16[8,16,16,256]{3,2,1,0:T(8,128)(2,1)}, bf16[8,16,16,256]{3,2,1,0:T(8,128)(2,1)}, u32[]{:S(2)}, u32[]{:S(2)}) collective-permute-start(bf16[8,16,16,256]{3,2,1,0:T(8,128)(2,1)} %copy-done.4), channel_id=1, source_target_pairs={{0,1},{1,0},{2,3},{3,2},{4,5},{5,4},{6,7},{7,6},{8,9},{9,8},{10,11... | collective-permute-start | bytes 3145736 | tf_op jit(solution)/shard_map/ppermute | solution.py:442
  44.5 26.9 %collective-permute-start.6 = (bf16[8,16,16,256]{3,2,1,0:T(8,128)(2,1)S(1)}, bf16[8,16,16,256]{3,2,1,0:T(8,128)(2,1)}, u32[]{:S(2)}, u32[]{:S(2)}) collective-permute-start(bf16[8,16,16,256]{3,2,1,0:T(8,128)(2,1)S(1)} %collective-permute-done.1.refs_2_), channel_id=1, source_target_pairs={{0,1},{1,0},{2,3},{3,2},{4,5},{5,4},{6,7},{7,6},{8,9},{9,8},{10,11... | collective-permute-start | bytes 3145736 | tf_op jit(solution)/shard_map/ppermute | solution.py:442
  50.1 1.0 slice-start.1
  53.1 1.4 copy-start.5
  56.2 1.3 copy-start.6
  59.1 3.8 %copy-start.3 = (bf16[96,16,256]{2,1,0:T(8,128)(2,1)}, bf16[96,16,256]{2,1,0:T(8,128)(2,1)S(1)}, u32[]{:S(2)}) copy-start(bf16[96,16,256]{2,1,0:T(8,128)(2,1)S(1)} %collective-permute-done.2.refs_3_) | copy-start | bytes 2359300
  63.0 8.4 %collective-permute-start.7 = (bf16[96,16,256]{2,1,0:T(8,128)(2,1)}, bf16[96,16,256]{2,1,0:T(8,128)(2,1)}, u32[]{:S(2)}, u32[]{:S(2)}) collective-permute-start(bf16[96,16,256]{2,1,0:T(8,128)(2,1)} %broadcast_select_fusion), channel_id=1, source_target_pairs={{0,1},{1,0},{2,3},{3,2},{4,5},{5,4},{6,7},{7,6},{8,9},{9,8},{10,11... | collective-permute-start | bytes 2359304 | tf_op jit(solution)/shard_map/ppermute | solution.py:442
  67.1 0.7 copy-start.12
  68.8 0.7 copy-start.11
  (1 other events, 0.7 us)

commit v5 on v4

--- a/solution.py
+++ b/solution.py
@@ -546,9 +546,10 @@
 
     pieces = [w_reduce, w_taps, w_expand, *split_float(norm_scale), *split_float(norm_shift)]
     column = reach_close(features, out_cotangent)
-    column, every = lax.optimization_barrier((column, gather_params(pieces)))
+    every = gather_params(pieces)
+    column[1], every = lax.optimization_barrier((column[1], every))
     sent = [trimmed(column[1]), trimmed(column[2])]
-    column, sent = lax.optimization_barrier((column, sent))
+    column[1], sent[0] = lax.optimization_barrier((column[1], sent[0]))
     far = reach_far(sent)
     early = other_core(column[1])
     every, early = lax.optimization_barrier((every, early))

time: 168 us -> 166 us (0.988)
  starting transfers between devices: 29.4 us -> 26.9 us
  waiting for transfers between devices: 4.89 us -> 7.04 us
    ppermute x4, starting transfers between devices: 17.9 us -> 14.5 us  [other_core(): return lax.ppermute(block, 'core', [(0, 1), (1, 0)])]
    ppermute x4, waiting for transfers between devices: 4.88 us -> 7.03 us  [shift(): lax.ppermute(block, axes, [(i, i + distance) for i in devices if i + dist...]
    concatenate x4 -> x2, other arithmetic: 3.63 us -> 2.35 us  [twice(): jnp.concatenate([jnp.concatenate([weights, zero], axis=-1), jnp.concatena...]
    unnamed x36 -> x30, local copies, waits for them, and re-layouts: 6.62 us -> 7.01 us
where the time goes in v5:
time: 166 us; the launch traced here: 165 us
  blocking collectives  63.4 us (38%)
  Pallas kernels  40.2 us (24%)
  starting transfers between devices  26.9 us (16%)
  local copies, waits for them, and re-layouts  14.2 us (9%)
  other arithmetic  12.6 us (8%)
  waiting for transfers between devices  7.04 us (4%)
    all_to_all x3, blocking collectives, swap_chunks(): return lax.all_to_all(parts, axes, 0, 0, tiled=True)  51.8 us
    pallas_call x1, Pallas kernels, run_kernel(): pl.pallas_call(whole_kernel, grid_spec=pltpu.PrefetchScalarGridSpec(num_s...  40.2 us
    ppermute x4, starting transfers between devices, other_core(): return lax.ppermute(block, 'core', [(0, 1), (1, 0)])  14.5 us
    ppermute x4, starting transfers between devices, shift(): lax.ppermute(block, axes, [(i, i + distance) for i in devices if i + dist...  12.4 us
    all_gather x1, blocking collectives, gather_params(): return lax.all_gather(packed, 'section', axis=0, tiled=False)  11.6 us
    ppermute x4, waiting for transfers between devices, shift(): lax.ppermute(block, axes, [(i, i + distance) for i in devices if i + dist...  7.03 us
    unnamed x30, local copies, waits for them, and re-layouts  7.01 us
    another operation x6, other arithmetic, tap_pair(): jnp.stack([grid((0, 1, 2, None), (0, 1, 2, None)), grid((0, 1, None, 2),...  3.85 us
  transfers between devices with their start and end apart: 8, of which 3 were waited for; matrix products, arithmetic and copies ran while one was open for 10% of the time, Pallas kernels for 0%

profile of v5, /device:TPU:1, one launch (start us, length us, event | category | flops | bytes accessed | tf_op | source)
XLA Modules:
  0.0 165.4 jit_solution(14194633728065541911)
XLA Ops:
  0.6 1.9 %constant_dynamic-update-slice_fusion.1 = bf16[8,16,16,256]{3,2,1,0:T(8,128)(2,1)} fusion(bf16[4,16,16,256]{3,2,1,0:T(8,128)(2,1)} %param.9), kind=kLoop, calls=%fused_computation.91 | loop fusion | bytes 1048576
  3.5 4.2 %collective-permute-start = (bf16[8,16,16,256]{3,2,1,0:T(8,128)(2,1)}, bf16[8,16,16,256]{3,2,1,0:T(8,128)(2,1)S(1)}, u32[]{:S(2)}, u32[]{:S(2)}) collective-permute-start(bf16[8,16,16,256]{3,2,1,0:T(8,128)(2,1)} %constant_dynamic-update-slice_fusion.refs_0_), channel_id=1, source_target_pairs={{0,2},{1,3},{2,4},{3,5},{4,6},{5,7},{6,8},{7,9},{8,10},{9,11},{10,... | collective-permute-start | bytes 3145736 | tf_op jit(solution)/shard_map/ppermute | solution.py:438
  7.7 1.3 collective-permute-start.1
  11.6 11.6 %all-gather.1 = bf16[4,556,128]{2,1,0:T(8,128)(2,1)S(1)} all-gather(bf16[1,556,128]{2,1,0:T(8,128)(2,1)S(1)} %bitcast.102), channel_id=2, replica_groups=mesh['section'=4,'z'=8,'y'=8,'core'=2] {'section'}, dimensions={0}, use_global_device_ids=true | all-gather | bytes 711680 | tf_op jit(solution)/shard_map/all_gather | solution.py:488
  23.2 3.3 %collective-permute-done.refs_1_ = bf16[8,16,16,256]{3,2,1,0:T(8,128)(2,1)S(1)} collective-permute-done((bf16[8,16,16,256]{3,2,1,0:T(8,128)(2,1)}, bf16[8,16,16,256]{3,2,1,0:T(8,128)(2,1)S(1)}, u32[]{:S(2)}, u32[]{:S(2)}) %collective-permute-start) | collective-permute-done | bytes 1048608 | tf_op jit(solution)/shard_map/ppermute | solution.py:438
  26.6 1.2 pad_maximum_fusion.2
  27.8 6.7 %collective-permute-start.4 = (bf16[8,16,16,256]{3,2,1,0:T(8,128)(2,1)S(1)}, bf16[8,16,16,256]{3,2,1,0:T(8,128)(2,1)}, u32[]{:S(2)}, u32[]{:S(2)}) collective-permute-start(bf16[8,16,16,256]{3,2,1,0:T(8,128)(2,1)S(1)} %collective-permute-done.refs_1_), channel_id=1, source_target_pairs={{0,1},{1,0},{2,3},{3,2},{4,5},{5,4},{6,7},{7,6},{8,9},{9,8},{10,11... | collective-permute-start | bytes 3145736 | tf_op jit(solution)/shard_map/ppermute | solution.py:442
  34.5 1.9 %collective-permute-start.5 = (bf16[8,16,16,256]{3,2,1,0:T(8,128)(2,1)}, bf16[8,16,16,256]{3,2,1,0:T(8,128)(2,1)}, u32[]{:S(2)}, u32[]{:S(2)}) collective-permute-start(bf16[8,16,16,256]{3,2,1,0:T(8,128)(2,1)} %constant_dynamic-update-slice_fusion.refs_0_), channel_id=1, source_target_pairs={{0,1},{1,0},{2,3},{3,2},{4,5},{5,4},{6,7},{7,6},{8,9},{9,8},{10,11... | collective-permute-start | bytes 3145736 | tf_op jit(solution)/shard_map/ppermute | solution.py:442
  36.5 1.2 pad_maximum_fusion.3
  37.7 1.3 collective-permute-start.3
  39.0 5.6 %collective-permute-start.2 = (bf16[96,16,256]{2,1,0:T(8,128)(2,1)}, bf16[96,16,256]{2,1,0:T(8,128)(2,1)}, u32[]{:S(2)}, u32[]{:S(2)}) collective-permute-start(bf16[96,16,256]{2,1,0:T(8,128)(2,1)} %pad_maximum_fusion.2), channel_id=1, source_target_pairs={{0,2},{1,3},{2,4},{3,5},{4,6},{5,7},{6,8},{7,9},{8,10},{9,11},{10,... | collective-permute-start | bytes 2359304 | tf_op jit(solution)/shard_map/ppermute | solution.py:438
  44.6 2.7 %collective-permute-start.6 = (bf16[8,16,16,256]{3,2,1,0:T(8,128)(2,1)S(1)}, bf16[8,16,16,256]{3,2,1,0:T(8,128)(2,1)}, u32[]{:S(2)}, u32[]{:S(2)}) collective-permute-start(bf16[8,16,16,256]{3,2,1,0:T(8,128)(2,1)S(1)} %collective-permute-done.1.refs_2_), channel_id=1, source_target_pairs={{0,1},{1,0},{2,3},{3,2},{4,5},{5,4},{6,7},{7,6},{8,9},{9,8},{10,11... | collective-permute-start | bytes 3145736 | tf_op jit(solution)/shard_map/ppermute | solution.py:442
  48.2 1.1 fusion.27
  51.2 1.3 fusion.22
  52.5 1.1 fusion.24
  55.5 1.1 pad_maximum_fusion.1.refs_13_
  56.6 2.8 %collective-permute-done.3.refs_4_ = bf16[96,16,256]{2,1,0:T(8,128)(2,1)} collective-permute-done((bf16[96,16,256]{2,1,0:T(8,128)(2,1)}, bf16[96,16,256]{2,1,0:T(8,128)(2,1)}, u32[]{:S(2)}, u32[]{:S(2)}) %collective-permute-start.3) | collective-permute-done | bytes 786464 | tf_op jit(solution)/shard_map/ppermute | solution.py:438
  60.3 2.1 %broadcast_select_fusion = bf16[96,16,256]{2,1,0:T(8,128)(2,1)} fusion(bf16[96,16,256]{2,1,0:T(8,128)(2,1)} %collective-permute-done.3.refs_4_, bf16[96,16,256]{2,1,0:T(8,128)(2,1)} %collective-permute-done.2.refs_3_, pred[]{:T(512)S(6)} %eq.19), kind=kLoop, calls=%fused_computation.16 | loop fusion | flops 393216 | bytes 2359297 | tf_op jit(solution)/shard_map/jit(_where)/select_n | solution.py:460
  62.5 3.2 %collective-permute-start.7 = (bf16[96,16,256]{2,1,0:T(8,128)(2,1)}, bf16[96,16,256]{2,1,0:T(8,128)(2,1)S(1)}, u32[]{:S(2)}, u32[]{:S(2)}) collective-permute-start(bf16[96,16,256]{2,1,0:T(8,128)(2,1)} %broadcast_select_fusion), channel_id=1, source_target_pairs={{0,1},{1,0},{2,3},{3,2},{4,5},{5,4},{6,7},{7,6},{8,9},{9,8},{10,11... | collective-permute-start | bytes 2359304 | tf_op jit(solution)/shard_map/ppermute | solution.py:442
  68.8 1.1 copy.107.refs_10_
  70.8 40.2 %shard_map.128 = (bf16[4,16,16,256]{3,2,1,0:T(8,128)(2,1)}, bf16[4,16,16,256]{3,2,1,0:T(8,128)(2,1)}, bf16[640,128]{1,0:T(8,128)(2,1)}) custom-call(s32[6]{0:T(128)} %pad_add_fusion.meta, s32[512]{0:T(512)} %owner.1, s32[2048]{0:T(1024)} %reshape.95.near, bf16[8,16,16,256]{3,2,1,0:T(8,128)(2,1)} %constant_dynamic-update-slice_fusion.refs_0_, ...), custom_call_target="tpu_custom_call" | custom-call | tf_op jit(solution)/shard_map/pallas_call | solution.py:399
  111.0 20.2 %all_to_all.21 = bf16[16,40,128]{2,1,0:T(8,128)(2,1)S(1)} all-to-all(bf16[16,40,128]{2,1,0:T(8,128)(2,1)} %bitcast.109), channel_id=1, replica_groups=mesh['section'=4,'z'=8,'y'=8,'core'=2] {'y','core'}, dimensions={0} | all-to-all | bytes 327680 | tf_op jit(solution)/shard_map/all_to_all | solution.py:466
  131.2 18.5 %all_to_all.22 = bf16[8,40,128]{2,1,0:T(8,128)(2,1)S(1)} all-to-all(bf16[8,40,128]{2,1,0:T(8,128)(2,1)S(1)} %tile.4), channel_id=1, replica_groups=mesh['section'=4,'z'=8,'y'=8,'core'=2] {'z'}, dimensions={0} | all-to-all | bytes 163840 | tf_op jit(solution)/shard_map/all_to_all | solution.py:466
  149.8 13.1 %all_to_all.23 = bf16[16,40,128]{2,1,0:T(8,128)(2,1)S(1)} all-to-all(bf16[16,40,128]{2,1,0:T(8,128)(2,1)S(1)} %tile.5), channel_id=1, replica_groups=mesh['section'=4,'z'=8,'y'=8,'core'=2] {'y','core'}, dimensions={0} | all-to-all | bytes 327680 | tf_op jit(solution)/shard_map/all_to_all | solution.py:466
  (100 shorter events, 15.6 us)
Async XLA Ops:
  0.6 1.9 %copy-start.5 = (bf16[4,16,16,256]{3,2,1,0:T(8,128)(2,1)S(1)}, bf16[4,16,16,256]{3,2,1,0:T(8,128)(2,1)}, u32[]{:S(2)}) copy-start(bf16[4,16,16,256]{3,2,1,0:T(8,128)(2,1)} %param.10) | copy-start | bytes 1572868
  2.6 6.4 %copy-start.8 = (bf16[1,64,256]{2,1,0:T(8,128)(2,1)S(1)}, bf16[1,64,256]{2,1,0:T(8,128)(2,1)}, u32[]{:S(2)}) copy-start(bf16[1,64,256]{2,1,0:T(8,128)(2,1)} %param.13) | copy-start | bytes 98308
  3.5 5.6 %copy-start.7 = (bf16[1,256,64]{1,2,0:T(8,128)(2,1)S(1)}, bf16[1,256,64]{1,2,0:T(8,128)(2,1)}, u32[]{:S(2)}) copy-start(bf16[1,256,64]{1,2,0:T(8,128)(2,1)} %param.11) | copy-start | bytes 98308
  3.5 23.0 %collective-permute-start = (bf16[8,16,16,256]{3,2,1,0:T(8,128)(2,1)}, bf16[8,16,16,256]{3,2,1,0:T(8,128)(2,1)S(1)}, u32[]{:S(2)}, u32[]{:S(2)}) collective-permute-start(bf16[8,16,16,256]{3,2,1,0:T(8,128)(2,1)} %constant_dynamic-update-slice_fusion.refs_0_), channel_id=1, source_target_pairs={{0,2},{1,3},{2,4},{3,5},{4,6},{5,7},{6,8},{7,9},{8,10},{9,11},{10,... | collective-permute-start | bytes 3145736 | tf_op jit(solution)/shard_map/ppermute | solution.py:438
  7.7 28.7 %collective-permute-start.1 = (bf16[8,16,16,256]{3,2,1,0:T(8,128)(2,1)}, bf16[8,16,16,256]{3,2,1,0:T(8,128)(2,1)S(1)}, u32[]{:S(2)}, u32[]{:S(2)}) collective-permute-start(bf16[8,16,16,256]{3,2,1,0:T(8,128)(2,1)} %constant_dynamic-update-slice_fusion.refs_0_), channel_id=1, source_target_pairs={{2,0},{3,1},{4,2},{5,3},{6,4},{7,5},{8,6},{9,7},{10,8},{11,9},{12,... | collective-permute-start | bytes 3145736 | tf_op jit(solution)/shard_map/ppermute | solution.py:438
  9.0 0.9 copy-start.6
  10.1 0.7 copy-start.11
  10.7 0.7 copy-start.12
  26.5 1.3 copy-start
  27.8 19.5 %collective-permute-start.4 = (bf16[8,16,16,256]{3,2,1,0:T(8,128)(2,1)S(1)}, bf16[8,16,16,256]{3,2,1,0:T(8,128)(2,1)}, u32[]{:S(2)}, u32[]{:S(2)}) collective-permute-start(bf16[8,16,16,256]{3,2,1,0:T(8,128)(2,1)S(1)} %collective-permute-done.refs_1_), channel_id=1, source_target_pairs={{0,1},{1,0},{2,3},{3,2},{4,5},{5,4},{6,7},{7,6},{8,9},{9,8},{10,11... | collective-permute-start | bytes 3145736 | tf_op jit(solution)/shard_map/ppermute | solution.py:442
  34.5 35.4 %collective-permute-start.5 = (bf16[8,16,16,256]{3,2,1,0:T(8,128)(2,1)}, bf16[8,16,16,256]{3,2,1,0:T(8,128)(2,1)}, u32[]{:S(2)}, u32[]{:S(2)}) collective-permute-start(bf16[8,16,16,256]{3,2,1,0:T(8,128)(2,1)} %constant_dynamic-update-slice_fusion.refs_0_), channel_id=1, source_target_pairs={{0,1},{1,0},{2,3},{3,2},{4,5},{5,4},{6,7},{7,6},{8,9},{9,8},{10,11... | collective-permute-start | bytes 3145736 | tf_op jit(solution)/shard_map/ppermute | solution.py:442
  36.4 8.2 %copy-start.1 = (bf16[8,16,16,256]{3,2,1,0:T(8,128)(2,1)}, bf16[8,16,16,256]{3,2,1,0:T(8,128)(2,1)S(1)}, u32[]{:S(2)}) copy-start(bf16[8,16,16,256]{3,2,1,0:T(8,128)(2,1)S(1)} %collective-permute-done.1.refs_2_) | copy-start | bytes 3145732
  37.7 21.8 %collective-permute-start.3 = (bf16[96,16,256]{2,1,0:T(8,128)(2,1)}, bf16[96,16,256]{2,1,0:T(8,128)(2,1)}, u32[]{:S(2)}, u32[]{:S(2)}) collective-permute-start(bf16[96,16,256]{2,1,0:T(8,128)(2,1)} %pad_maximum_fusion.3), channel_id=1, source_target_pairs={{2,0},{3,1},{4,2},{5,3},{6,4},{7,5},{8,6},{9,7},{10,8},{11,9},{12,... | collective-permute-start | bytes 2359304 | tf_op jit(solution)/shard_map/ppermute | solution.py:438
  39.0 21.3 %collective-permute-start.2 = (bf16[96,16,256]{2,1,0:T(8,128)(2,1)}, bf16[96,16,256]{2,1,0:T(8,128)(2,1)}, u32[]{:S(2)}, u32[]{:S(2)}) collective-permute-start(bf16[96,16,256]{2,1,0:T(8,128)(2,1)} %pad_maximum_fusion.2), channel_id=1, source_target_pairs={{0,2},{1,3},{2,4},{3,5},{4,6},{5,7},{6,8},{7,9},{8,10},{9,11},{10,... | collective-permute-start | bytes 2359304 | tf_op jit(solution)/shard_map/ppermute | solution.py:438
  44.6 25.3 %collective-permute-start.6 = (bf16[8,16,16,256]{3,2,1,0:T(8,128)(2,1)S(1)}, bf16[8,16,16,256]{3,2,1,0:T(8,128)(2,1)}, u32[]{:S(2)}, u32[]{:S(2)}) collective-permute-start(bf16[8,16,16,256]{3,2,1,0:T(8,128)(2,1)S(1)} %collective-permute-done.1.refs_2_), channel_id=1, source_target_pairs={{0,1},{1,0},{2,3},{3,2},{4,5},{5,4},{6,7},{7,6},{8,9},{9,8},{10,11... | collective-permute-start | bytes 3145736 | tf_op jit(solution)/shard_map/ppermute | solution.py:442
  52.5 1.2 copy-start.2
  52.5 1.6 copy-start.3
  62.5 7.4 %collective-permute-start.7 = (bf16[96,16,256]{2,1,0:T(8,128)(2,1)}, bf16[96,16,256]{2,1,0:T(8,128)(2,1)S(1)}, u32[]{:S(2)}, u32[]{:S(2)}) collective-permute-start(bf16[96,16,256]{2,1,0:T(8,128)(2,1)} %broadcast_select_fusion), channel_id=1, source_target_pairs={{0,1},{1,0},{2,3},{3,2},{4,5},{5,4},{6,7},{7,6},{8,9},{9,8},{10,11... | collective-permute-start | bytes 2359304 | tf_op jit(solution)/shard_map/ppermute | solution.py:442
  65.7 0.7 copy-start.10
  67.3 0.7 copy-start.9
  69.9 0.9 copy-start.4

commit v6 on v2

--- a/solution.py
+++ b/solution.py
@@ -169,7 +169,7 @@
     )
 
 
-def pool_copies(sources, pools, sems):
+def pool_copies(sources, pools, stored, weights, sems):
     feats, cots = ([], [])
 
     def add(group, source, target):
@@ -192,10 +192,12 @@
                         pools[1].at[at, pl.ds(end * (SIDE - RIM), RIM)],
                     )
                 at += 1
+    for k, (source, target) in enumerate(zip(stored, weights)):
+        add(feats if k < 3 else cots, source, target)
     return (feats, cots)
 
 
-COPIES = 2 * (3 * 2 + 8 * 3)
+COPIES = 2 * (3 * 2 + 8 * 3) + 6
 
 
 def inner_tile(region, lane):
@@ -212,13 +214,15 @@
 
 
 def whole_kernel(meta, owner, near, *refs):
-    sources, refs = ((refs[:5], refs[5:10]), refs[10:])
-    (w_red, w_tap, w_exp, v_red, v_tap, v_exp, norms, out, grad_in, grads,
+    sources, stored, refs = ((refs[:5], refs[5:10]), refs[10:16], refs[16:])
+    weights, refs = (refs[-6:], refs[:-6])
+    w_red, w_tap, w_exp, v_red, v_tap, v_exp = weights
+    (norms, out, grad_in, grads,
      feats, cots, sems, region, present, masks, gates, stack, center, products, s_one, s_two, s_three,
      a_own, h_one, h_two, d_one, total) = refs
     pair = pl.program_id(0)
     here, section = (meta[0], meta[1])
-    copies = pool_copies(sources, (feats, cots), sems)
+    copies = pool_copies(sources, (feats, cots), stored, weights, sems)
 
     @pl.when(pair == 0)
     def _():
@@ -396,8 +400,8 @@
         grid_spec=pltpu.PrefetchScalarGridSpec(
             num_scalar_prefetch=len(scalars),
             grid=(2,),
-            in_specs=[pl.BlockSpec(memory_space=pl.ANY)] * len(sources)
-            + [whole(item) for item in weights],
+            in_specs=[pl.BlockSpec(memory_space=pl.ANY)] * (len(sources) + 6)
+            + [whole(weights[6])],
             out_specs=[pair, pair, whole(grads)],
             scratch_shapes=[
                 pool,
@@ -418,6 +422,7 @@
                 pltpu.VMEM(narrow, BF),
                 pltpu.VMEM(narrow, BF),
                 pltpu.VMEM((640, 128), F32),
+                *[pltpu.VMEM(item.shape, BF) for item in weights[:6]],
             ],
         ),
         out_shape=[tiles, tiles, grads],

time: 164 us -> 163 us (level)
  no operation moved by 1% of the time
where the time goes in v6:
time: 163 us; the launch traced here: 162 us
  blocking collectives  56.9 us (35%)
  Pallas kernels  40.5 us (25%)
  starting transfers between devices  29.9 us (18%)
  local copies, waits for them, and re-layouts  18.1 us (11%)
  other arithmetic  11.7 us (7%)
  waiting for transfers between devices  4.14 us (3%)
    all_to_all x3, blocking collectives, swap_chunks(): return lax.all_to_all(parts, axes, 0, 0, tiled=True)  46.9 us
    pallas_call x1, Pallas kernels, run_kernel(): pl.pallas_call(whole_kernel, grid_spec=pltpu.PrefetchScalarGridSpec(num_s...  40.5 us
    ppermute x5, starting transfers between devices, other_core(): return lax.ppermute(block, 'core', [(0, 1), (1, 0)])  18.4 us
    ppermute x4, starting transfers between devices, shift(): lax.ppermute(block, axes, [(i, i + distance) for i in devices if i + dist...  11.5 us
    all_gather x1, blocking collectives, gather_params(): every = lax.all_gather(packed, 'section', axis=0, tiled=False)  9.98 us
    unnamed x38, local copies, waits for them, and re-layouts  7.95 us
    another operation x6, other arithmetic, tap_pair(): jnp.stack([grid((0, 1, 2, None), (0, 1, 2, None)), grid((0, 1, None, 2),...  5.01 us
    ppermute x4, waiting for transfers between devices, shift(): lax.ppermute(block, axes, [(i, i + distance) for i in devices if i + dist...  4.05 us
  transfers between devices with their start and end apart: 9, of which 2 were waited for; matrix products, arithmetic and copies ran while one was open for 12% of the time, Pallas kernels for 0%

profile of v6, /device:TPU:1, one launch (start us, length us, event | category | flops | bytes accessed | tf_op | source)
XLA Modules:
  0.0 162.4 jit_solution(4976665663990893624)
XLA Ops:
  0.6 1.9 %constant_dynamic-update-slice_fusion.1 = bf16[8,16,16,256]{3,2,1,0:T(8,128)(2,1)} fusion(bf16[4,16,16,256]{3,2,1,0:T(8,128)(2,1)} %param.9), kind=kLoop, calls=%fused_computation.90 | loop fusion | bytes 1048576
  3.4 8.9 %collective-permute-start.4 = (bf16[8,16,16,256]{3,2,1,0:T(8,128)(2,1)}, bf16[8,16,16,256]{3,2,1,0:T(8,128)(2,1)}, u32[]{:S(2)}, u32[]{:S(2)}) collective-permute-start(bf16[8,16,16,256]{3,2,1,0:T(8,128)(2,1)} %constant_dynamic-update-slice_fusion.refs_0_), channel_id=1, source_target_pairs={{0,1},{1,0},{2,3},{3,2},{4,5},{5,4},{6,7},{7,6},{8,9},{9,8},{10,11... | collective-permute-start | bytes 3145736 | tf_op jit(solution)/shard_map/ppermute | solution.py:441
  12.4 1.3 collective-permute-start.1
  13.7 4.1 %collective-permute-start = (bf16[8,16,16,256]{3,2,1,0:T(8,128)(2,1)}, bf16[8,16,16,256]{3,2,1,0:T(8,128)(2,1)S(1)}, u32[]{:S(2)}, u32[]{:S(2)}) collective-permute-start(bf16[8,16,16,256]{3,2,1,0:T(8,128)(2,1)} %constant_dynamic-update-slice_fusion.refs_0_), channel_id=1, source_target_pairs={{0,2},{1,3},{2,4},{3,5},{4,6},{5,7},{6,8},{7,9},{8,10},{9,11},{10,... | collective-permute-start | bytes 3145736 | tf_op jit(solution)/shard_map/ppermute | solution.py:437
  19.9 10.0 %all-gather.1 = bf16[4,556,128]{2,1,0:T(8,128)(2,1)S(1)} all-gather(bf16[1,556,128]{2,1,0:T(8,128)(2,1)S(1)} %bitcast.102), channel_id=2, replica_groups=mesh['section'=4,'z'=8,'y'=8,'core'=2] {'section'}, dimensions={0}, use_global_device_ids=true | all-gather | bytes 711680 | tf_op jit(solution)/shard_map/all_gather | solution.py:485
  30.9 1.2 reshape_reshape.3
  32.4 1.1 fusion.27
  35.2 4.0 %collective-permute-done.1.refs_2_ = bf16[8,16,16,256]{3,2,1,0:T(8,128)(2,1)S(1)} collective-permute-done((bf16[8,16,16,256]{3,2,1,0:T(8,128)(2,1)}, bf16[8,16,16,256]{3,2,1,0:T(8,128)(2,1)S(1)}, u32[]{:S(2)}, u32[]{:S(2)}) %collective-permute-start.1) | collective-permute-done | bytes 1048608 | tf_op jit(solution)/shard_map/ppermute | solution.py:437
  39.3 1.2 pad_maximum_fusion.3
  40.5 1.3 collective-permute-start.3
  41.8 1.2 pad_maximum_fusion.2
  43.0 4.9 %collective-permute-start.2 = (bf16[96,16,256]{2,1,0:T(8,128)(2,1)}, bf16[96,16,256]{2,1,0:T(8,128)(2,1)}, u32[]{:S(2)}, u32[]{:S(2)}) collective-permute-start(bf16[96,16,256]{2,1,0:T(8,128)(2,1)} %pad_maximum_fusion.2), channel_id=1, source_target_pairs={{0,2},{1,3},{2,4},{3,5},{4,6},{5,7},{6,8},{7,9},{8,10},{9,11},{10,... | collective-permute-start | bytes 2359304 | tf_op jit(solution)/shard_map/ppermute | solution.py:437
  52.0 1.3 pad_maximum_fusion
  56.1 1.3 fusion.22
  57.3 3.3 %collective-permute-start.6 = (bf16[8,16,16,256]{3,2,1,0:T(8,128)(2,1)S(1)}, bf16[8,16,16,256]{3,2,1,0:T(8,128)(2,1)S(1)}, u32[]{:S(2)}, u32[]{:S(2)}) collective-permute-start(bf16[8,16,16,256]{3,2,1,0:T(8,128)(2,1)S(1)} %collective-permute-done.1.refs_2_), channel_id=1, source_target_pairs={{0,1},{1,0},{2,3},{3,2},{4,5},{5,4},{6,7},{7,6},{8,9},{9,8},{10,11... | collective-permute-start | bytes 3145736 | tf_op jit(solution)/shard_map/ppermute | solution.py:441
  60.6 1.9 %collective-permute-start.5 = (bf16[8,16,16,256]{3,2,1,0:T(8,128)(2,1)S(1)}, bf16[8,16,16,256]{3,2,1,0:T(8,128)(2,1)S(1)}, u32[]{:S(2)}, u32[]{:S(2)}) collective-permute-start(bf16[8,16,16,256]{3,2,1,0:T(8,128)(2,1)S(1)} %collective-permute-done.refs_1_), channel_id=1, source_target_pairs={{0,1},{1,0},{2,3},{3,2},{4,5},{5,4},{6,7},{7,6},{8,9},{9,8},{10,11... | collective-permute-start | bytes 3145736 | tf_op jit(solution)/shard_map/ppermute | solution.py:441
  62.7 1.1 fusion.24
  63.8 2.4 %collective-permute-start.8 = (bf16[96,16,256]{2,1,0:T(8,128)(2,1)}, bf16[96,16,256]{2,1,0:T(8,128)(2,1)S(1)}, u32[]{:S(2)}, u32[]{:S(2)}) collective-permute-start(bf16[96,16,256]{2,1,0:T(8,128)(2,1)} %collective-permute-done.3.refs_4_), channel_id=1, source_target_pairs={{0,1},{1,0},{2,3},{3,2},{4,5},{5,4},{6,7},{7,6},{8,9},{9,8},{10,11... | collective-permute-start | bytes 2359304 | tf_op jit(solution)/shard_map/ppermute | solution.py:441
  66.3 1.9 %collective-permute-start.7 = (bf16[96,16,256]{2,1,0:T(8,128)(2,1)}, bf16[96,16,256]{2,1,0:T(8,128)(2,1)S(1)}, u32[]{:S(2)}, u32[]{:S(2)}) collective-permute-start(bf16[96,16,256]{2,1,0:T(8,128)(2,1)} %collective-permute-done.2.refs_3_), channel_id=1, source_target_pairs={{0,1},{1,0},{2,3},{3,2},{4,5},{5,4},{6,7},{7,6},{8,9},{9,8},{10,11... | collective-permute-start | bytes 2359304 | tf_op jit(solution)/shard_map/ppermute | solution.py:441
  69.5 1.1 pad_maximum_fusion.1.refs_14_
  72.4 40.5 %shard_map.128 = (bf16[4,16,16,256]{3,2,1,0:T(8,128)(2,1)}, bf16[4,16,16,256]{3,2,1,0:T(8,128)(2,1)}, bf16[640,128]{1,0:T(8,128)(2,1)}) custom-call(s32[6]{0:T(128)} %pad_add_fusion.meta, s32[512]{0:T(512)} %owner.1, s32[2048]{0:T(1024)} %reshape.95.near, bf16[8,16,16,256]{3,2,1,0:T(8,128)(2,1)} %constant_dynamic-update-slice_fusion.refs_0_, ...), custom_call_target="tpu_custom_call" | custom-call | tf_op jit(solution)/shard_map/pallas_call | solution.py:398
  112.9 13.6 %all_to_all.21 = bf16[16,40,128]{2,1,0:T(8,128)(2,1)S(1)} all-to-all(bf16[16,40,128]{2,1,0:T(8,128)(2,1)} %bitcast.109), channel_id=1, replica_groups=mesh['section'=4,'z'=8,'y'=8,'core'=2] {'y','core'}, dimensions={0} | all-to-all | bytes 327680 | tf_op jit(solution)/shard_map/all_to_all | solution.py:460
  126.5 19.9 %all_to_all.22 = bf16[8,40,128]{2,1,0:T(8,128)(2,1)S(1)} all-to-all(bf16[8,40,128]{2,1,0:T(8,128)(2,1)S(1)} %tile.4), channel_id=1, replica_groups=mesh['section'=4,'z'=8,'y'=8,'core'=2] {'z'}, dimensions={0} | all-to-all | bytes 163840 | tf_op jit(solution)/shard_map/all_to_all | solution.py:460
  146.5 13.4 %all_to_all.23 = bf16[16,40,128]{2,1,0:T(8,128)(2,1)S(1)} all-to-all(bf16[16,40,128]{2,1,0:T(8,128)(2,1)S(1)} %tile.5), channel_id=1, replica_groups=mesh['section'=4,'z'=8,'y'=8,'core'=2] {'y','core'}, dimensions={0} | all-to-all | bytes 327680 | tf_op jit(solution)/shard_map/all_to_all | solution.py:460
  (109 shorter events, 18.6 us)
Async XLA Ops:
  0.6 1.9 %copy-start.7 = (bf16[4,16,16,256]{3,2,1,0:T(8,128)(2,1)S(1)}, bf16[4,16,16,256]{3,2,1,0:T(8,128)(2,1)}, u32[]{:S(2)}) copy-start(bf16[4,16,16,256]{3,2,1,0:T(8,128)(2,1)} %param.10) | copy-start | bytes 1572868
  2.6 15.2 %copy-start.15 = (f32[1,384]{1,0:T(1,128)S(1)}, f32[1,384]{1,0:T(1,128)}, u32[]{:S(2)}) copy-start(f32[1,384]{1,0:T(1,128)} %param.14) | copy-start | bytes 4612
  2.6 15.2 %copy-start.12 = (bf16[1,64,256]{2,1,0:T(8,128)(2,1)S(1)}, bf16[1,64,256]{2,1,0:T(8,128)(2,1)}, u32[]{:S(2)}) copy-start(bf16[1,64,256]{2,1,0:T(8,128)(2,1)} %param.13) | copy-start | bytes 98308
  3.4 14.3 %copy-start.16 = (f32[1,384]{1,0:T(1,128)S(1)}, f32[1,384]{1,0:T(1,128)}, u32[]{:S(2)}) copy-start(f32[1,384]{1,0:T(1,128)} %param.15) | copy-start | bytes 4612
  3.4 67.1 %collective-permute-start.4 = (bf16[8,16,16,256]{3,2,1,0:T(8,128)(2,1)}, bf16[8,16,16,256]{3,2,1,0:T(8,128)(2,1)}, u32[]{:S(2)}, u32[]{:S(2)}) collective-permute-start(bf16[8,16,16,256]{3,2,1,0:T(8,128)(2,1)} %constant_dynamic-update-slice_fusion.refs_0_), channel_id=1, source_target_pairs={{0,1},{1,0},{2,3},{3,2},{4,5},{5,4},{6,7},{7,6},{8,9},{9,8},{10,11... | collective-permute-start | bytes 3145736 | tf_op jit(solution)/shard_map/ppermute | solution.py:441
  12.4 26.9 %collective-permute-start.1 = (bf16[8,16,16,256]{3,2,1,0:T(8,128)(2,1)}, bf16[8,16,16,256]{3,2,1,0:T(8,128)(2,1)S(1)}, u32[]{:S(2)}, u32[]{:S(2)}) collective-permute-start(bf16[8,16,16,256]{3,2,1,0:T(8,128)(2,1)} %constant_dynamic-update-slice_fusion.refs_0_), channel_id=1, source_target_pairs={{2,0},{3,1},{4,2},{5,3},{6,4},{7,5},{8,6},{9,7},{10,8},{11,9},{12,... | collective-permute-start | bytes 3145736 | tf_op jit(solution)/shard_map/ppermute | solution.py:437
  13.7 28.1 %collective-permute-start = (bf16[8,16,16,256]{3,2,1,0:T(8,128)(2,1)}, bf16[8,16,16,256]{3,2,1,0:T(8,128)(2,1)S(1)}, u32[]{:S(2)}, u32[]{:S(2)}) collective-permute-start(bf16[8,16,16,256]{3,2,1,0:T(8,128)(2,1)} %constant_dynamic-update-slice_fusion.refs_0_), channel_id=1, source_target_pairs={{0,2},{1,3},{2,4},{3,5},{4,6},{5,7},{6,8},{7,9},{8,10},{9,11},{10,... | collective-permute-start | bytes 3145736 | tf_op jit(solution)/shard_map/ppermute | solution.py:437
  18.6 0.9 copy-start.10
  39.2 18.1 %copy-start = (bf16[8,16,16,256]{3,2,1,0:T(8,128)(2,1)}, bf16[8,16,16,256]{3,2,1,0:T(8,128)(2,1)S(1)}, u32[]{:S(2)}) copy-start(bf16[8,16,16,256]{3,2,1,0:T(8,128)(2,1)S(1)} %collective-permute-done.1.refs_2_) | copy-start | bytes 3145732
  40.5 23.4 %collective-permute-start.3 = (bf16[96,16,256]{2,1,0:T(8,128)(2,1)}, bf16[96,16,256]{2,1,0:T(8,128)(2,1)}, u32[]{:S(2)}, u32[]{:S(2)}) collective-permute-start(bf16[96,16,256]{2,1,0:T(8,128)(2,1)} %pad_maximum_fusion.3), channel_id=1, source_target_pairs={{2,0},{3,1},{4,2},{5,3},{6,4},{7,5},{8,6},{9,7},{10,8},{11,9},{12,... | collective-permute-start | bytes 2359304 | tf_op jit(solution)/shard_map/ppermute | solution.py:437
  41.8 18.8 %copy-start.1 = (bf16[8,16,16,256]{3,2,1,0:T(8,128)(2,1)}, bf16[8,16,16,256]{3,2,1,0:T(8,128)(2,1)S(1)}, u32[]{:S(2)}) copy-start(bf16[8,16,16,256]{3,2,1,0:T(8,128)(2,1)S(1)} %collective-permute-done.refs_1_) | copy-start | bytes 3145732
  43.0 23.2 %collective-permute-start.2 = (bf16[96,16,256]{2,1,0:T(8,128)(2,1)}, bf16[96,16,256]{2,1,0:T(8,128)(2,1)}, u32[]{:S(2)}, u32[]{:S(2)}) collective-permute-start(bf16[96,16,256]{2,1,0:T(8,128)(2,1)} %pad_maximum_fusion.2), channel_id=1, source_target_pairs={{0,2},{1,3},{2,4},{3,5},{4,6},{5,7},{6,8},{7,9},{8,10},{9,11},{10,... | collective-permute-start | bytes 2359304 | tf_op jit(solution)/shard_map/ppermute | solution.py:437
  49.1 0.9 copy-start.9
  50.0 0.9 copy-start.8
  55.1 0.9 copy-start.4
  56.1 6.5 %copy-start.13 = (s32[512]{0:T(512)S(1)}, s32[512]{0:T(512)}, u32[]{:S(2)}) copy-start(s32[512]{0:T(512)} %owner.1) | copy-start | bytes 6148
  57.3 13.2 %collective-permute-start.6 = (bf16[8,16,16,256]{3,2,1,0:T(8,128)(2,1)S(1)}, bf16[8,16,16,256]{3,2,1,0:T(8,128)(2,1)S(1)}, u32[]{:S(2)}, u32[]{:S(2)}) collective-permute-start(bf16[8,16,16,256]{3,2,1,0:T(8,128)(2,1)S(1)} %collective-permute-done.1.refs_2_), channel_id=1, source_target_pairs={{0,1},{1,0},{2,3},{3,2},{4,5},{5,4},{6,7},{7,6},{8,9},{9,8},{10,11... | collective-permute-start | bytes 3145736 | tf_op jit(solution)/shard_map/ppermute | solution.py:441
  60.6 9.9 %collective-permute-start.5 = (bf16[8,16,16,256]{3,2,1,0:T(8,128)(2,1)S(1)}, bf16[8,16,16,256]{3,2,1,0:T(8,128)(2,1)S(1)}, u32[]{:S(2)}, u32[]{:S(2)}) collective-permute-start(bf16[8,16,16,256]{3,2,1,0:T(8,128)(2,1)S(1)} %collective-permute-done.refs_1_), channel_id=1, source_target_pairs={{0,1},{1,0},{2,3},{3,2},{4,5},{5,4},{6,7},{7,6},{8,9},{9,8},{10,11... | collective-permute-start | bytes 3145736 | tf_op jit(solution)/shard_map/ppermute | solution.py:441
  63.8 6.7 %collective-permute-start.8 = (bf16[96,16,256]{2,1,0:T(8,128)(2,1)}, bf16[96,16,256]{2,1,0:T(8,128)(2,1)S(1)}, u32[]{:S(2)}, u32[]{:S(2)}) collective-permute-start(bf16[96,16,256]{2,1,0:T(8,128)(2,1)} %collective-permute-done.3.refs_4_), channel_id=1, source_target_pairs={{0,1},{1,0},{2,3},{3,2},{4,5},{5,4},{6,7},{7,6},{8,9},{9,8},{10,11... | collective-permute-start | bytes 2359304 | tf_op jit(solution)/shard_map/ppermute | solution.py:441
  66.3 4.4 %collective-permute-start.7 = (bf16[96,16,256]{2,1,0:T(8,128)(2,1)}, bf16[96,16,256]{2,1,0:T(8,128)(2,1)S(1)}, u32[]{:S(2)}, u32[]{:S(2)}) collective-permute-start(bf16[96,16,256]{2,1,0:T(8,128)(2,1)} %collective-permute-done.2.refs_3_), channel_id=1, source_target_pairs={{0,1},{1,0},{2,3},{3,2},{4,5},{5,4},{6,7},{7,6},{8,9},{9,8},{10,11... | collective-permute-start | bytes 2359304 | tf_op jit(solution)/shard_map/ppermute | solution.py:441
  70.5 1.0 copy-start.2
  70.5 1.3 copy-start.3
  70.6 1.5 copy-start.5
  70.6 1.7 %copy-start.6 = (bf16[96,16,256]{2,1,0:T(8,128)(2,1)}, bf16[96,16,256]{2,1,0:T(8,128)(2,1)S(1)}, u32[]{:S(2)}) copy-start(bf16[96,16,256]{2,1,0:T(8,128)(2,1)S(1)} %collective-permute-done.7.refs_8_) | copy-start | bytes 2359300
  (2 other events, 1.5 us)
